TPU v7x, 32 devices: a whole 2x2x4 slice. The times are simulated.
32 devices in a mesh: dp: 8 (over z, x), head: 4 (over y, core).
Axes of the slice: x: 2, y: 2, z: 4, core: 2. Of those that a mesh axis runs over, the one named last changes fastest.
Arguments:
- tokens: bfloat16 [8192, 768], P(('dp', 'head')), may hold values from -6 to 6
- cotangent: bfloat16 [8192, 768], P(('dp', 'head')), may hold values from -6 to 6
- segments: int32 [8, 1024], P('dp'), may hold values from -1 to 169, as said below
- attention_master: float32 [768, 3072], P('dp')
- feedforward_master: float32 [768, 6144], P('dp'), may hold values from -0.21875 to 0.21875
- vector_master: float32 [12, 768], P(None, 'dp')
- attention_moment: float32 [768, 3072], P('dp'), may hold values from -0.0024414062 to 0.0024414062
- feedforward_moment: float32 [768, 6144], P('dp'), may hold values from -0.0024414062 to 0.0024414062
- vector_moment: float32 [12, 768], P(None, 'dp'), may hold values from -0.0024414062 to 0.0024414062
- attention_second: float32 [768, 3072], P('dp'), may hold values from 1.4110135e-07 to 5.644054e-07
- feedforward_second: float32 [768, 6144], P('dp'), may hold values from 1.4110135e-07 to 5.644054e-07
- vector_second: float32 [12, 768], P(None, 'dp'), may hold values from 1.4110135e-07 to 5.644054e-07
- attention_teacher: float32 [768, 3072], P('dp'), may hold values from -0.21875 to 0.21875
- feedforward_teacher: float32 [768, 6144], P('dp'), may hold values from -0.21875 to 0.21875
- vector_teacher: float32 [12, 768], P(None, 'dp')
Outputs:
- block_output: bfloat16 [8192, 768], P(('dp', 'head'))
- input_gradient: float32 [8192, 768], P(('dp', 'head'))
- gradient_norm: float32 [], replicated
- new_attention_master: float32 [768, 3072], P('dp')
- new_feedforward_master: float32 [768, 6144], P('dp')
- new_vector_master: float32 [12, 768], P(None, 'dp')
- new_attention_moment: float32 [768, 3072], P('dp')
- new_feedforward_moment: float32 [768, 6144], P('dp')
- new_vector_moment: float32 [12, 768], P(None, 'dp')
- new_attention_second: float32 [768, 3072], P('dp')
- new_feedforward_second: float32 [768, 6144], P('dp')
- new_vector_second: float32 [12, 768], P(None, 'dp')
- new_attention_teacher: float32 [768, 3072], P('dp')
- new_feedforward_teacher: float32 [768, 6144], P('dp')
- new_vector_teacher: float32 [12, 768], P(None, 'dp')
- attention_copy: bfloat16 [768, 3072], P('dp')
- feedforward_copy: bfloat16 [768, 6144], P('dp')
- vector_copy: bfloat16 [12, 768], P(None, 'dp')
Inputs may be any that keep to these rules, and one draw needn't show every extreme that they name: `segments`: in each pack, segment numbers start at 0 and rise by one from image to image; an image holds 2 + p * p tokens for some p from 2 to 12; -1 marks padding at the end of the pack, one token of it or more. In every draw one pack holds only images of 2 x 2 patches, as many as fit, so that its last image number is the largest possible.
All inputs are finite; a program needn't handle non-finite values.
Results may differ from a plain program's by a relative error of at most 0.012.
The roundings to bfloat16 on the way count: a program that leaves them out, or rounds other values in their place, can miss the bound.
Values may be sent and summed in bfloat16 or wider, within the bound.
No kernel may reach another device: no remote copies, remote signals or barrier semaphores. Data moves between devices by JAX's collectives and lax.ppermute only.
A program may use at most 192 MiB of HBM per device.

v0:
```python
import functools

import jax
import jax.numpy as jnp
import numpy as np
from jax import lax
from jax.experimental import pallas as pl
from jax.experimental.pallas import tpu as pltpu
from jax.sharding import PartitionSpec as P

HEADS = 12
HEAD_DIM = 64
ADAM_STEP = 3

norm_epsilon = 1e-06
beta_one = 0.5
beta_two = 0.5
adam_epsilon = 1e-08
learn_rate = 0.05
weight_decay = 0.05
teacher_keep = 0.8
clip_limit = 1.0
masked_score = -1e30

BF = jnp.bfloat16
F32 = jnp.float32


def dot_rows(left, right):
    return lax.dot_general(left, right, (((0,), (0,)), ((), ())), preferred_element_type=F32)


def dot_cols(left, right):
    return lax.dot_general(left, right, (((1,), (1,)), ((), ())), preferred_element_type=F32)


def dot(left, right):
    return jnp.dot(left, right, preferred_element_type=F32)


def normalize(values):
    center = jnp.mean(values, axis=-1, keepdims=True)
    deviate = values - center
    spread = jnp.mean(deviate * deviate, axis=-1, keepdims=True)
    inverse = lax.rsqrt(spread + norm_epsilon)
    return deviate * inverse, inverse


def norm_back(hat, inverse, gain, grad):
    scaled = grad * gain
    mean_one = jnp.mean(scaled, axis=-1, keepdims=True)
    mean_two = jnp.mean(scaled * hat, axis=-1, keepdims=True)
    return inverse * (scaled - mean_one - hat * mean_two)


def head_lanes(index, shape):
    lane = lax.broadcasted_iota(jnp.int32, shape, 1)
    return (lane >= index * HEAD_DIM) & (lane < (index + 1) * HEAD_DIM)


def unit_rows(rows, columns):
    row = lax.broadcasted_iota(jnp.int32, (rows, columns), 0)
    column = lax.broadcasted_iota(jnp.int32, (rows, columns), 1)
    return jnp.where(row == column, 1.0, 0.0).astype(BF)


def smem():
    return pl.BlockSpec(memory_space=pltpu.SMEM)


def vmem():
    return pl.BlockSpec(memory_space=pltpu.VMEM)


def whole(*shape):
    return pl.BlockSpec(shape, lambda *index: (0,) * len(shape))


def shaped(shape, kind):
    return jax.ShapeDtypeStruct(shape, kind)


def params(mebibytes):
    return pltpu.CompilerParams(vmem_limit_bytes=mebibytes * 2**20)


COST_SCALE = 1.0


def cost(microseconds):
    return pl.CostEstimate(
        flops=0, transcendentals=0, bytes_accessed=int(microseconds * COST_SCALE * 3.6e6)
    )


def pin(array):
    return pltpu.with_memory_space_constraint(array, pltpu.HBM)


def far_space():
    return pl.BlockSpec(memory_space=pltpu.HBM)


def run(
    kernel,
    name,
    outputs,
    inputs,
    microseconds,
    scratch=(),
    mebibytes=16,
    lazy=(),
    save=(),
    far=(),
    scalars=1,
):
    single = not isinstance(outputs, tuple)
    outputs = [outputs] if single else list(outputs)
    lazy, save, far = list(lazy), list(save), list(far)
    count, produced, own = len(inputs), len(outputs), len(scratch)
    buffers = [pltpu.VMEM(inputs[i].shape, inputs[i].dtype) for i in lazy]
    buffers += [pltpu.VMEM(outputs[i].shape, outputs[i].dtype) for i in far]
    moves = len(lazy) + len(save) + len(far)
    if moves:
        buffers.append(pltpu.SemaphoreType.DMA((moves,)))

    def body(*refs):
        items = list(refs[: count + produced])
        saved = refs[count + produced : count + produced + len(save)]
        rest = refs[count + produced + len(save) :]
        inner, extra = rest[:own], rest[own:]
        copies, number = [], 0
        for j, i in enumerate(lazy):
            copies.append(pltpu.make_async_copy(refs[i], extra[j], extra[-1].at[number]))
            items[i] = extra[j]
            number += 1
        stores = []
        for j, i in enumerate(save):
            stores.append(pltpu.make_async_copy(refs[i], saved[j], extra[-1].at[number]))
            number += 1
        last = []
        for j, i in enumerate(far):
            buffer = extra[len(lazy) + j]
            last.append(pltpu.make_async_copy(buffer, refs[count + i], extra[-1].at[number]))
            items[count + i] = buffer
            number += 1
        for copy in copies + stores:
            copy.start()
        for copy in copies:
            copy.wait()
        kernel(*items, *inner)
        for copy in last:
            copy.start()
        for copy in stores + last:
            copy.wait()

    shapes = [pltpu.HBM(item.shape, item.dtype) if i in far else item for i, item in enumerate(outputs)]
    results = pl.pallas_call(
        body,
        out_shape=shapes + [pltpu.HBM(inputs[i].shape, inputs[i].dtype) for i in save],
        in_specs=[smem()] * scalars
        + [far_space() if i in lazy else vmem() for i in range(scalars, count)],
        out_specs=[far_space() if i in far else vmem() for i in range(produced)]
        + [far_space()] * len(save),
        scratch_shapes=list(scratch) + buffers,
        compiler_params=params(mebibytes),
        cost_estimate=cost(microseconds),
        name=name,
    )(*[pin(item) if i in lazy else item for i, item in enumerate(inputs)])
    return results[0] if single and not save else tuple(results)


GROUPS = 4


def pack_kernel(cols, scal, *refs):
    vector_ref, out_ref = refs[4:6]
    for side in range(2):

        @pl.when(scal[0] % 2 == side)
        def _():
            for i in range(4):
                out_ref[:, i * cols : (i + 1) * cols] = refs[i][
                    :, side * cols : (side + 1) * cols
                ].astype(BF)

    vector = vector_ref[...].astype(BF)
    out_ref[:, 4 * cols :] = dot_rows(vector, unit_rows(vector.shape[0], 128)).astype(BF)


def pack_attention(scal, attention, vector, cols):
    rows = attention.shape[0]

    def pair(i):
        return pl.BlockSpec((rows, 2 * cols), lambda step, scal: (0, 2 * i + scal[0] // 2))

    return pl.pallas_call(
        functools.partial(pack_kernel, cols),
        out_shape=shaped((rows, 4 * cols + 128), BF),
        grid_spec=pltpu.PrefetchScalarGridSpec(
            num_scalar_prefetch=1,
            grid=(1,),
            in_specs=[pair(i) for i in range(4)] + [whole(*vector.shape)],
            out_specs=whole(rows, 4 * cols + 128),
        ),
        compiler_params=params(8),
        cost_estimate=cost(1.5),
        name="pack_attention",
    )(scal, *[attention] * 4, vector)


def cast_kernel(scal, in_ref, out_ref):
    out_ref[...] = in_ref[...].astype(BF)


def pack_forward(scal, forward, part):
    rows = forward.shape[0]
    return pl.pallas_call(
        cast_kernel,
        out_shape=shaped((rows, 2 * part), BF),
        grid_spec=pltpu.PrefetchScalarGridSpec(
            num_scalar_prefetch=1,
            grid=(2,),
            in_specs=[pl.BlockSpec((rows, part), lambda i, scal: (0, GROUPS * i + scal[0]))],
            out_specs=pl.BlockSpec((rows, part), lambda i, scal: (0, i)),
        ),
        compiler_params=params(8),
        cost_estimate=cost(1.5),
        name="pack_forward",
    )(scal, forward)


def place_rows(scal, pieces, target):
    rows = pieces[0].shape[0]
    if len(pieces) == 1:
        target[...] = pieces[0][...]
        return
    for i, piece in enumerate(pieces):
        start = pl.multiple_of(scal[1 + i] * rows, rows)
        target[pl.ds(start, rows), :] = piece[...]


def place_members(scal, pieces, target):
    rows = pieces[0].shape[0]
    for i, piece in enumerate(pieces):
        start = pl.multiple_of((scal[0] ^ i) * rows, rows)
        target[pl.ds(start, rows), :] = piece[...]


def place_kernel(scal, *refs):
    place_members(scal, refs[0:4], refs[4])


def place_blocks(scal, blocks):
    rows, width = blocks[0].shape
    wide = shaped((GROUPS * rows, width), BF)
    return run(place_kernel, "place_blocks", wide, (scal, *blocks), 0.5, mebibytes=2)


def fold(value):
    rows, columns = value.shape
    count = 128 // (columns - 128)
    share = rows // count
    rest = [value[i * share : (i + 1) * share, 128:] for i in range(count)]
    return value[:, :128], jnp.concatenate(rest, axis=1)


def folded_rows(rows, columns):
    return rows + rows * (columns - 128) // 128


def project_kernel(count, cols, scal, seg_ref, x_ref, *refs):
    pieces = refs[:count]
    q_ref, k_ref, v_ref, w_ref, wo_ref, vec_ref, col_ref, a_ref, hat_ref = refs[count : 9 + count]
    weights, wq_ref, wk_ref, wv_ref = refs[9 + count : 13 + count]
    place_rows(scal, pieces, weights)
    for i, ref in enumerate((wq_ref, wk_ref, wv_ref)):
        ref[...] = weights[:, i * cols : (i + 1) * cols]
    w_ref[...] = weights[:, : 3 * cols]
    top, rest = fold(weights[:, 3 * cols : 4 * cols])
    wo_ref[: top.shape[0], :] = top
    wo_ref[top.shape[0] :, :] = rest
    unit = unit_rows(16, 128)
    vec_ref[...] = dot_cols(unit, weights[:, 4 * cols :])
    start = pl.multiple_of(scal[0] * cols, cols)
    own = dot_cols(unit, weights[pl.ds(start, cols), 4 * cols :])
    query_bias, value_bias = own[2:3, :], own[3:4, :]
    gain, shift = vec_ref[0:1, :], vec_ref[1:2, :]
    numbers = jnp.broadcast_to(seg_ref[...].astype(F32), (8, seg_ref.shape[1])).astype(BF)
    col_ref[...] = dot_rows(numbers, unit_rows(8, 128))[:, 0:1].astype(jnp.int32)
    block = 256

    def step(i, carry):
        rows = pl.ds(pl.multiple_of(i * block, block), block)
        hat, _ = normalize(x_ref[rows, :].astype(F32))
        normed = (hat * gain + shift).astype(BF)
        a_ref[rows, :] = normed
        hat_ref[rows, :] = hat.astype(BF)
        q_ref[rows, :] = (dot(normed, wq_ref[...]) + query_bias).astype(BF)
        k_ref[rows, :] = dot(normed, wk_ref[...]).astype(BF)
        v_ref[rows, :] = (dot(normed, wv_ref[...]) + value_bias).astype(BF)
        return carry

    lax.fori_loop(0, x_ref.shape[0] // block, step, 0)


def project(scal, segments, x_all, pieces, cols):
    length, width = x_all.shape
    outputs = (
        (shaped((length, cols), BF),) * 3
        + (shaped((width, 3 * cols), BF),)
        + (shaped((folded_rows(width, cols), 128), BF),)
        + (shaped((16, width), F32), shaped((length, 1), jnp.int32))
        + (shaped((length, width), BF),) * 2
    )
    return run(
        functools.partial(project_kernel, len(pieces), cols),
        "project",
        outputs,
        (scal, segments, x_all, *pieces),
        4.5,
        [pltpu.VMEM((width, 4 * cols + 128), BF)] + [pltpu.VMEM((width, cols), BF)] * 3,
    )


CHUNK = 128
WINDOWS = (4, 5, 8)


def key_window(seg, start, size, length):
    def image(place):
        number = seg[0, place]
        return jnp.where(number < 0, length, number)

    first, last = image(start), image(start + size - 1)
    low, high = jnp.int32(0), jnp.int32(0)
    for chunk in range(length // CHUNK):
        low += (image(chunk * CHUNK + CHUNK - 1) < first).astype(jnp.int32)
        high += (image(chunk * CHUNK) <= last).astype(jnp.int32)
    return low, high - low


def each_window(low, count, length, body):
    chunks = length // CHUNK
    sizes = [size for size in WINDOWS if size < chunks] + [chunks]
    below = 0
    for size in sizes:

        @pl.when((count > below) & (count <= size))
        def _():
            start = jnp.minimum(low, chunks - size) * CHUNK
            body(pl.multiple_of(start, CHUNK), size * CHUNK)

        below = size


def each_head(per, size, body, carry):
    if size > WINDOWS[0] * CHUNK:
        return lax.fori_loop(0, per, body, carry)
    for head in range(per):
        carry = body(head, carry)
    return carry


def attend_kernel(per, first, scal, seg, q_ref, k_ref, v_ref, seg_row_ref, seg_col_ref, *refs):
    out_ref, held = refs[-2:]
    block = 256
    length = k_ref.shape[0]

    def step(i, carry):
        start = pl.multiple_of(first + i * block, block)
        near = pl.ds(pl.multiple_of(i * block, block), block)
        low, count = key_window(seg, start, block, length)

        def body(key_start, size):
            window = pl.ds(key_start, size)
            keys, values = k_ref[window, :], v_ref[window, :]
            same = seg_col_ref[pl.ds(start, block), :] == seg_row_ref[:, window]
            queries = q_ref[pl.ds(start, block), :] * jnp.asarray(HEAD_DIM**-0.5, BF)

            def one(head, result):
                lanes = head_lanes(head, queries.shape)
                score = dot_cols(jnp.where(lanes, queries, jnp.zeros_like(queries)), keys)
                score = jnp.where(same, score, masked_score)
                largest = jnp.max(score, axis=1, keepdims=True)
                power = jnp.exp(score - largest)
                total = jnp.sum(power, axis=1, keepdims=True)
                chance = (power * (1.0 / total)).astype(BF)
                return jnp.where(lanes, dot(chance, values), result)

            result = each_head(per, size, one, jnp.zeros(queries.shape, F32))
            held[near, :] = result.astype(BF)

        each_window(low, count, length, body)
        return carry

    lax.fori_loop(0, held.shape[0] // block, step, 0)
    top, rest = fold(held[...])
    out_ref[: top.shape[0], :] = top
    out_ref[top.shape[0] :, :] = rest


def attend(scal, queries, keys, values, seg_row, seg_col, per, first, count, kept=()):
    inputs = (scal, seg_row, queries, keys, values, seg_row, seg_col, *kept)
    return run(
        functools.partial(attend_kernel, per, first),
        "attend",
        shaped((folded_rows(count, queries.shape[1]), 128), BF),
        inputs,
        7.0 * count / queries.shape[0],
        [pltpu.VMEM((count, queries.shape[1]), BF)],
        save=(2, 3, 4, 6, *range(7, len(inputs))) if kept else (),
        scalars=2,
    )


def forward_kernel(count, cols, parts, scal, x_ref, dy_ref, *refs):
    mixed, w_out = [refs[k * parts : (k + 1) * parts] for k in range(4)], refs[4 * parts :][:4]
    refs = refs[4 * parts + 4 :]
    pieces = refs[:count]
    vec_ref = refs[count]
    c_ref, u_ref, df_ref, keep_ref, send_ref, h_ref, w_ref, rows_ref, sums_ref, o_ref = refs[
        1 + count : 11 + count
    ]
    out_weight = refs[11 + count]
    member = scal[0]
    length, width = x_ref.shape
    part = w_ref.shape[1] // 2
    block = length // GROUPS
    narrow = cols - 128
    place_rows(scal, pieces, w_ref)

    def unfold(target, first, column, item):
        rows = item.shape[0] * 128 // cols
        share = rows * narrow // 128
        target[first : first + rows, column : column + 128] = item[:rows, :]
        for i in range(rows // share):
            start = first + i * share
            target[start : start + share, column + 128 : column + cols] = item[
                rows:, i * narrow : (i + 1) * narrow
            ]

    for index in range(GROUPS):

        @pl.when(member == index)
        def _():
            for k in range(GROUPS):
                column = (index ^ k) * cols
                unfold(out_weight, 0, column, w_out[k])
                for half in range(parts):
                    unfold(o_ref, half * (length // parts), column, mixed[k][half])

    rows_ref[...] = out_weight[pl.ds(pl.multiple_of(member * cols, cols), cols), :]
    zero = jnp.zeros((1, width), F32)
    up_bias = vec_ref[pl.ds(8 + member, 1), :]

    def run_block(step, carry):
        rows = pl.ds(pl.multiple_of(step * block, block), block)
        resid = x_ref[rows, :].astype(F32) + vec_ref[4:5, :] + dot(o_ref[rows, :], out_weight[...])

        @pl.when(step == member)
        def _():
            h_ref[...] = resid

        hat, _ = normalize(resid)
        normed = (hat * vec_ref[5:6, :] + vec_ref[6:7, :]).astype(BF)
        c_ref[rows, :] = normed
        pre = dot(normed, w_ref[:, :part]) + up_bias
        phi = 0.5 * (1.0 + lax.erf(pre * 0.7071067811865476))
        u_ref[rows, :] = (pre * phi).astype(BF)
        slope = phi + pre * (jnp.exp(-0.5 * pre * pre) * 0.3989422804014327)
        grad_pre = (dot(dy_ref[rows, :], w_ref[:, part:]) * slope).astype(BF)
        df_ref[rows, :] = grad_pre
        grad_normed = dot_cols(grad_pre, w_ref[:, :part])
        split_store(member, step, grad_normed, keep_ref, send_ref)
        return (
            carry[0] + jnp.sum(grad_normed * hat, axis=0, keepdims=True),
            carry[1] + jnp.sum(grad_normed, axis=0, keepdims=True),
            carry[2] + jnp.sum(grad_pre.astype(F32), axis=0, keepdims=True),
        )

    carry = lax.fori_loop(0, GROUPS, run_block, (zero, zero, zero))
    sums_ref[...] = jnp.zeros_like(sums_ref)
    for i in range(3):
        sums_ref[i : i + 1, :] = carry[i]


def split_store(member, index, value, keep_ref, send_ref):
    mine = (index % 2) == (member % 2)
    rows = value.shape[0]
    place = pl.ds(pl.multiple_of((index // 2) * rows, rows), rows)

    @pl.when(mine)
    def _():
        keep_ref[place, :] = value

    @pl.when(jnp.logical_not(mine))
    def _():
        send_ref[place, :] = value.astype(BF)


def forward_back(scal, x_all, dy_all, mixed, w_out, pieces, vec, cols):
    length, width = x_all.shape
    part = pieces[0].shape[1] // 2
    rows = length // GROUPS
    outputs = (
        shaped((length, width), BF),
        shaped((length, part), BF),
        shaped((length, part), BF),
        shaped((2 * rows, width), F32),
        shaped((2 * rows, width), BF),
        shaped((rows, width), F32),
        shaped((width, 2 * part), BF),
        shaped((cols, width), BF),
        shaped((8, width), F32),
        shaped((length, width), BF),
    )
    flat = [item for items in mixed for item in items]
    return run(
        functools.partial(forward_kernel, len(pieces), cols, len(mixed[0])),
        "forward_back",
        outputs,
        (scal, x_all, dy_all, *flat, *w_out, *pieces, vec),
        13.0,
        [pltpu.VMEM((width, width), BF)],
    )


def forward_grads_kernel(scal, c_ref, u_ref, df_ref, dy_ref, *refs):
    g_ref = refs[-1]
    part = u_ref.shape[1]
    third = c_ref.shape[1] // 3

    def weight(i, carry):
        lanes = pl.ds(pl.multiple_of(i * third, third), third)
        g_ref[lanes, :part] = dot_rows(c_ref[:, lanes], df_ref[...]).astype(BF)
        g_ref[lanes, part:] = dot_rows(dy_ref[:, lanes], u_ref[...]).astype(BF)
        return carry

    lax.fori_loop(0, 3, weight, 0)


def forward_grads(scal, normed, active, grad_pre, dy_all, kept):
    width = normed.shape[1]
    part = active.shape[1]
    outputs = shaped((width, 2 * part), BF)
    inputs = (scal, normed, active, grad_pre, dy_all, *kept)
    return run(
        forward_grads_kernel,
        "forward_grads",
        outputs,
        inputs,
        4.0,
        save=(2, *range(5, len(inputs))),
    )


def branch_kernel(scal, u_ref, w_ref, dy_ref, keep_ref, send_ref, own_ref):
    own_ref[...] = dy_ref[...]
    part = u_ref.shape[1]
    block = u_ref.shape[0] // GROUPS

    def branch(i, carry):
        rows = pl.ds(pl.multiple_of(i * block, block), block)
        split_store(scal[0], i, dot_cols(u_ref[rows, :], w_ref[:, part:]), keep_ref, send_ref)
        return carry

    lax.fori_loop(0, GROUPS, branch, 0)


def branch_part(scal, active, weights, cotangent):
    rows = active.shape[0] // GROUPS
    width = weights.shape[0]
    return run(
        branch_kernel,
        "branch_part",
        (
            shaped((2 * rows, width), F32),
            shaped((2 * rows, width), BF),
            shaped(cotangent.shape, BF),
        ),
        (scal, active, weights, cotangent),
        3.0,
        lazy=(1, 2, 3),
        far=(0,),
    )


def merge_kernel(scal, keep_ref, got_ref, mine_ref, send_ref):
    rows = mine_ref.shape[0]
    mine = pl.ds(pl.multiple_of((scal[0] // 2) * rows, rows), rows)
    other = pl.ds(pl.multiple_of((1 - scal[0] // 2) * rows, rows), rows)
    mine_ref[...] = keep_ref[mine, :] + got_ref[mine, :].astype(F32)
    send_ref[...] = (keep_ref[other, :] + got_ref[other, :].astype(F32)).astype(BF)


def merge(scal, keep, got, lazy=()):
    rows, width = keep.shape
    outputs = (shaped((rows // 2, width), F32), shaped((rows // 2, width), BF))
    return run(merge_kernel, "merge", outputs, (scal, keep, got), 0.7, mebibytes=8, lazy=lazy)


def resid_kernel(scal, mine_ref, got_ref, h_ref, dy_ref, vec_ref, dh_ref, dp_ref, sums_ref):
    grad = mine_ref[...] + got_ref[...].astype(F32)
    hat, inverse = normalize(h_ref[...])
    dy = dy_ref[...].astype(F32)
    grad_resid = dy + norm_back(hat, inverse, vec_ref[5:6, :], grad)
    dh_ref[...] = grad_resid
    low = grad_resid.astype(BF)
    dp_ref[...] = low
    sums_ref[...] = jnp.zeros_like(sums_ref)
    sums_ref[0:1, :] = jnp.sum(low.astype(F32), axis=0, keepdims=True)
    sums_ref[1:2, :] = jnp.sum(dy, axis=0, keepdims=True)


def resid_back(scal, mine, got, resid, cotangent, vec):
    rows, width = mine.shape
    outputs = (shaped((rows, width), F32), shaped((rows, width), BF), shaped((8, width), F32))
    return run(resid_kernel, "resid_back", outputs, (scal, mine, got, resid, cotangent, vec), 0.8)


def mixed_kernel(cols, scal, *refs):
    grads, (o_ref, rows_ref, do_ref, g_ref, all_ref, own_ref) = refs[0:4], refs[4:10]
    place_members(scal, grads, all_ref)
    do_ref[...] = dot_cols(all_ref[...], rows_ref[...]).astype(BF)
    for index in range(GROUPS):

        @pl.when(scal[0] == index)
        def _():
            own_ref[...] = all_ref[:, index * cols : (index + 1) * cols]

    g_ref[...] = dot_rows(o_ref[...], own_ref[...]).astype(BF)


def mixed_back(scal, grads, mixed, w_rows):
    cols, width = w_rows.shape
    length = mixed.shape[0]
    return run(
        functools.partial(mixed_kernel, cols),
        "mixed_back",
        (shaped((length, cols), BF), shaped((width, cols), BF)),
        (scal, *grads, mixed, w_rows),
        2.5,
        [pltpu.VMEM((length, width), BF), pltpu.VMEM((length, cols), BF)],
        lazy=(5, 6),
    )


def attend_back_kernel(
    per, scal, seg, q_ref, k_ref, v_ref, do_ref, seg_row_ref, seg_col_ref, *refs
):
    out_ref, k_acc, v_acc = refs[-3:]
    cols = q_ref.shape[1]
    block = 256
    length = k_ref.shape[0]
    k_acc[...] = jnp.zeros_like(k_acc)
    v_acc[...] = jnp.zeros_like(v_acc)

    def step(i, carry):
        start = pl.multiple_of(i * block, block)
        rows = pl.ds(start, block)
        low, count = key_window(seg, start, block, length)

        def body(key_start, size):
            window = pl.ds(key_start, size)
            keys, values = k_ref[window, :], v_ref[window, :]
            same = seg_col_ref[window, :] == seg_row_ref[:, rows]
            queries = q_ref[rows, :] * jnp.asarray(HEAD_DIM**-0.5, BF)
            grads = do_ref[rows, :]

            def one(head, carry):
                grad_query, grad_key, grad_value = carry
                lanes = head_lanes(head, queries.shape)
                query = jnp.where(lanes, queries, jnp.zeros_like(queries))
                grad = jnp.where(lanes, grads, jnp.zeros_like(grads))
                score = jnp.where(same, dot_cols(keys, query), masked_score)
                largest = jnp.max(score, axis=0, keepdims=True)
                power = jnp.exp(score - largest)
                total = jnp.sum(power, axis=0, keepdims=True)
                chance = power * (1.0 / total)
                grad_chance = dot_cols(values, grad)
                inner = jnp.sum(chance * grad_chance, axis=0, keepdims=True)
                grad_score = (chance * (grad_chance - inner)).astype(BF)
                return (
                    jnp.where(lanes, dot_rows(grad_score, keys), grad_query),
                    grad_key + dot(grad_score, query),
                    grad_value + dot(chance.astype(BF), grad),
                )

            zeros = jnp.zeros(keys.shape, F32)
            grad_query, grad_key, grad_value = each_head(
                per, size, one, (jnp.zeros(queries.shape, F32), zeros, zeros)
            )
            k_acc[window, :] += grad_key
            v_acc[window, :] += grad_value
            out_ref[rows, :cols] = (grad_query * HEAD_DIM**-0.5).astype(BF)

        each_window(low, count, length, body)
        return carry

    lax.fori_loop(0, q_ref.shape[0] // block, step, 0)
    out_ref[:, cols : 2 * cols] = k_acc[...].astype(BF)
    out_ref[:, 2 * cols :] = v_acc[...].astype(BF)


def attend_back(scal, queries, keys, values, grad_out, seg_row, seg_col, per, kept):
    length, cols = queries.shape
    wide = pltpu.VMEM(queries.shape, F32)
    inputs = (scal, seg_row, queries, keys, values, grad_out, seg_row, seg_col, *kept)
    return run(
        functools.partial(attend_back_kernel, per),
        "attend_back",
        shaped((length, 3 * cols), BF),
        inputs,
        16.0,
        [wide, wide],
        lazy=(2, 3, 4, 7),
        save=range(8, len(inputs)),
        scalars=2,
    )


def query_grads_kernel(cols, scal, *refs):
    a_ref, hat_ref, out_ref, grad_ref, w_ref, forward_ref, resid_ref = refs[0:7]
    g_ref, rows_ref, table_ref = refs[7:10]
    member = scal[0]
    length, width = a_ref.shape
    ones = jnp.ones((length, 8), BF)
    grad = grad_ref[...]
    row = lax.broadcasted_iota(jnp.int32, (8, 3 * cols), 0)
    rest = dot_rows(ones, grad)
    terms = jnp.zeros((8, 3 * cols), F32)
    for term in range(3):
        high = rest.astype(BF).astype(F32)
        terms = jnp.where(row == term, high, terms)
        rest = rest - high
    terms = terms.astype(BF)

    rows_ref[...] = jnp.zeros_like(rows_ref)
    rows_ref[4:5, :] = resid_ref[0:1, :]
    rows_ref[5:7, :] = forward_ref[0:2, :]
    rows_ref[7:8, :] = resid_ref[1:2, :]
    rows_ref[pl.ds(8 + member, 1), :] = forward_ref[2:3, :]
    rest = rows_ref[...]
    unit = unit_rows(16, 128)
    table = jnp.zeros((width, 128), F32)
    for _ in range(3):
        high = rest.astype(BF)
        rest = rest - high.astype(F32)
        table += dot_rows(high, unit)
    table_ref[...] = table

    block = 256
    lane = lax.broadcasted_iota(jnp.int32, (block, 128), 1)

    def step(i, carry):
        lanes = pl.ds(pl.multiple_of(i * block, block), block)
        weight = w_ref[lanes, :]
        g_ref[lanes, : 3 * cols] = dot_rows(a_ref[:, lanes], grad).astype(BF)
        product = dot_rows(hat_ref[:, lanes], grad) * weight.astype(F32)
        gain = jnp.sum(product, axis=1, keepdims=True)
        shift = jnp.sum(dot_cols(weight, terms), axis=1, keepdims=True)
        table = jnp.where(lane == 0, gain, table_ref[lanes, :])
        table_ref[lanes, :] = jnp.where(lane == 1, shift, table)
        return carry

    lax.fori_loop(0, width // block, step, 0)
    g_ref[:, 3 * cols : 4 * cols] = out_ref[...]
    own = pl.ds(pl.multiple_of(member * cols, cols), cols)
    bias = table_ref[own, :]
    near = lax.broadcasted_iota(jnp.int32, (cols, 128), 1)
    for i, column in ((0, 2), (2, 3)):
        part = grad_ref[:, i * cols : (i + 1) * cols]
        bias = jnp.where(near == column, dot_rows(part, ones)[:, 0:1], bias)
    table_ref[own, :] = bias
    total = table_ref[:, 0:16]
    high = total.astype(BF)
    g_ref[:, 4 * cols : 4 * cols + 16] = high
    g_ref[:, 4 * cols + 16 : 4 * cols + 32] = (total - high.astype(F32)).astype(BF)
    g_ref[:, 4 * cols + 32 :] = jnp.zeros((width, 96), BF)


def query_grads(scal, normed, hat, grad_out, grad, weights, sums_forward, sums_resid):
    width, cols = grad_out.shape
    return run(
        functools.partial(query_grads_kernel, cols),
        "query_grads",
        shaped((width, 4 * cols + 128), BF),
        (scal, normed, hat, grad_out, grad, weights, sums_forward, sums_resid),
        4.0,
        [pltpu.VMEM((16, width), F32), pltpu.VMEM((width, 128), F32)],
        lazy=(1, 2, 3, 5, 6, 7),
        far=(0,),
    )


def project_back_kernel(scal, grad_ref, w_ref, keep_ref, send_ref):
    block = grad_ref.shape[0] // GROUPS

    def step(i, carry):
        rows = pl.ds(pl.multiple_of(i * block, block), block)
        split_store(scal[0], i, dot_cols(grad_ref[rows, :], w_ref[...]), keep_ref, send_ref)
        return carry

    lax.fori_loop(0, GROUPS, step, 0)


def project_back(scal, grad, weights):
    rows, width = grad.shape[0] // 2, weights.shape[0]
    return run(
        project_back_kernel,
        "project_back",
        (shaped((rows, width), F32), shaped((rows, width), BF)),
        (scal, grad, weights),
        3.0,
        lazy=(2,),
    )


def input_kernel(scal, mine_ref, got_ref, x_ref, dh_ref, vec_ref, out_ref):
    grad = mine_ref[...] + got_ref[...].astype(F32)
    hat, inverse = normalize(x_ref[...].astype(F32))
    out_ref[...] = dh_ref[...] + norm_back(hat, inverse, vec_ref[0:1, :], grad)


def input_back(scal, mine, got, tokens, grad_resid, vec):
    inputs = (scal, mine, got, tokens, grad_resid, vec)
    return run(input_kernel, "input_back", shaped(mine.shape, F32), inputs, 1.0, lazy=(2, 3, 4, 5))


def output_kernel(scal, mine_ref, got_ref, h_ref, vec_ref, out_ref):
    branch = mine_ref[...] + got_ref[...].astype(F32) + vec_ref[7:8, :]
    out_ref[...] = (h_ref[...] + branch).astype(BF)


def output_sum(scal, mine, got, resid, vec):
    inputs = (scal, mine, got, resid, vec)
    return run(output_kernel, "output_sum", shaped(mine.shape, BF), inputs, 0.8, lazy=(2, 3, 4))


def owned_kernel(scal, in_ref, low_ref):
    total = in_ref[0].astype(F32)
    for i in range(1, in_ref.shape[0]):
        total += in_ref[i].astype(F32)
    low_ref[...] = total.astype(BF)


def owned_sum(scal, pieces):
    outputs = shaped(pieces.shape[1:], BF)
    return run(owned_kernel, "owned_sum", outputs, (scal, pieces), 1.5, lazy=(1,))


def squares_kernel(scal, *refs):
    sums = []
    for piece in refs[:4]:
        wide = piece[...].astype(F32)
        sums.append(jnp.sum(wide * wide))
    total = (sums[0] + sums[1]) + (sums[2] + sums[3])
    refs[4][...] = jnp.full(refs[4].shape, total, F32)


def squares_of(scal, pieces):
    outputs = shaped((8, 128), F32)
    return run(squares_kernel, "squares_of", outputs, (scal, *pieces), 1.0, save=range(1, 5))


def owned_vector_kernel(cols, scal, in_ref, low_ref):
    total = in_ref[0].astype(F32)
    for i in range(1, in_ref.shape[0]):
        total += in_ref[i].astype(F32)
    low_ref[:, : 4 * cols] = total[:, : 4 * cols].astype(BF)
    vector = total[:, 4 * cols :]
    low_ref[:, 4 * cols : 4 * cols + 128] = vector.astype(BF)
    low_ref[:, 4 * cols + 128 :] = (vector - vector.astype(BF).astype(F32)).astype(BF)


def owned_vector(scal, pieces, cols):
    _, rows, width = pieces.shape
    return run(
        functools.partial(owned_vector_kernel, cols),
        "owned_vector",
        shaped((rows, width + 128), BF),
        (scal, pieces),
        1.5,
    )


def join_kernel(cols, count, scal, *refs):
    pieces, forward_ref = refs[0:4], refs[4]
    gradient_ref, vector_ref, squares_ref = refs[5:8]
    width = gradient_ref.shape[1] // 4
    for member in range(GROUPS):

        @pl.when(scal[0] == member)
        def _():
            for i in range(4):
                for k in range(GROUPS):
                    start = i * width + (member ^ k) * cols
                    gradient_ref[:, start : start + cols] = pieces[k][
                        :, i * cols : (i + 1) * cols
                    ].astype(F32)

    def vector_of(piece):
        high = piece[:, 4 * cols : 4 * cols + 128].astype(F32)
        return high + piece[:, 4 * cols + 128 :].astype(F32)

    halves = [vector_of(piece) for piece in pieces]
    table = (halves[0] + halves[1]) + (halves[2] + halves[3])
    rows = lax.broadcasted_iota(jnp.int32, (16, 128), 0)
    lanes = lax.broadcasted_iota(jnp.int32, (16, 128), 1)
    unit = jnp.where((lanes == rows) | (lanes == rows + 16), 1.0, 0.0)
    vector = lax.dot_general(
        unit,
        table,
        (((1,), (1,)), ((), ())),
        preferred_element_type=F32,
        precision=lax.Precision.HIGHEST,
    )[:count]
    vector_ref[...] = vector
    gradient = gradient_ref[...]
    total = jnp.sum(gradient * gradient) + jnp.sum(vector * vector)
    total = forward_ref[...] + total
    for i in range(squares_ref.shape[0] // 8):
        squares_ref[8 * i : 8 * i + 8, :] = total


def join(scal, pieces, squares, width, count, cols, owners):
    rows = pieces[0].shape[0]
    return run(
        functools.partial(join_kernel, cols, count),
        "join",
        (
            shaped((rows, 4 * width), F32),
            shaped((count, rows), F32),
            shaped((8 * owners, 128), F32),
        ),
        (scal, *pieces, squares),
        1.5,
    )


def clip_factor(total_ref):
    total = total_ref[0]
    for i in range(1, total_ref.shape[0]):
        total += total_ref[i]
    norm = jnp.sqrt(total[0:1, 0:1])
    return norm, jnp.minimum(1.0, clip_limit / (norm + 1e-06))


def adam_kernel(counts, scal, total_ref, attention_ref, vector_ref, *refs):
    pieces, sources, targets, norm_ref = refs[0:4], refs[4:16], refs[16:31], refs[31]
    held, copies = refs[32:44], refs[44:47]
    loads, stores = refs[47:50], refs[50:53]
    grads, grad_loads = refs[53:57], refs[57]
    norm, factor = clip_factor(total_ref)
    norm_ref[...] = jnp.broadcast_to(norm, norm_ref.shape)
    decays = (weight_decay, weight_decay, 0.0)

    def chunk(kind, i):
        if counts[kind] == 1:
            return (slice(None), slice(None))
        size = held[4 * kind].shape[1] // counts[kind]
        return (slice(None), pl.ds(pl.multiple_of(i * size, size), size))

    def load(kind, i, state):
        place = chunk(kind, i)
        number = 4 * kind + state
        return pltpu.make_async_copy(
            sources[number].at[place], held[number].at[place], loads[kind].at[i, state]
        )

    def store(kind, i, state):
        place = chunk(kind, i)
        source = held[4 * kind + state] if state < 4 else copies[kind]
        return pltpu.make_async_copy(
            source.at[place], targets[3 * state + kind].at[place], stores[kind].at[i, state]
        )

    def every(kind, action):
        def step(i, carry):
            action(kind, i)
            return carry

        lax.fori_loop(0, counts[kind], step, 0)

    def start(kind, i):
        for state in range(4):
            load(kind, i, state).start()

    def work(kind, i):
        for state in range(4):
            load(kind, i, state).wait()
        place = chunk(kind, i)
        if kind == 0:
            gradient = attention_ref[place]
        elif kind == 2:
            gradient = vector_ref[...]
        else:
            size = held[4].shape[1] // counts[1]
            half = pl.ds(pl.multiple_of((i // GROUPS) * size, size), size)
            source = scal[0] ^ (i % GROUPS)
            gradient = grads[0][:, half]
            for k in range(1, GROUPS):
                gradient = jnp.where(source == k, grads[k][:, half], gradient)
            gradient = gradient.astype(F32)
        results = adam_update(
            *[held[4 * kind + state][place] for state in range(4)], gradient, factor, decays[kind]
        )
        for state, value in zip((0, 1, 2, 3), results):
            held[4 * kind + state][place] = value
        copies[kind][place] = results[0].astype(BF)
        for state in range(5):
            store(kind, i, state).start()

    def finish(kind, i):
        for state in range(5):
            store(kind, i, state).wait()

    moves = [
        pltpu.make_async_copy(piece, grad, grad_loads.at[i])
        for i, (piece, grad) in enumerate(zip(pieces, grads))
    ]
    for move in moves:
        move.start()
    for kind in (1, 0, 2):
        every(kind, start)
    for move in moves:
        move.wait()
    for kind in (1, 0, 2):
        every(kind, work)
    for kind in (1, 0, 2):
        every(kind, finish)


def adam(scal, totals, attention_grad, vector_grad, forward_grads_by_member, states):
    counts = (4, 2 * GROUPS, 1)
    kinds = [states[4 * kind].shape for kind in range(3)]
    out_shape = [pltpu.HBM(shape, F32) for _ in range(4) for shape in kinds]
    out_shape += [pltpu.HBM(shape, BF) for shape in kinds]
    out_shape += [shaped((8, 128), F32)]
    return pl.pallas_call(
        functools.partial(adam_kernel, counts),
        out_shape=out_shape,
        in_specs=[smem()] + [vmem()] * 3 + [far_space()] * 16,
        out_specs=[far_space()] * 15 + [vmem()],
        scratch_shapes=[pltpu.VMEM(kinds[kind], F32) for kind in range(3) for _ in range(4)]
        + [pltpu.VMEM(shape, BF) for shape in kinds]
        + [pltpu.SemaphoreType.DMA((count, 4)) for count in counts]
        + [pltpu.SemaphoreType.DMA((count, 5)) for count in counts]
        + [pltpu.VMEM(item.shape, item.dtype) for item in forward_grads_by_member]
        + [pltpu.SemaphoreType.DMA((GROUPS,))],
        compiler_params=params(32),
        cost_estimate=cost(9.0),
        name="adam",
    )(scal, totals, attention_grad, vector_grad, *map(pin, forward_grads_by_member), *map(pin, states))


def adam_update(master, moment, second, teacher, gradient, factor, decay_rate):
    clipped = gradient * factor
    moment_new = beta_one * moment + (1.0 - beta_one) * clipped
    second_new = beta_two * second + (1.0 - beta_two) * clipped * clipped
    scale_one = 1.0 - beta_one**ADAM_STEP
    scale_two = 1.0 - beta_two**ADAM_STEP
    update = (moment_new * (1.0 / scale_one)) / (
        jnp.sqrt(second_new * (1.0 / scale_two)) + adam_epsilon
    )
    master_new = master * (1.0 - learn_rate * decay_rate) - learn_rate * update
    teacher_new = teacher_keep * teacher + (1.0 - teacher_keep) * master_new
    return (master_new, moment_new, second_new, teacher_new)


def swap(part, bit):
    return lax.ppermute(part, "head", [(i, i ^ bit) for i in range(4)])


def spread(part, *others):
    across = swap(part, 2)
    if others:
        return [
            part,
            swap(after(part, *others), 1),
            across,
            swap(after(across, *others), 1),
        ]
    return [part, swap(part, 1), across, swap(across, 1)]


RING = (0, 2, 4, 6, 7, 5, 3, 1)


def ring_owners(count):
    if count != len(RING):
        return np.zeros((count, 1), np.int32)
    table = []
    for device in range(count):
        place = RING.index(device)
        owners = [device]
        for hop in range(1, count // 2 + 1):
            owners.append(RING[(place - hop) % count])
            if hop < count // 2:
                owners.append(RING[(place + hop) % count])
        table.append(owners)
    return np.asarray(table, np.int32)


def after(value, *others):
    return lax.optimization_barrier((value, *others))[0]


class Ring:
    def __init__(self, block, count):
        self.count = count
        self.hops = count // 2 if count == len(RING) else 1
        self.front = self.rear = block
        self.pieces = [block]
        self.done = 0

    def hop(self, *others):
        self.done += 1
        if self.count != len(RING):
            self.pieces = [lax.all_gather(after(self.front, *others), "dp", axis=0, tiled=True)]
            return self
        ahead = [(RING[i], RING[(i + 1) % self.count]) for i in range(self.count)]
        back = [(target, source) for source, target in ahead]
        last = self.done == self.hops
        if self.done > 1 or others:
            self.front, self.rear = lax.optimization_barrier((self.front, self.rear, *others))[:2]
        self.front = lax.ppermute(self.front, "dp", ahead)
        self.pieces.append(self.front)
        if not last:
            self.rear = lax.ppermute(self.rear, "dp", back)
            self.pieces.append(self.rear)
        return self

    def rest(self):
        while self.done < self.hops:
            self.hop()
        return self.pieces


def exchange_owned(grads, count):
    blocks = grads.reshape(count, -1, grads.shape[1])
    return lax.all_to_all(blocks, "dp", split_axis=0, concat_axis=0)


def local(
    tokens,
    cotangent,
    segments,
    attention_master,
    feedforward_master,
    vector_master,
    attention_moment,
    feedforward_moment,
    vector_moment,
    attention_second,
    feedforward_second,
    vector_second,
    attention_teacher,
    feedforward_teacher,
    vector_teacher,
):
    width = tokens.shape[1]
    owners = lax.axis_size("dp")
    groups = lax.axis_size("head")
    hidden = feedforward_master.shape[1] // 2
    per = HEADS // groups
    cols = per * HEAD_DIM
    part = hidden // groups

    owner_table = ring_owners(owners)
    table = np.concatenate(
        [
            np.tile(np.arange(groups, dtype=np.int32), owners)[:, None],
            np.repeat(owner_table, groups, axis=0),
        ],
        axis=1,
    )
    place = lax.axis_index("dp") * groups + lax.axis_index("head")
    scal = lax.dynamic_index_in_dim(jnp.asarray(table), place, 0, keepdims=False)
    first = Ring(pack_attention(scal, attention_master, vector_master, cols), owners)
    first.rest()
    ringed = owners == len(RING)
    early = first.pieces[-3:-1] if ringed else first.pieces
    token_across, grad_across = swap(tokens, 2), swap(cotangent, 2)
    token, token_across = lax.optimization_barrier((tokens, token_across, *early))[:2]
    x_all = place_blocks(scal, [token, swap(token, 1), token_across, swap(token_across, 1)])
    second = Ring(pack_forward(scal, feedforward_master, part), owners)
    second.hop(first.pieces[-1])

    queries, keys, values, w_qkv, w_o, vec, seg_col, normed, hat = project(
        scal, segments, x_all, first.pieces, cols
    )
    half = x_all.shape[0] // 2
    w_across = swap(w_o, 2)
    mixed_low, *kept = attend(
        scal,
        after(queries, grad_across),
        keys,
        values,
        segments,
        seg_col,
        per,
        0,
        half,
        (w_qkv, vec, normed, hat),
    )
    far_q, far_k, far_v, far_col, far_weights, far_vec, *far_normed = kept
    low_across = swap(mixed_low, 2)
    w_across = after(w_across, mixed_low)
    if ringed:
        second.hop(mixed_low)
    mixed_high = attend(
        scal, after(queries, w_across), keys, values, segments, seg_col, per, half, half
    )
    high_across = swap(after(mixed_high, low_across), 2)
    if ringed:
        second.hop(mixed_high)
    w_across, low_across, w_o, mixed_low, grad, grad_across = lax.optimization_barrier(
        (w_across, low_across, w_o, mixed_low, cotangent, grad_across, high_across)
    )[:6]
    dy_all = place_blocks(scal, [grad, swap(grad, 1), grad_across, swap(grad_across, 1)])
    w_out = [w_o, swap(w_o, 1), w_across, swap(w_across, 1)]
    mixed = [
        (mixed_low, mixed_high),
        (swap(mixed_low, 1), swap(mixed_high, 1)),
        (low_across, high_across),
        (swap(low_across, 1), swap(high_across, 1)),
    ]
    (
        normed_two,
        active,
        grad_pre,
        keep,
        send,
        resid,
        w_ff,
        w_rows,
        sums_forward,
        mixed_all,
    ) = forward_back(scal, x_all, dy_all, mixed, w_out, second.rest(), vec, cols)
    grad_ff, far_active, *kept = forward_grads(
        scal,
        normed_two,
        active,
        grad_pre,
        dy_all,
        (resid, sums_forward, w_rows, w_ff, mixed_all),
    )
    far_resid, far_sums, far_rows, far_ff, far_mixed = kept
    got = swap(send, 1)
    grad_ff, got = lax.optimization_barrier((grad_ff, got))
    owned_ff = exchange_owned(grad_ff, owners)
    mine, send = merge(scal, keep, got)
    keep_branch, send_branch, cot_own = branch_part(
        scal, far_active, after(far_ff, send), cotangent
    )
    got = swap(send, 2)
    grad_resid, grad_low, sums_resid = resid_back(
        scal, after(mine, send_branch), got, resid, cot_own, vec
    )
    low_blocks = spread(grad_low)
    mine, send = merge(
        scal, keep_branch, swap(after(send_branch, grad_low), 1), lazy=(1,)
    )
    low_blocks[0] = after(low_blocks[0], send)
    grad_mixed, grad_out = mixed_back(scal, low_blocks, far_mixed, far_rows)
    grad_qkv, far_dh, far_sums_resid, far_grad_out = attend_back(
        scal,
        far_q,
        far_k,
        far_v,
        grad_mixed,
        segments,
        far_col,
        per,
        (grad_resid, sums_resid, grad_out),
    )
    got_branch = swap(send, 2)
    pack = query_grads(
        scal,
        after(far_normed[0], got_branch),
        far_normed[1],
        far_grad_out,
        grad_qkv,
        far_weights,
        far_sums,
        far_sums_resid,
    )
    owned_pack = exchange_owned(pack, owners)
    forward_parts = spread(owned_sum(scal, after(owned_ff, pack)))
    forward_squares, *forward_parts = squares_of(scal, forward_parts)
    keep, send = project_back(scal, grad_qkv, after(far_weights, pack))
    mine_input, send = merge(scal, keep, swap(send, 1))
    block_output = output_sum(scal, after(mine, pack), got_branch, far_resid, far_vec)
    got_input = swap(send, 2)
    owned_pack = after(owned_pack, block_output, forward_squares, got_input)
    input_gradient = input_back(scal, mine_input, got_input, tokens, far_dh, far_vec)
    attention_parts = spread(owned_vector(scal, owned_pack, cols))
    attention_grad, vector_grad, squares = join(
        scal, attention_parts, forward_squares, width, vector_master.shape[0], cols, owners
    )
    totals = lax.all_to_all(
        squares.reshape(owners, 8, 128), "dp", split_axis=0, concat_axis=0
    )
    *results, norm = adam(
        scal,
        totals,
        attention_grad,
        vector_grad,
        forward_parts,
        (
            attention_master,
            attention_moment,
            attention_second,
            attention_teacher,
            feedforward_master,
            feedforward_moment,
            feedforward_second,
            feedforward_teacher,
            vector_master,
            vector_moment,
            vector_second,
            vector_teacher,
        ),
    )
    return (block_output, input_gradient, norm[0, 0], *results)


def solution(mesh):
    rows = P(("dp", "head"), None)
    shard = P("dp", None)
    vector = P(None, "dp")
    return jax.shard_map(
        local,
        mesh=mesh,
        in_specs=(rows, rows, shard) + (shard, shard, vector) * 4,
        out_specs=(rows, rows, P()) + (shard, shard, vector) * 5,
        check_vma=False,
    )
```

profile of v0, /device:TPU:0, one launch (start us, length us, event | category | flops | bytes accessed | tf_op | source)
XLA Modules:
  0.0 220.6 jit_solution(11893450047546744203)
XLA Ops:
  0.7 0.7 dynamic-slice_bitcast_fusion.scal.refs_0_
  1.4 1.3 copy-done
  2.6 0.7 copy-done.5
  3.3 0.9 pack_attention.1.refs_3_
  4.2 3.0 %collective-permute-start.2 = (bf16[96,896]{1,0:T(8,128)(2,1)S(1)}, bf16[96,896]{1,0:T(8,128)(2,1)S(1)}, u32[]{:S(2)}, u32[]{:S(2)}) collective-permute-start(bf16[96,896]{1,0:T(8,128)(2,1)S(1)} %pack_attention.1.refs_3_), channel_id=1, source_target_pairs={{8,0},{16,8},{24,16},{28,24},{20,28},{12,20},{4,12},{0,4},{9,1},{1... | collective-permute-start | bytes 516104 | tf_op jit(solution)/shard_map/ppermute | solution.py:1131
  7.4 4.3 %collective-permute-done.2.refs_5_ = bf16[96,896]{1,0:T(8,128)(2,1)S(1)} collective-permute-done((bf16[96,896]{1,0:T(8,128)(2,1)S(1)}, bf16[96,896]{1,0:T(8,128)(2,1)S(1)}, u32[]{:S(2)}, u32[]{:S(2)}) %collective-permute-start.2) | collective-permute-done | bytes 172064 | tf_op jit(solution)/shard_map/ppermute | solution.py:1131
  11.7 1.4 collective-permute-done.1.refs_4_
  13.5 1.6 collective-permute-start.4
  15.1 1.5 collective-permute-start
  16.6 1.9 collective-permute-done.3.refs_6_
  18.9 1.7 collective-permute-start.5
  20.9 3.4 %collective-permute-done.5.refs_8_ = bf16[96,896]{1,0:T(8,128)(2,1)S(1)} collective-permute-done((bf16[96,896]{1,0:T(8,128)(2,1)S(1)}, bf16[96,896]{1,0:T(8,128)(2,1)S(1)}, u32[]{:S(2)}, u32[]{:S(2)}) %collective-permute-start.5) | collective-permute-done | bytes 172064 | tf_op jit(solution)/shard_map/ppermute | solution.py:1128
  24.3 1.7 collective-permute-done.6.refs_9_
  26.0 1.6 collective-permute-start.9
  28.1 1.5 collective-permute-start.11
  29.6 0.7 pack_forward.1.refs_15_
  30.3 1.1 collective-permute-done.9.refs_10_
  31.4 1.6 collective-permute-start.22
  34.1 3.9 %project.1 = (bf16[1024,192]{1,0:T(8,128)(2,1)S(1)}, bf16[1024,192]{1,0:T(8,128)(2,1)S(1)}, bf16[1024,192]{1,0:T(8,128)(2,1)S(1)}, bf16[768,576]{1,0:T(8,128)(2,...) custom-call(s32[9]{0:T(128)S(1)} %dynamic-slice_bitcast_fusion.scal., ...), custom_call_target="tpu_custom_call" | custom-call | bytes 16200000 | tf_op jit(solution)/shard_map/project/pallas_call | solution.py:158
  38.0 1.1 collective-permute-done.11.refs_3_
  39.1 1.5 collective-permute-start.10
  40.6 3.4 %attend.2 = (bf16[768,128]{1,0:T(8,128)(2,1)S(1)}, bf16[1024,192]{1,0:T(8,128)(2,1)}, bf16[1024,192]{1,0:T(8,128)(2,1)}, bf16[1024,192]{1,0:T(8,128)(2,1)}, s32[...) custom-call(s32[9]{0:T(128)S(1)} %dynamic-slice_bitcast_fusion.scal., ...), custom_call_target="tpu_custom_call" | custom-call | bytes 12600000 | tf_op jit(solution)/shard_map/attend/pallas_call | solution.py:158
  44.0 1.6 collective-permute-start.24
  46.6 0.7 collective-permute-done.10.refs_13_
  47.3 3.2 %attend.3.refs_4_ = bf16[768,128]{1,0:T(8,128)(2,1)S(1)} custom-call(s32[9]{0:T(128)S(1)} %dynamic-slice_bitcast_fusion.scal.refs_0_, s32[1,1024]{1,0:T(1,128)S(1)} %copy-done.4, bf16[1024,192]{1,0:T(8,128)(2,1)S(1)} %get-tuple-element.151.refs_2_, bf16[1024,192]{1,0:T(8,128)(2,1)S(1)} %get-tuple-element.142.refs_3_, ...), custom_call_target="tpu_custom_call" | custom-call | bytes 12600000 | tf_op jit(solution)/shard_map/attend/pallas_call | solution.py:158
  50.5 1.2 collective-permute-done.12.refs_7_
  51.7 1.3 collective-permute-start.13
  53.1 1.5 collective-permute-start.26
  55.2 2.3 %collective-permute-done.13.refs_8_ = bf16[768,128]{1,0:T(8,128)(2,1)S(1)} collective-permute-done((bf16[768,128]{1,0:T(8,128)(2,1)S(1)}, bf16[768,128]{1,0:T(8,128)(2,1)S(1)}, u32[]{:S(2)}, u32[]{:S(2)}) %collective-permute-start.13) | collective-permute-done | bytes 196640 | tf_op jit(solution)/shard_map/ppermute | solution.py:1073
  57.9 2.2 collective-permute-done.26.refs_20_
  60.1 2.3 %collective-permute-done.27.refs_21_ = bf16[96,1536]{1,0:T(8,128)(2,1)S(1)} collective-permute-done((bf16[96,1536]{1,0:T(8,128)(2,1)S(1)}, bf16[96,1536]{1,0:T(8,128)(2,1)S(1)}, u32[]{:S(2)}, u32[]{:S(2)}) %collective-permute-start.27) | collective-permute-done | bytes 294944 | tf_op jit(solution)/shard_map/ppermute | solution.py:1131
  62.9 2.0 collective-permute-start.28
  66.7 5.2 %collective-permute-done.28.refs_22_ = bf16[96,1536]{1,0:T(8,128)(2,1)S(1)} collective-permute-done((bf16[96,1536]{1,0:T(8,128)(2,1)S(1)}, bf16[96,1536]{1,0:T(8,128)(2,1)S(1)}, u32[]{:S(2)}, u32[]{:S(2)}) %collective-permute-start.28) | collective-permute-done | bytes 294944 | tf_op jit(solution)/shard_map/ppermute | solution.py:1128
  71.9 11.2 %forward_back.1 = (bf16[1024,768]{1,0:T(8,128)(2,1)S(1)}, bf16[1024,768]{1,0:T(8,128)(2,1)S(1)}, bf16[1024,768]{1,0:T(8,128)(2,1)S(1)}, f32[512,768]{1,0:T(8,128...) custom-call(s32[9]{0:T(128)S(1)} %dynamic-slice_bitcast_fusion.scal., ...), custom_call_target="tpu_custom_call" | custom-call | bytes 46800000 | tf_op jit(solution)/shard_map/forward_back/pallas_call | solution.py:158
  83.2 5.1 %forward_grads.1 = (bf16[768,1536]{1,0:T(8,128)(2,1)}, bf16[1024,768]{1,0:T(8,128)(2,1)}, f32[256,768]{1,0:T(8,128)}, f32[8,768]{1,0:T(8,128)}, bf16[192,768]{1,...) custom-call(s32[9]{0:T(128)S(1)} %dynamic-slice_bitcast_fusion.scal.refs_0_, ...), custom_call_target="tpu_custom_call" | custom-call | bytes 14400000 | tf_op jit(solution)/shard_map/forward_grads/pallas_call | solution.py:158
  88.4 4.4 %all-to-all-start.1 = ((bf16[8,96,1536]{2,1,0:T(8,128)(2,1)}), bf16[8,96,1536]{2,1,0:T(8,128)(2,1)}, u32[]{:S(2)}, u32[]{:S(2)}) async-start(bf16[8,96,1536]{2,1,0:T(8,128)(2,1)} %bitcast.2), calls=%async_computation.1 | async-start | bytes 4718592 | tf_op jit(solution)/shard_map/all_to_all | solution.py:1143
  93.6 6.1 %branch_part.1 = (f32[512,768]{1,0:T(8,128)}, bf16[512,768]{1,0:T(8,128)(2,1)S(1)}, bf16[256,768]{1,0:T(8,128)(2,1)S(1)}) custom-call(s32[9]{0:T(128)S(1)} %dynamic-slice_bitcast_fusion.scal.refs_0_, bf16[1024,768]{1,0:T(8,128)(2,1)} %get-tuple-element.174.refs_1_, bf16[768,1536]{1,0:T(8,128)(2,1)} %get-tuple-element.181.refs_2_, bf16[256,768]{1,0:T(8,128)(2,1)} %refs_3_.4), custom_call_target="tpu_custom_call" | custom-call | bytes 10800000 | tf_op jit(solution)/shard_map/branch_part/pallas_call | solution.py:158
  99.7 5.3 %collective-permute-done.30.refs_2_ = bf16[256,768]{1,0:T(8,128)(2,1)S(1)} collective-permute-done((bf16[256,768]{1,0:T(8,128)(2,1)S(1)}, bf16[256,768]{1,0:T(8,128)(2,1)S(1)}, u32[]{:S(2)}, u32[]{:S(2)}) %collective-permute-start.30) | collective-permute-done | bytes 393248 | tf_op jit(solution)/shard_map/ppermute | solution.py:1073
  105.0 1.2 resid_back.1
  106.8 11.0 %collective-permute-done.34.refs_3_ = bf16[256,768]{1,0:T(8,128)(2,1)S(1)} collective-permute-done((bf16[256,768]{1,0:T(8,128)(2,1)S(1)}, bf16[256,768]{1,0:T(8,128)(2,1)S(1)}, u32[]{:S(2)}, u32[]{:S(2)}) %collective-permute-start.34) | collective-permute-done | bytes 393248 | tf_op jit(solution)/shard_map/ppermute | solution.py:1073
  117.9 2.1 merge.4
  120.4 4.3 %mixed_back.1 = (bf16[1024,192]{1,0:T(8,128)(2,1)S(1)}, bf16[768,192]{1,0:T(8,128)(2,1)S(1)}) custom-call(s32[9]{0:T(128)S(1)} %dynamic-slice_bitcast_fusion.scal.refs_0_, bf16[256,768]{1,0:T(8,128)(2,1)S(1)} %get-tuple-element.197.refs_1_, bf16[256,768]{1,0:T(8,128)(2,1)S(1)} %collective-permute-done.33.refs_2_, ...), custom_call_target="tpu_custom_call" | custom-call | bytes 9000000 | tf_op jit(solution)/shard_map/mixed_back/pallas_call | solution.py:158
  124.6 12.2 %attend_back.1 = (bf16[1024,576]{1,0:T(8,128)(2,1)S(1)}, f32[256,768]{1,0:T(8,128)}, f32[8,768]{1,0:T(8,128)}, bf16[768,192]{1,0:T(8,128)(2,1)}) custom-call(s32[9]{0:T(128)S(1)} %dynamic-slice_bitcast_fusion.scal.refs_0_, s32[1,1024]{1,0:T(1,128)S(1)} %copy-done.4, bf16[1024,192]{1,0:T(8,128)(2,1)} %get-tuple-element.194.refs_2_, ...), custom_call_target="tpu_custom_call" | custom-call | bytes 57600000 | tf_op jit(solution)/shard_map/attend_back/pallas_call | solution.py:158
  136.9 0.7 copy-done.6
  137.6 8.8 %query_grads.1 = bf16[768,896]{1,0:T(8,128)(2,1)} custom-call(s32[9]{0:T(128)S(1)} %dynamic-slice_bitcast_fusion.scal.refs_0_, bf16[1024,768]{1,0:T(8,128)(2,1)} %get-tuple-element.192.refs_1_, bf16[1024,768]{1,0:T(8,128)(2,1)} %get-tuple-element.193.refs_2_, bf16[768,192]{1,0:T(8,128)(2,1)} %get-tuple-element.205.refs_3_, ...), custom_call_target="tpu_custom_call" | custom-call | bytes 14400000 | tf_op jit(solution)/shard_map/query_grads/pallas_call | solution.py:158
  146.4 1.1 all-to-all-done.1.refs_1_
  147.5 4.8 %all-to-all-start = ((bf16[8,96,896]{2,1,0:T(8,128)(2,1)}), bf16[8,96,896]{2,1,0:T(8,128)(2,1)S(1)}, u32[]{:S(2)}, u32[]{:S(2)}) async-start(bf16[8,96,896]{2,1,0:T(8,128)(2,1)} %bitcast.6), calls=%async_computation | async-start | bytes 2752512 | tf_op jit(solution)/shard_map/all_to_all | solution.py:1143
  152.3 3.9 %project_back.1 = (f32[512,768]{1,0:T(8,128)S(1)}, bf16[512,768]{1,0:T(8,128)(2,1)S(1)}) custom-call(s32[9]{0:T(128)S(1)} %dynamic-slice_bitcast_fusion.scal.refs_0_, bf16[1024,576]{1,0:T(8,128)(2,1)S(1)} %get-tuple-element.206.refs_4_.refs_1_, bf16[768,576]{1,0:T(8,128)(2,1)} %get-tuple-element.213.refs_5_.refs_2_), custom_call_target="tpu_custom_call" | custom-call | bytes 10800000 | tf_op jit(solution)/shard_map/project_back/pallas_call | solution.py:158
  156.5 2.5 %owned_sum.1.refs_1_ = bf16[96,1536]{1,0:T(8,128)(2,1)S(1)} custom-call(s32[9]{0:T(128)S(1)} %dynamic-slice_bitcast_fusion.scal.refs_0_, bf16[8,96,1536]{2,1,0:T(8,128)(2,1)} %all-to-all-done.1.refs_1_), custom_call_target="tpu_custom_call" | custom-call | bytes 5400000 | tf_op jit(solution)/shard_map/owned_sum/pallas_call | solution.py:158
  159.0 1.7 collective-permute-start.39
  161.9 7.0 %collective-permute-done.39.refs_3_ = bf16[96,1536]{1,0:T(8,128)(2,1)S(1)} collective-permute-done((bf16[96,1536]{1,0:T(8,128)(2,1)S(1)}, bf16[96,1536]{1,0:T(8,128)(2,1)S(1)}, u32[]{:S(2)}, u32[]{:S(2)}) %collective-permute-start.39) | collective-permute-done | bytes 294944 | tf_op jit(solution)/shard_map/ppermute | solution.py:1073
  168.9 2.7 %output_sum.1 = bf16[256,768]{1,0:T(8,128)(2,1)} custom-call(s32[9]{0:T(128)S(1)} %dynamic-slice_bitcast_fusion.scal.refs_0_, f32[256,768]{1,0:T(8,128)S(1)} %get-tuple-element.210.refs_1_, bf16[256,768]{1,0:T(8,128)(2,1)} %copy-done.6, f32[256,768]{1,0:T(8,128)} %get-tuple-element.211.refs_3_, f32[16,768]{1,0:T(8,128)} %get-tuple-element.212.refs_4_.refs_5_), custom_call_target="tpu_custom_call" | custom-call | bytes 2880000 | tf_op jit(solution)/shard_map/output_sum/pallas_call | solution.py:158
  171.6 1.6 squares_of.1
  173.2 3.7 %collective-permute-done.37.refs_2_ = bf16[256,768]{1,0:T(8,128)(2,1)} collective-permute-done((bf16[256,768]{1,0:T(8,128)(2,1)S(1)}, bf16[256,768]{1,0:T(8,128)(2,1)}, u32[]{:S(2)}, u32[]{:S(2)}) %collective-permute-start.37) | collective-permute-done | bytes 393248 | tf_op jit(solution)/shard_map/ppermute | solution.py:1073
  176.9 8.8 %all-to-all-done.refs_1_ = bf16[8,96,896]{2,1,0:T(8,128)(2,1)S(1)} async-done(((bf16[8,96,896]{2,1,0:T(8,128)(2,1)}), bf16[8,96,896]{2,1,0:T(8,128)(2,1)S(1)}, u32[]{:S(2)}, u32[]{:S(2)}) %all-to-all-start) | async-done | bytes 1376288 | tf_op jit(solution)/shard_map/all_to_all | solution.py:1143
  185.7 0.7 owned_vector.1.refs_1_
  186.4 1.7 collective-permute-start.42
  188.2 4.4 %collective-permute-done.42.refs_3_ = bf16[96,1024]{1,0:T(8,128)(2,1)S(1)} collective-permute-done((bf16[96,1024]{1,0:T(8,128)(2,1)S(1)}, bf16[96,1024]{1,0:T(8,128)(2,1)S(1)}, u32[]{:S(2)}, u32[]{:S(2)}) %collective-permute-start.42) | collective-permute-done | bytes 196640 | tf_op jit(solution)/shard_map/ppermute | solution.py:1073
  192.6 1.4 collective-permute-done.43.refs_4_
  194.1 2.1 join.1
  196.2 4.4 %all-to-all-start.2 = ((f32[8,8,128]{2,1,0:T(8,128)}), f32[8,8,128]{2,1,0:T(8,128)S(1)}, u32[]{:S(2)}, u32[]{:S(2)}) async-start(f32[8,8,128]{2,1,0:T(8,128)} %bitcast.3), calls=%async_computation.2 | async-start | bytes 65536 | tf_op jit(solution)/shard_map/all_to_all | solution.py:1303
  200.5 3.3 %input_back.1 = f32[256,768]{1,0:T(8,128)} custom-call(s32[9]{0:T(128)S(1)} %dynamic-slice_bitcast_fusion.scal.refs_0_, f32[256,768]{1,0:T(8,128)S(1)} %get-tuple-element.216.refs_1_, bf16[256,768]{1,0:T(8,128)(2,1)} %collective-permute-done.37.refs_2_, bf16[256,768]{1,0:T(8,128)(2,1)} %refs_3_.5, f32[256,768]{1,0:T(8,128)} %get-tuple-element.218.refs_4_, ...), custom_call_target="tpu_custom_call" | custom-call | bytes 3600000 | tf_op jit(solution)/shard_map/input_back/pallas_call | solution.py:158
  203.9 3.3 %all-to-all-done.2.total_ref = f32[8,8,128]{2,1,0:T(8,128)S(1)} async-done(((f32[8,8,128]{2,1,0:T(8,128)}), f32[8,8,128]{2,1,0:T(8,128)S(1)}, u32[]{:S(2)}, u32[]{:S(2)}) %all-to-all-start.2) | async-done | bytes 32800 | tf_op jit(solution)/shard_map/all_to_all | solution.py:1303
  207.2 12.8 %adam.1 = (f32[96,3072]{1,0:T(8,128)}, f32[96,6144]{1,0:T(8,128)}, f32[12,96]{1,0:T(8,128)}, f32[96,3072]{1,0:T(8,128)}, f32[96,6144]{1,0:T(8,128)}, /*index=5*/...) custom-call(s32[9]{0:T(128)S(1)} %dynamic-slice_bitcast_fusion.scal., ...), custom_call_target="tpu_custom_call" | custom-call | bytes 32400000 | tf_op jit(solution)/shard_map/adam/pallas_call | solution.py:1041
  (71 shorter events, 11.0 us)
Async XLA Ops:
  1.4 1.3 copy-start
  2.6 0.7 copy-start.5
  3.3 11.7 %copy-start.3 = (bf16[256,768]{1,0:T(8,128)(2,1)S(1)}, bf16[256,768]{1,0:T(8,128)(2,1)}, u32[]{:S(2)}) copy-start(bf16[256,768]{1,0:T(8,128)(2,1)} %refs_3_.5) | copy-start | bytes 1179652
  3.3 24.7 %copy-start.2 = (bf16[256,768]{1,0:T(8,128)(2,1)S(1)}, bf16[256,768]{1,0:T(8,128)(2,1)}, u32[]{:S(2)}) copy-start(bf16[256,768]{1,0:T(8,128)(2,1)} %refs_3_.4) | copy-start | bytes 1179652
  3.3 26.2 %copy-start.1 = (f32[96,6144]{1,0:T(8,128)S(1)}, f32[96,6144]{1,0:T(8,128)}, u32[]{:S(2)}) copy-start(f32[96,6144]{1,0:T(8,128)} %refs_8_.1) | copy-start | bytes 7077892
  4.2 7.5 %collective-permute-start.2 = (bf16[96,896]{1,0:T(8,128)(2,1)S(1)}, bf16[96,896]{1,0:T(8,128)(2,1)S(1)}, u32[]{:S(2)}, u32[]{:S(2)}) collective-permute-start(bf16[96,896]{1,0:T(8,128)(2,1)S(1)} %pack_attention.1.refs_3_), channel_id=1, source_target_pairs={{8,0},{16,8},{24,16},{28,24},{20,28},{12,20},{4,12},{0,4},{9,1},{1... | collective-permute-start | bytes 516104 | tf_op jit(solution)/shard_map/ppermute | solution.py:1131
  7.2 5.8 %collective-permute-start.1 = (bf16[96,896]{1,0:T(8,128)(2,1)S(1)}, bf16[96,896]{1,0:T(8,128)(2,1)S(1)}, u32[]{:S(2)}, u32[]{:S(2)}) collective-permute-start(bf16[96,896]{1,0:T(8,128)(2,1)S(1)} %pack_attention.1.refs_3_), channel_id=1, source_target_pairs={{0,8},{8,16},{16,24},{24,28},{28,20},{20,12},{12,4},{4,0},{1,9},{9... | collective-permute-start | bytes 516104 | tf_op jit(solution)/shard_map/ppermute | solution.py:1128
  13.0 5.4 %collective-permute-start.3 = (bf16[96,896]{1,0:T(8,128)(2,1)S(1)}, bf16[96,896]{1,0:T(8,128)(2,1)S(1)}, u32[]{:S(2)}, u32[]{:S(2)}) collective-permute-start(bf16[96,896]{1,0:T(8,128)(2,1)S(1)} %collective-permute-done.1.refs_4_), channel_id=1, source_target_pairs={{0,8},{8,16},{16,24},{24,28},{28,20},{20,12},{12,4},{4,0},{1,9},{9... | collective-permute-start | bytes 516104 | tf_op jit(solution)/shard_map/ppermute | solution.py:1128
  13.5 5.4 %collective-permute-start.4 = (bf16[96,896]{1,0:T(8,128)(2,1)S(1)}, bf16[96,896]{1,0:T(8,128)(2,1)S(1)}, u32[]{:S(2)}, u32[]{:S(2)}) collective-permute-start(bf16[96,896]{1,0:T(8,128)(2,1)S(1)} %collective-permute-done.2.refs_5_), channel_id=1, source_target_pairs={{8,0},{16,8},{24,16},{28,24},{20,28},{12,20},{4,12},{0,4},{9,1},{1... | collective-permute-start | bytes 516104 | tf_op jit(solution)/shard_map/ppermute | solution.py:1131
  15.1 12.5 %collective-permute-start = (bf16[256,768]{1,0:T(8,128)(2,1)S(1)}, bf16[256,768]{1,0:T(8,128)(2,1)S(1)}, u32[]{:S(2)}, u32[]{:S(2)}) collective-permute-start(bf16[256,768]{1,0:T(8,128)(2,1)S(1)} %copy-done.3), channel_id=1, source_target_pairs={{0,2},{1,3},{2,0},{3,1},{4,6},{5,7},{6,4},{7,5},{8,10},{9,11},{10,... | collective-permute-start | bytes 1179656 | tf_op jit(solution)/shard_map/ppermute | solution.py:1073
  18.9 5.4 %collective-permute-start.5 = (bf16[96,896]{1,0:T(8,128)(2,1)S(1)}, bf16[96,896]{1,0:T(8,128)(2,1)S(1)}, u32[]{:S(2)}, u32[]{:S(2)}) collective-permute-start(bf16[96,896]{1,0:T(8,128)(2,1)S(1)} %collective-permute-done.3.refs_6_), channel_id=1, source_target_pairs={{0,8},{8,16},{16,24},{24,28},{28,20},{20,12},{12,4},{4,0},{1,9},{9... | collective-permute-start | bytes 516104 | tf_op jit(solution)/shard_map/ppermute | solution.py:1128
  20.6 5.4 %collective-permute-start.6 = (bf16[96,896]{1,0:T(8,128)(2,1)S(1)}, bf16[96,896]{1,0:T(8,128)(2,1)S(1)}, u32[]{:S(2)}, u32[]{:S(2)}) collective-permute-start(bf16[96,896]{1,0:T(8,128)(2,1)S(1)} %collective-permute-done.4.refs_7_), channel_id=1, source_target_pairs={{8,0},{16,8},{24,16},{28,24},{20,28},{12,20},{4,12},{0,4},{9,1},{1... | collective-permute-start | bytes 516104 | tf_op jit(solution)/shard_map/ppermute | solution.py:1131
  26.0 5.4 %collective-permute-start.9 = (bf16[96,896]{1,0:T(8,128)(2,1)S(1)}, bf16[96,896]{1,0:T(8,128)(2,1)S(1)}, u32[]{:S(2)}, u32[]{:S(2)}) collective-permute-start(bf16[96,896]{1,0:T(8,128)(2,1)S(1)} %collective-permute-done.5.refs_8_), channel_id=1, source_target_pairs={{0,8},{8,16},{16,24},{24,28},{28,20},{20,12},{12,4},{4,0},{1,9},{9... | collective-permute-start | bytes 516104 | tf_op jit(solution)/shard_map/ppermute | solution.py:1128
  27.5 5.9 %collective-permute-start.7 = (bf16[256,768]{1,0:T(8,128)(2,1)S(1)}, bf16[256,768]{1,0:T(8,128)(2,1)S(1)}, u32[]{:S(2)}, u32[]{:S(2)}) collective-permute-start(bf16[256,768]{1,0:T(8,128)(2,1)S(1)} %copy-done.3), channel_id=1, source_target_pairs={{0,1},{1,0},{2,3},{3,2},{4,5},{5,4},{6,7},{7,6},{8,9},{9,8},{10,11... | collective-permute-start | bytes 1179656 | tf_op jit(solution)/shard_map/ppermute | solution.py:1073
  27.5 5.9 %collective-permute-start.8 = (bf16[256,768]{1,0:T(8,128)(2,1)S(1)}, bf16[256,768]{1,0:T(8,128)(2,1)S(1)}, u32[]{:S(2)}, u32[]{:S(2)}) collective-permute-start(bf16[256,768]{1,0:T(8,128)(2,1)S(1)} %collective-permute-done.refs_3_), channel_id=1, source_target_pairs={{0,1},{1,0},{2,3},{3,2},{4,5},{5,4},{6,7},{7,6},{8,9},{9,8},{10,11... | collective-permute-start | bytes 1179656 | tf_op jit(solution)/shard_map/ppermute | solution.py:1073
  28.1 11.0 %collective-permute-start.11 = (bf16[256,768]{1,0:T(8,128)(2,1)S(1)}, bf16[256,768]{1,0:T(8,128)(2,1)S(1)}, u32[]{:S(2)}, u32[]{:S(2)}) collective-permute-start(bf16[256,768]{1,0:T(8,128)(2,1)S(1)} %copy-done.2), channel_id=1, source_target_pairs={{0,2},{1,3},{2,0},{3,1},{4,6},{5,7},{6,4},{7,5},{8,10},{9,11},{10,... | collective-permute-start | bytes 1179656 | tf_op jit(solution)/shard_map/ppermute | solution.py:1073
  30.3 3.8 %copy-start.4 = (s32[1,1024]{1,0:T(1,128)S(1)}, s32[1,1024]{1,0:T(1,128)}, u32[]{:S(2)}) copy-start(s32[1,1024]{1,0:T(1,128)} %refs_6_.2) | copy-start | bytes 12292
  31.4 12.6 %collective-permute-start.22 = (bf16[96,1536]{1,0:T(8,128)(2,1)S(1)}, bf16[96,1536]{1,0:T(8,128)(2,1)S(1)}, u32[]{:S(2)}, u32[]{:S(2)}) collective-permute-start(bf16[96,1536]{1,0:T(8,128)(2,1)S(1)} %pack_forward.1.refs_15_), channel_id=1, source_target_pairs={{0,8},{8,16},{16,24},{24,28},{28,20},{20,12},{12,4},{4,0},{1,9},{9... | collective-permute-start | bytes 884744 | tf_op jit(solution)/shard_map/ppermute | solution.py:1128
  32.9 11.0 %collective-permute-start.23 = (bf16[96,1536]{1,0:T(8,128)(2,1)S(1)}, bf16[96,1536]{1,0:T(8,128)(2,1)S(1)}, u32[]{:S(2)}, u32[]{:S(2)}) collective-permute-start(bf16[96,1536]{1,0:T(8,128)(2,1)S(1)} %pack_forward.1.refs_15_), channel_id=1, source_target_pairs={{8,0},{16,8},{24,16},{28,24},{20,28},{12,20},{4,12},{0,4},{9,1},{1... | collective-permute-start | bytes 884744 | tf_op jit(solution)/shard_map/ppermute | solution.py:1131
  39.1 8.2 %collective-permute-start.10 = (bf16[1152,128]{1,0:T(8,128)(2,1)S(1)}, bf16[1152,128]{1,0:T(8,128)(2,1)S(1)}, u32[]{:S(2)}, u32[]{:S(2)}) collective-permute-start(bf16[1152,128]{1,0:T(8,128)(2,1)S(1)} %get-tuple-element.157.refs_11_), channel_id=1, source_target_pairs={{0,2},{1,3},{2,0},{3,1},{4,6},{5,7},{6,4},{7,5},{8,10},{9,11},{10,... | collective-permute-start | bytes 884744 | tf_op jit(solution)/shard_map/ppermute | solution.py:1073
  44.0 9.1 %collective-permute-start.24 = (bf16[96,1536]{1,0:T(8,128)(2,1)S(1)}, bf16[96,1536]{1,0:T(8,128)(2,1)S(1)}, u32[]{:S(2)}, u32[]{:S(2)}) collective-permute-start(bf16[96,1536]{1,0:T(8,128)(2,1)S(1)} %collective-permute-done.22.refs_16_), channel_id=1, source_target_pairs={{0,8},{8,16},{16,24},{24,28},{28,20},{20,12},{12,4},{4,0},{1,9},{9... | collective-permute-start | bytes 884744 | tf_op jit(solution)/shard_map/ppermute | solution.py:1128
  45.6 7.5 %collective-permute-start.25 = (bf16[96,1536]{1,0:T(8,128)(2,1)S(1)}, bf16[96,1536]{1,0:T(8,128)(2,1)S(1)}, u32[]{:S(2)}, u32[]{:S(2)}) collective-permute-start(bf16[96,1536]{1,0:T(8,128)(2,1)S(1)} %collective-permute-done.23.refs_17_), channel_id=1, source_target_pairs={{8,0},{16,8},{24,16},{28,24},{20,28},{12,20},{4,12},{0,4},{9,1},{1... | collective-permute-start | bytes 884744 | tf_op jit(solution)/shard_map/ppermute | solution.py:1131
  46.1 5.7 %collective-permute-start.12 = (bf16[768,128]{1,0:T(8,128)(2,1)S(1)}, bf16[768,128]{1,0:T(8,128)(2,1)S(1)}, u32[]{:S(2)}, u32[]{:S(2)}) collective-permute-start(bf16[768,128]{1,0:T(8,128)(2,1)S(1)} %get-tuple-element.155.refs_3_), channel_id=1, source_target_pairs={{0,2},{1,3},{2,0},{3,1},{4,6},{5,7},{6,4},{7,5},{8,10},{9,11},{10,... | collective-permute-start | bytes 589832 | tf_op jit(solution)/shard_map/ppermute | solution.py:1073
  51.7 5.7 %collective-permute-start.13 = (bf16[768,128]{1,0:T(8,128)(2,1)S(1)}, bf16[768,128]{1,0:T(8,128)(2,1)S(1)}, u32[]{:S(2)}, u32[]{:S(2)}) collective-permute-start(bf16[768,128]{1,0:T(8,128)(2,1)S(1)} %attend.3.refs_4_), channel_id=1, source_target_pairs={{0,2},{1,3},{2,0},{3,1},{4,6},{5,7},{6,4},{7,5},{8,10},{9,11},{10,... | collective-permute-start | bytes 589832 | tf_op jit(solution)/shard_map/ppermute | solution.py:1073
  53.1 7.0 %collective-permute-start.26 = (bf16[96,1536]{1,0:T(8,128)(2,1)S(1)}, bf16[96,1536]{1,0:T(8,128)(2,1)S(1)}, u32[]{:S(2)}, u32[]{:S(2)}) collective-permute-start(bf16[96,1536]{1,0:T(8,128)(2,1)S(1)} %collective-permute-done.24.refs_18_), channel_id=1, source_target_pairs={{0,8},{8,16},{16,24},{24,28},{28,20},{20,12},{12,4},{4,0},{1,9},{9... | collective-permute-start | bytes 884744 | tf_op jit(solution)/shard_map/ppermute | solution.py:1128
  54.7 7.8 %collective-permute-start.27 = (bf16[96,1536]{1,0:T(8,128)(2,1)S(1)}, bf16[96,1536]{1,0:T(8,128)(2,1)S(1)}, u32[]{:S(2)}, u32[]{:S(2)}) collective-permute-start(bf16[96,1536]{1,0:T(8,128)(2,1)S(1)} %collective-permute-done.25.refs_19_), channel_id=1, source_target_pairs={{8,0},{16,8},{24,16},{28,24},{20,28},{12,20},{4,12},{0,4},{9,1},{1... | collective-permute-start | bytes 884744 | tf_op jit(solution)/shard_map/ppermute | solution.py:1131
  57.4 7.6 %collective-permute-start.14 = (bf16[256,768]{1,0:T(8,128)(2,1)S(1)}, bf16[256,768]{1,0:T(8,128)(2,1)S(1)}, u32[]{:S(2)}, u32[]{:S(2)}) collective-permute-start(bf16[256,768]{1,0:T(8,128)(2,1)S(1)} %copy-done.2), channel_id=1, source_target_pairs={{0,1},{1,0},{2,3},{3,2},{4,5},{5,4},{6,7},{7,6},{8,9},{9,8},{10,11... | collective-permute-start | bytes 1179656 | tf_op jit(solution)/shard_map/ppermute | solution.py:1073
  57.4 7.6 %collective-permute-start.15 = (bf16[256,768]{1,0:T(8,128)(2,1)S(1)}, bf16[256,768]{1,0:T(8,128)(2,1)S(1)}, u32[]{:S(2)}, u32[]{:S(2)}) collective-permute-start(bf16[256,768]{1,0:T(8,128)(2,1)S(1)} %collective-permute-done.11.refs_3_), channel_id=1, source_target_pairs={{0,1},{1,0},{2,3},{3,2},{4,5},{5,4},{6,7},{7,6},{8,9},{9,8},{10,11... | collective-permute-start | bytes 1179656 | tf_op jit(solution)/shard_map/ppermute | solution.py:1073
  57.9 4.5 %collective-permute-start.17 = (bf16[768,128]{1,0:T(8,128)(2,1)S(1)}, bf16[768,128]{1,0:T(8,128)(2,1)S(1)}, u32[]{:S(2)}, u32[]{:S(2)}) collective-permute-start(bf16[768,128]{1,0:T(8,128)(2,1)S(1)} %attend.3.refs_4_), channel_id=1, source_target_pairs={{0,1},{1,0},{2,3},{3,2},{4,5},{5,4},{6,7},{7,6},{8,9},{9,8},{10,11... | collective-permute-start | bytes 589832 | tf_op jit(solution)/shard_map/ppermute | solution.py:1073
  60.1 2.8 %collective-permute-start.16 = (bf16[768,128]{1,0:T(8,128)(2,1)S(1)}, bf16[768,128]{1,0:T(8,128)(2,1)S(1)}, u32[]{:S(2)}, u32[]{:S(2)}) collective-permute-start(bf16[768,128]{1,0:T(8,128)(2,1)S(1)} %get-tuple-element.155.refs_3_), channel_id=1, source_target_pairs={{0,1},{1,0},{2,3},{3,2},{4,5},{5,4},{6,7},{7,6},{8,9},{9,8},{10,11... | collective-permute-start | bytes 589832 | tf_op jit(solution)/shard_map/ppermute | solution.py:1073
  62.4 4.3 %collective-permute-start.20 = (bf16[1152,128]{1,0:T(8,128)(2,1)S(1)}, bf16[1152,128]{1,0:T(8,128)(2,1)S(1)}, u32[]{:S(2)}, u32[]{:S(2)}) collective-permute-start(bf16[1152,128]{1,0:T(8,128)(2,1)S(1)} %get-tuple-element.157.refs_11_), channel_id=1, source_target_pairs={{0,1},{1,0},{2,3},{3,2},{4,5},{5,4},{6,7},{7,6},{8,9},{9,8},{10,11... | collective-permute-start | bytes 884744 | tf_op jit(solution)/shard_map/ppermute | solution.py:1073
  62.4 4.3 %collective-permute-start.21 = (bf16[1152,128]{1,0:T(8,128)(2,1)S(1)}, bf16[1152,128]{1,0:T(8,128)(2,1)S(1)}, u32[]{:S(2)}, u32[]{:S(2)}) collective-permute-start(bf16[1152,128]{1,0:T(8,128)(2,1)S(1)} %collective-permute-done.10.refs_13_), channel_id=1, source_target_pairs={{0,1},{1,0},{2,3},{3,2},{4,5},{5,4},{6,7},{7,6},{8,9},{9,8},{10,11... | collective-permute-start | bytes 884744 | tf_op jit(solution)/shard_map/ppermute | solution.py:1073
  62.9 9.0 %collective-permute-start.28 = (bf16[96,1536]{1,0:T(8,128)(2,1)S(1)}, bf16[96,1536]{1,0:T(8,128)(2,1)S(1)}, u32[]{:S(2)}, u32[]{:S(2)}) collective-permute-start(bf16[96,1536]{1,0:T(8,128)(2,1)S(1)} %collective-permute-done.26.refs_20_), channel_id=1, source_target_pairs={{0,8},{8,16},{16,24},{24,28},{28,20},{20,12},{12,4},{4,0},{1,9},{9... | collective-permute-start | bytes 884744 | tf_op jit(solution)/shard_map/ppermute | solution.py:1128
  65.0 1.4 collective-permute-start.18
  65.0 1.7 collective-permute-start.19
  83.1 5.2 %collective-permute-start.29 = (bf16[512,768]{1,0:T(8,128)(2,1)S(1)}, bf16[512,768]{1,0:T(8,128)(2,1)S(1)}, u32[]{:S(2)}, u32[]{:S(2)}) collective-permute-start(bf16[512,768]{1,0:T(8,128)(2,1)S(1)} %get-tuple-element.178), channel_id=1, source_target_pairs={{0,1},{1,0},{2,3},{3,2},{4,5},{5,4},{6,7},{7,6},{8,9},{9,8},{10,11... | collective-permute-start | bytes 2359304 | tf_op jit(solution)/shard_map/ppermute | solution.py:1073
  88.4 59.2 %all-to-all-start.1 = ((bf16[8,96,1536]{2,1,0:T(8,128)(2,1)}), bf16[8,96,1536]{2,1,0:T(8,128)(2,1)}, u32[]{:S(2)}, u32[]{:S(2)}) async-start(bf16[8,96,1536]{2,1,0:T(8,128)(2,1)} %bitcast.2), calls=%async_computation.1 | async-start | bytes 4718592 | tf_op jit(solution)/shard_map/all_to_all | solution.py:1143
  93.5 11.6 %collective-permute-start.30 = (bf16[256,768]{1,0:T(8,128)(2,1)S(1)}, bf16[256,768]{1,0:T(8,128)(2,1)S(1)}, u32[]{:S(2)}, u32[]{:S(2)}) collective-permute-start(bf16[256,768]{1,0:T(8,128)(2,1)S(1)} %get-tuple-element.180), channel_id=1, source_target_pairs={{0,2},{1,3},{2,0},{3,1},{4,6},{5,7},{6,4},{7,5},{8,10},{9,11},{10,... | collective-permute-start | bytes 1179656 | tf_op jit(solution)/shard_map/ppermute | solution.py:1073
  106.2 11.6 %collective-permute-start.31 = (bf16[512,768]{1,0:T(8,128)(2,1)S(1)}, bf16[512,768]{1,0:T(8,128)(2,1)S(1)}, u32[]{:S(2)}, u32[]{:S(2)}) collective-permute-start(bf16[512,768]{1,0:T(8,128)(2,1)S(1)} %get-tuple-element.188), channel_id=1, source_target_pairs={{0,1},{1,0},{2,3},{3,2},{4,5},{5,4},{6,7},{7,6},{8,9},{9,8},{10,11... | collective-permute-start | bytes 2359304 | tf_op jit(solution)/shard_map/ppermute | solution.py:1073
  106.3 11.5 %collective-permute-start.34 = (bf16[256,768]{1,0:T(8,128)(2,1)S(1)}, bf16[256,768]{1,0:T(8,128)(2,1)S(1)}, u32[]{:S(2)}, u32[]{:S(2)}) collective-permute-start(bf16[256,768]{1,0:T(8,128)(2,1)S(1)} %get-tuple-element.197.refs_1_), channel_id=1, source_target_pairs={{0,2},{1,3},{2,0},{3,1},{4,6},{5,7},{6,4},{7,5},{8,10},{9,11},{10,... | collective-permute-start | bytes 1179656 | tf_op jit(solution)/shard_map/ppermute | solution.py:1073
  106.7 13.7 %collective-permute-start.33 = (bf16[256,768]{1,0:T(8,128)(2,1)S(1)}, bf16[256,768]{1,0:T(8,128)(2,1)S(1)}, u32[]{:S(2)}, u32[]{:S(2)}) collective-permute-start(bf16[256,768]{1,0:T(8,128)(2,1)S(1)} %get-tuple-element.197.refs_1_), channel_id=1, source_target_pairs={{0,1},{1,0},{2,3},{3,2},{4,5},{5,4},{6,7},{7,6},{8,9},{9,8},{10,11... | collective-permute-start | bytes 1179656 | tf_op jit(solution)/shard_map/ppermute | solution.py:1073
  117.8 2.5 %collective-permute-start.35 = (bf16[256,768]{1,0:T(8,128)(2,1)S(1)}, bf16[256,768]{1,0:T(8,128)(2,1)S(1)}, u32[]{:S(2)}, u32[]{:S(2)}) collective-permute-start(bf16[256,768]{1,0:T(8,128)(2,1)S(1)} %collective-permute-done.34.refs_3_), channel_id=1, source_target_pairs={{0,1},{1,0},{2,3},{3,2},{4,5},{5,4},{6,7},{7,6},{8,9},{9,8},{10,11... | collective-permute-start | bytes 1179656 | tf_op jit(solution)/shard_map/ppermute | solution.py:1073
  120.0 16.8 %collective-permute-start.32 = (bf16[256,768]{1,0:T(8,128)(2,1)S(1)}, bf16[256,768]{1,0:T(8,128)(2,1)S(1)}, u32[]{:S(2)}, u32[]{:S(2)}) collective-permute-start(bf16[256,768]{1,0:T(8,128)(2,1)S(1)} %get-tuple-element.191), channel_id=1, source_target_pairs={{0,2},{1,3},{2,0},{3,1},{4,6},{5,7},{6,4},{7,5},{8,10},{9,11},{10,... | collective-permute-start | bytes 1179656 | tf_op jit(solution)/shard_map/ppermute | solution.py:1073
  136.8 0.7 copy-start.6
  147.5 38.2 %all-to-all-start = ((bf16[8,96,896]{2,1,0:T(8,128)(2,1)}), bf16[8,96,896]{2,1,0:T(8,128)(2,1)S(1)}, u32[]{:S(2)}, u32[]{:S(2)}) async-start(bf16[8,96,896]{2,1,0:T(8,128)(2,1)} %bitcast.6), calls=%async_computation | async-start | bytes 2752512 | tf_op jit(solution)/shard_map/all_to_all | solution.py:1143
  156.3 4.5 %collective-permute-start.36 = (bf16[512,768]{1,0:T(8,128)(2,1)S(1)}, bf16[512,768]{1,0:T(8,128)(2,1)S(1)}, u32[]{:S(2)}, u32[]{:S(2)}) collective-permute-start(bf16[512,768]{1,0:T(8,128)(2,1)S(1)} %get-tuple-element.215), channel_id=1, source_target_pairs={{0,1},{1,0},{2,3},{3,2},{4,5},{5,4},{6,7},{7,6},{8,9},{9,8},{10,11... | collective-permute-start | bytes 2359304 | tf_op jit(solution)/shard_map/ppermute | solution.py:1073
  159.0 9.9 %collective-permute-start.39 = (bf16[96,1536]{1,0:T(8,128)(2,1)S(1)}, bf16[96,1536]{1,0:T(8,128)(2,1)S(1)}, u32[]{:S(2)}, u32[]{:S(2)}) collective-permute-start(bf16[96,1536]{1,0:T(8,128)(2,1)S(1)} %owned_sum.1.refs_1_), channel_id=1, source_target_pairs={{0,2},{1,3},{2,0},{3,1},{4,6},{5,7},{6,4},{7,5},{8,10},{9,11},{10,... | collective-permute-start | bytes 884744 | tf_op jit(solution)/shard_map/ppermute | solution.py:1073
  161.4 15.4 %collective-permute-start.37 = (bf16[256,768]{1,0:T(8,128)(2,1)S(1)}, bf16[256,768]{1,0:T(8,128)(2,1)}, u32[]{:S(2)}, u32[]{:S(2)}) collective-permute-start(bf16[256,768]{1,0:T(8,128)(2,1)S(1)} %get-tuple-element.217), channel_id=1, source_target_pairs={{0,2},{1,3},{2,0},{3,1},{4,6},{5,7},{6,4},{7,5},{8,10},{9,11},{10,... | collective-permute-start | bytes 1179656 | tf_op jit(solution)/shard_map/ppermute | solution.py:1073
  161.9 9.7 %collective-permute-start.38 = (bf16[96,1536]{1,0:T(8,128)(2,1)S(1)}, bf16[96,1536]{1,0:T(8,128)(2,1)S(1)}, u32[]{:S(2)}, u32[]{:S(2)}) collective-permute-start(bf16[96,1536]{1,0:T(8,128)(2,1)S(1)} %owned_sum.1.refs_1_), channel_id=1, source_target_pairs={{0,1},{1,0},{2,3},{3,2},{4,5},{5,4},{6,7},{7,6},{8,9},{9,8},{10,11... | collective-permute-start | bytes 884744 | tf_op jit(solution)/shard_map/ppermute | solution.py:1073
  168.9 2.7 %collective-permute-start.40 = (bf16[96,1536]{1,0:T(8,128)(2,1)S(1)}, bf16[96,1536]{1,0:T(8,128)(2,1)S(1)}, u32[]{:S(2)}, u32[]{:S(2)}) collective-permute-start(bf16[96,1536]{1,0:T(8,128)(2,1)S(1)} %collective-permute-done.39.refs_3_), channel_id=1, source_target_pairs={{0,1},{1,0},{2,3},{3,2},{4,5},{5,4},{6,7},{7,6},{8,9},{9,8},{10,11... | collective-permute-start | bytes 884744 | tf_op jit(solution)/shard_map/ppermute | solution.py:1073
  186.4 6.2 %collective-permute-start.42 = (bf16[96,1024]{1,0:T(8,128)(2,1)S(1)}, bf16[96,1024]{1,0:T(8,128)(2,1)S(1)}, u32[]{:S(2)}, u32[]{:S(2)}) collective-permute-start(bf16[96,1024]{1,0:T(8,128)(2,1)S(1)} %owned_vector.1.refs_1_), channel_id=1, source_target_pairs={{0,2},{1,3},{2,0},{3,1},{4,6},{5,7},{6,4},{7,5},{8,10},{9,11},{10,... | collective-permute-start | bytes 589832 | tf_op jit(solution)/shard_map/ppermute | solution.py:1073
  188.2 4.5 %collective-permute-start.41 = (bf16[96,1024]{1,0:T(8,128)(2,1)S(1)}, bf16[96,1024]{1,0:T(8,128)(2,1)S(1)}, u32[]{:S(2)}, u32[]{:S(2)}) collective-permute-start(bf16[96,1024]{1,0:T(8,128)(2,1)S(1)} %owned_vector.1.refs_1_), channel_id=1, source_target_pairs={{0,1},{1,0},{2,3},{3,2},{4,5},{5,4},{6,7},{7,6},{8,9},{9,8},{10,11... | collective-permute-start | bytes 589832 | tf_op jit(solution)/shard_map/ppermute | solution.py:1073
  192.6 1.4 collective-permute-start.43
  196.2 11.0 %all-to-all-start.2 = ((f32[8,8,128]{2,1,0:T(8,128)}), f32[8,8,128]{2,1,0:T(8,128)S(1)}, u32[]{:S(2)}, u32[]{:S(2)}) async-start(f32[8,8,128]{2,1,0:T(8,128)} %bitcast.3), calls=%async_computation.2 | async-start | bytes 65536 | tf_op jit(solution)/shard_map/all_to_all | solution.py:1303
where the time goes:
time: 221 us
  Pallas kernels  95.5 us (43%)
  waiting for transfers between devices  76 us (34%)
  starting transfers between devices  44.2 us (20%)
  local copies, waits for them, and re-layouts  3.94 us (2%)
    pallas_call x22, Pallas kernels, run(): pl.pallas_call(body, out_shape=shapes + [pltpu.HBM(inputs[i].shape, input...  81.1 us
    ppermute x30, waiting for transfers between devices, swap(): return lax.ppermute(part, 'head', [(i, i ^ bit) for i in range(4)])  38.8 us
    ppermute x8, waiting for transfers between devices, hop(): self.front = lax.ppermute(self.front, 'dp', ahead)  15 us
    ppermute x30, starting transfers between devices, swap(): return lax.ppermute(part, 'head', [(i, i ^ bit) for i in range(4)])  13.7 us
    pallas_call x1, Pallas kernels, adam(): pl.pallas_call(functools.partial(adam_kernel, counts), out_shape=out_shap...  12.8 us
    ppermute x8, starting transfers between devices, hop(): self.front = lax.ppermute(self.front, 'dp', ahead)  10.6 us
    all_to_all x2, waiting for transfers between devices, exchange_owned(): return lax.all_to_all(blocks, 'dp', split_axis=0, concat_axis=0)  9.98 us
    all_to_all x2, starting transfers between devices, exchange_owned(): return lax.all_to_all(blocks, 'dp', split_axis=0, concat_axis=0)  9.17 us
  transfers between devices with their start and end apart: 47, of which 25 were waited for; matrix products, arithmetic and copies ran while one was open for 0% of the time, Pallas kernels for 31%

commit v1 on v0

--- a/solution.py
+++ b/solution.py
@@ -112,7 +112,9 @@
     lazy=(),
     save=(),
     far=(),
+    late=(),
     scalars=1,
+    scalar_outputs=(),
 ):
     single = not isinstance(outputs, tuple)
     outputs = [outputs] if single else list(outputs)
@@ -146,9 +148,13 @@
             number += 1
         for copy in copies + stores:
             copy.start()
-        for copy in copies:
-            copy.wait()
-        kernel(*items, *inner)
+        for i, copy in zip(lazy, copies):
+            if i not in late:
+                copy.wait()
+        if late:
+            kernel(*items, *inner, ready=lambda i: copies[lazy.index(i)].wait())
+        else:
+            kernel(*items, *inner)
         for copy in last:
             copy.start()
         for copy in stores + last:
@@ -160,7 +166,10 @@
         out_shape=shapes + [pltpu.HBM(inputs[i].shape, inputs[i].dtype) for i in save],
         in_specs=[smem()] * scalars
         + [far_space() if i in lazy else vmem() for i in range(scalars, count)],
-        out_specs=[far_space() if i in far else vmem() for i in range(produced)]
+        out_specs=[
+            far_space() if i in far else smem() if i in scalar_outputs else vmem()
+            for i in range(produced)
+        ]
         + [far_space()] * len(save),
         scratch_shapes=list(scratch) + buffers,
         compiler_params=params(mebibytes),
@@ -236,8 +245,10 @@
         target[...] = pieces[0][...]
         return
     for i, piece in enumerate(pieces):
-        start = pl.multiple_of(scal[1 + i] * rows, rows)
-        target[pl.ds(start, rows), :] = piece[...]
+        size = piece.shape[0]
+        first = rows - size if i == len(RING) else 0
+        start = pl.multiple_of(scal[1 + i] * rows + first, size)
+        target[pl.ds(start, size), :] = piece[...]
 
 
 def place_members(scal, pieces, target):
@@ -271,8 +282,11 @@
 
 def project_kernel(count, cols, scal, seg_ref, x_ref, *refs):
     pieces = refs[:count]
-    q_ref, k_ref, v_ref, w_ref, wo_ref, vec_ref, col_ref, a_ref, hat_ref = refs[count : 9 + count]
-    weights, wq_ref, wk_ref, wv_ref = refs[9 + count : 13 + count]
+    q_ref, k_ref, v_ref, w_ref, wo_ref, vec_ref, col_ref, a_ref, hat_ref, ranges_ref = refs[
+        count : 10 + count
+    ]
+    weights, wq_ref, wk_ref, wv_ref = refs[10 + count : 14 + count]
+    key_ranges(seg_ref[...], ranges_ref)
     place_rows(scal, pieces, weights)
     for i, ref in enumerate((wq_ref, wk_ref, wv_ref)):
         ref[...] = weights[:, i * cols : (i + 1) * cols]
@@ -312,6 +326,7 @@
         + (shaped((folded_rows(width, cols), 128), BF),)
         + (shaped((16, width), F32), shaped((length, 1), jnp.int32))
         + (shaped((length, width), BF),) * 2
+        + (shaped((16,), jnp.int32),)
     )
     return run(
         functools.partial(project_kernel, len(pieces), cols),
@@ -319,63 +334,68 @@
         outputs,
         (scal, segments, x_all, *pieces),
         4.5,
-        [pltpu.VMEM((width, 4 * cols + 128), BF)] + [pltpu.VMEM((width, cols), BF)] * 3,
-    )
-
-
-CHUNK = 128
-WINDOWS = (4, 5, 8)
-
-
-def key_window(seg, start, size, length):
-    def image(place):
-        number = seg[0, place]
-        return jnp.where(number < 0, length, number)
-
-    first, last = image(start), image(start + size - 1)
-    low, high = jnp.int32(0), jnp.int32(0)
-    for chunk in range(length // CHUNK):
-        low += (image(chunk * CHUNK + CHUNK - 1) < first).astype(jnp.int32)
-        high += (image(chunk * CHUNK) <= last).astype(jnp.int32)
-    return low, high - low
-
-
-def each_window(low, count, length, body):
-    chunks = length // CHUNK
-    sizes = [size for size in WINDOWS if size < chunks] + [chunks]
-    below = 0
-    for size in sizes:
-
-        @pl.when((count > below) & (count <= size))
+        scalar_outputs=(9,),
+        scratch=[pltpu.VMEM((width, 4 * cols + 128), BF)] + [pltpu.VMEM((width, cols), BF)] * 3,
+    )
+
+
+QUERIES = 256
+WINDOWS = (512, 576)
+
+
+def key_ranges(numbers, ranges_ref):
+    length = numbers.shape[1]
+    images = jnp.where(numbers < 0, length, numbers)
+    place = lax.broadcasted_iota(jnp.int32, numbers.shape, 1)
+    for block in range(length // QUERIES):
+        first = jnp.max(jnp.where(place == block * QUERIES, images, 0))
+        last = jnp.max(jnp.where(place == (block + 1) * QUERIES - 1, images, 0))
+        ranges_ref[2 * block] = jnp.sum((images < first).astype(jnp.int32))
+        ranges_ref[2 * block + 1] = jnp.sum((images <= last).astype(jnp.int32))
+
+
+def each_window(ranges, block, length, body):
+    low, high = ranges[2 * block], ranges[2 * block + 1]
+    taken = jnp.bool_(False)
+    for size in [size for size in WINDOWS if size < length] + [length]:
+        start = (jnp.minimum(low, length - size) // 16) * 16
+        fits = high - start <= size
+
+        @pl.when(fits & jnp.logical_not(taken))
         def _():
-            start = jnp.minimum(low, chunks - size) * CHUNK
-            body(pl.multiple_of(start, CHUNK), size * CHUNK)
-
-        below = size
+            body(pl.multiple_of(start, 16), size)
+
+        taken = taken | fits
 
 
 def each_head(per, size, body, carry):
-    if size > WINDOWS[0] * CHUNK:
+    if size > WINDOWS[0]:
         return lax.fori_loop(0, per, body, carry)
     for head in range(per):
         carry = body(head, carry)
     return carry
 
 
-def attend_kernel(per, first, scal, seg, q_ref, k_ref, v_ref, seg_row_ref, seg_col_ref, *refs):
+def attend_kernel(per, first, scal, ranges, q_ref, k_ref, v_ref, seg_row_ref, seg_col_ref, *refs):
     out_ref, held = refs[-2:]
-    block = 256
+    block = QUERIES
     length = k_ref.shape[0]
 
     def step(i, carry):
         start = pl.multiple_of(first + i * block, block)
         near = pl.ds(pl.multiple_of(i * block, block), block)
-        low, count = key_window(seg, start, block, length)
 
         def body(key_start, size):
             window = pl.ds(key_start, size)
             keys, values = k_ref[window, :], v_ref[window, :]
-            same = seg_col_ref[pl.ds(start, block), :] == seg_row_ref[:, window]
+            numbers = seg_row_ref[...]
+            if size < length:
+                span = size - size % 128 + 256
+                base = jnp.minimum(key_start // 128, (length - span) // 128) * 128
+                numbers = seg_row_ref[:, pl.ds(pl.multiple_of(base, 128), span)]
+                numbers = jnp.broadcast_to(numbers, (8, span))
+                numbers = pltpu.roll(numbers, span - (key_start - base), 1)[0:1, :size]
+            same = seg_col_ref[pl.ds(start, block), :] == numbers
             queries = q_ref[pl.ds(start, block), :] * jnp.asarray(HEAD_DIM**-0.5, BF)
 
             def one(head, result):
@@ -391,7 +411,7 @@
             result = each_head(per, size, one, jnp.zeros(queries.shape, F32))
             held[near, :] = result.astype(BF)
 
-        each_window(low, count, length, body)
+        each_window(ranges, first // block + i, length, body)
         return carry
 
     lax.fori_loop(0, held.shape[0] // block, step, 0)
@@ -400,8 +420,8 @@
     out_ref[top.shape[0] :, :] = rest
 
 
-def attend(scal, queries, keys, values, seg_row, seg_col, per, first, count, kept=()):
-    inputs = (scal, seg_row, queries, keys, values, seg_row, seg_col, *kept)
+def attend(scal, ranges, queries, keys, values, seg_row, seg_col, per, first, count, kept=()):
+    inputs = (scal, ranges, queries, keys, values, seg_row, seg_col, *kept)
     return run(
         functools.partial(attend_kernel, per, first),
         "attend",
@@ -619,7 +639,7 @@
     return run(resid_kernel, "resid_back", outputs, (scal, mine, got, resid, cotangent, vec), 0.8)
 
 
-def mixed_kernel(cols, scal, *refs):
+def mixed_kernel(cols, scal, *refs, ready):
     grads, (o_ref, rows_ref, do_ref, g_ref, all_ref, own_ref) = refs[0:4], refs[4:10]
     place_members(scal, grads, all_ref)
     do_ref[...] = dot_cols(all_ref[...], rows_ref[...]).astype(BF)
@@ -629,6 +649,7 @@
         def _():
             own_ref[...] = all_ref[:, index * cols : (index + 1) * cols]
 
+    ready(5)
     g_ref[...] = dot_rows(o_ref[...], own_ref[...]).astype(BF)
 
 
@@ -643,11 +664,12 @@
         2.5,
         [pltpu.VMEM((length, width), BF), pltpu.VMEM((length, cols), BF)],
         lazy=(5, 6),
+        late=(5,),
     )
 
 
 def attend_back_kernel(
-    per, scal, seg, q_ref, k_ref, v_ref, do_ref, seg_row_ref, seg_col_ref, *refs
+    per, scal, ranges, q_ref, k_ref, v_ref, do_ref, seg_row_ref, seg_col_ref, *refs, ready
 ):
     out_ref, k_acc, v_acc = refs[-3:]
     cols = q_ref.shape[1]
@@ -655,11 +677,12 @@
     length = k_ref.shape[0]
     k_acc[...] = jnp.zeros_like(k_acc)
     v_acc[...] = jnp.zeros_like(v_acc)
+    for position in (2, 3, 4, 7):
+        ready(position)
 
     def step(i, carry):
         start = pl.multiple_of(i * block, block)
         rows = pl.ds(start, block)
-        low, count = key_window(seg, start, block, length)
 
         def body(key_start, size):
             window = pl.ds(key_start, size)
@@ -695,7 +718,7 @@
             v_acc[window, :] += grad_value
             out_ref[rows, :cols] = (grad_query * HEAD_DIM**-0.5).astype(BF)
 
-        each_window(low, count, length, body)
+        each_window(ranges, i, length, body)
         return carry
 
     lax.fori_loop(0, q_ref.shape[0] // block, step, 0)
@@ -703,10 +726,10 @@
     out_ref[:, 2 * cols :] = v_acc[...].astype(BF)
 
 
-def attend_back(scal, queries, keys, values, grad_out, seg_row, seg_col, per, kept):
+def attend_back(scal, ranges, queries, keys, values, grad_out, seg_row, seg_col, per, kept):
     length, cols = queries.shape
     wide = pltpu.VMEM(queries.shape, F32)
-    inputs = (scal, seg_row, queries, keys, values, grad_out, seg_row, seg_col, *kept)
+    inputs = (scal, ranges, queries, keys, values, grad_out, seg_row, seg_col, *kept)
     return run(
         functools.partial(attend_back_kernel, per),
         "attend_back",
@@ -715,81 +738,104 @@
         16.0,
         [wide, wide],
         lazy=(2, 3, 4, 7),
+        late=(2, 3, 4, 7),
         save=range(8, len(inputs)),
         scalars=2,
     )
 
 
-def query_grads_kernel(cols, scal, *refs):
-    a_ref, hat_ref, out_ref, grad_ref, w_ref, forward_ref, resid_ref = refs[0:7]
-    g_ref, rows_ref, table_ref = refs[7:10]
-    member = scal[0]
-    length, width = a_ref.shape
-    ones = jnp.ones((length, 8), BF)
-    grad = grad_ref[...]
+def table_kernel(scal, forward_ref, resid_ref, table_ref, rows_ref):
+    rows_ref[...] = jnp.zeros_like(rows_ref)
+    rows_ref[4:5, :] = resid_ref[0:1, :]
+    rows_ref[5:7, :] = forward_ref[0:2, :]
+    rows_ref[7:8, :] = resid_ref[1:2, :]
+    rows_ref[pl.ds(8 + scal[0], 1), :] = forward_ref[2:3, :]
+    rest = rows_ref[...]
+    unit = unit_rows(16, 128)
+    table = jnp.zeros(table_ref.shape, F32)
+    for _ in range(3):
+        high = rest.astype(BF)
+        rest = rest - high.astype(F32)
+        table += dot_rows(high, unit)
+    table_ref[...] = table
+
+
+def vector_table(scal, sums_forward, sums_resid):
+    width = sums_resid.shape[1]
+    return run(
+        table_kernel,
+        "vector_table",
+        shaped((width, 128), F32),
+        (scal, sums_forward, sums_resid),
+        1.0,
+        [pltpu.VMEM((16, width), F32)],
+        mebibytes=8,
+        lazy=(1,),
+    )
+
+
+def query_grads_kernel(cols, scal, *refs, ready):
+    a_ref, hat_ref, out_ref, grad_ref, w_ref, table_ref, g_ref = refs
+    width = a_ref.shape[1]
+    block = 256
+    ready(1)
+
+    def weights(i, carry):
+        lanes = pl.ds(pl.multiple_of(i * block, block), block)
+        g_ref[lanes, : 3 * cols] = dot_rows(a_ref[:, lanes], grad_ref[...]).astype(BF)
+        return carry
+
+    lax.fori_loop(0, width // block, weights, 0)
     row = lax.broadcasted_iota(jnp.int32, (8, 3 * cols), 0)
-    rest = dot_rows(ones, grad)
+    rest = dot_rows(jnp.ones((a_ref.shape[0], 8), BF), grad_ref[...])
     terms = jnp.zeros((8, 3 * cols), F32)
     for term in range(3):
         high = rest.astype(BF).astype(F32)
         terms = jnp.where(row == term, high, terms)
         rest = rest - high
     terms = terms.astype(BF)
-
-    rows_ref[...] = jnp.zeros_like(rows_ref)
-    rows_ref[4:5, :] = resid_ref[0:1, :]
-    rows_ref[5:7, :] = forward_ref[0:2, :]
-    rows_ref[7:8, :] = resid_ref[1:2, :]
-    rows_ref[pl.ds(8 + member, 1), :] = forward_ref[2:3, :]
-    rest = rows_ref[...]
-    unit = unit_rows(16, 128)
-    table = jnp.zeros((width, 128), F32)
-    for _ in range(3):
-        high = rest.astype(BF)
-        rest = rest - high.astype(F32)
-        table += dot_rows(high, unit)
-    table_ref[...] = table
-
-    block = 256
+    for position in (2, 3, 5, 6):
+        ready(position)
     lane = lax.broadcasted_iota(jnp.int32, (block, 128), 1)
 
-    def step(i, carry):
+    def vectors(i, carry):
         lanes = pl.ds(pl.multiple_of(i * block, block), block)
         weight = w_ref[lanes, :]
-        g_ref[lanes, : 3 * cols] = dot_rows(a_ref[:, lanes], grad).astype(BF)
-        product = dot_rows(hat_ref[:, lanes], grad) * weight.astype(F32)
+        product = dot_rows(hat_ref[:, lanes], grad_ref[...]) * weight.astype(F32)
         gain = jnp.sum(product, axis=1, keepdims=True)
         shift = jnp.sum(dot_cols(weight, terms), axis=1, keepdims=True)
         table = jnp.where(lane == 0, gain, table_ref[lanes, :])
         table_ref[lanes, :] = jnp.where(lane == 1, shift, table)
         return carry
 
-    lax.fori_loop(0, width // block, step, 0)
+    lax.fori_loop(0, width // block, vectors, 0)
     g_ref[:, 3 * cols : 4 * cols] = out_ref[...]
-    own = pl.ds(pl.multiple_of(member * cols, cols), cols)
+    own = pl.ds(pl.multiple_of(scal[0] * cols, cols), cols)
     bias = table_ref[own, :]
     near = lax.broadcasted_iota(jnp.int32, (cols, 128), 1)
+    ones = jnp.ones((8, 8), BF)
     for i, column in ((0, 2), (2, 3)):
-        part = grad_ref[:, i * cols : (i + 1) * cols]
-        bias = jnp.where(near == column, dot_rows(part, ones)[:, 0:1], bias)
+        part = dot_rows(terms[:, i * cols : (i + 1) * cols], ones)
+        bias = jnp.where(near == column, part[:, 0:1], bias)
     table_ref[own, :] = bias
-    total = table_ref[:, 0:16]
+    total = table_ref[...]
     high = total.astype(BF)
-    g_ref[:, 4 * cols : 4 * cols + 16] = high
-    g_ref[:, 4 * cols + 16 : 4 * cols + 32] = (total - high.astype(F32)).astype(BF)
+    low = (total - high.astype(F32)).astype(BF)
+    g_ref[:, 4 * cols : 4 * cols + 16] = high[:, 0:16]
+    g_ref[:, 4 * cols + 16 : 4 * cols + 32] = low[:, 0:16]
     g_ref[:, 4 * cols + 32 :] = jnp.zeros((width, 96), BF)
 
 
-def query_grads(scal, normed, hat, grad_out, grad, weights, sums_forward, sums_resid):
+def query_grads(scal, normed, hat, grad_out, grad, weights, table):
     width, cols = grad_out.shape
     return run(
         functools.partial(query_grads_kernel, cols),
         "query_grads",
         shaped((width, 4 * cols + 128), BF),
-        (scal, normed, hat, grad_out, grad, weights, sums_forward, sums_resid),
+        (scal, normed, hat, grad_out, grad, weights, table),
         4.0,
-        [pltpu.VMEM((16, width), F32), pltpu.VMEM((width, 128), F32)],
-        lazy=(1, 2, 3, 5, 6, 7),
+        lazy=(1, 2, 3, 5, 6),
+        late=(1, 2, 3, 5, 6),
         far=(0,),
     )
 
@@ -870,8 +916,10 @@
         total += in_ref[i].astype(F32)
     low_ref[:, : 4 * cols] = total[:, : 4 * cols].astype(BF)
     vector = total[:, 4 * cols :]
-    low_ref[:, 4 * cols : 4 * cols + 128] = vector.astype(BF)
-    low_ref[:, 4 * cols + 128 :] = (vector - vector.astype(BF).astype(F32)).astype(BF)
+    high = vector.astype(BF).astype(F32)
+    lane = lax.broadcasted_iota(jnp.int32, vector.shape, 1)
+    rest = pltpu.roll(vector - high, 32, 1)
+    low_ref[:, 4 * cols :] = jnp.where(lane < 32, high, rest).astype(BF)
 
 
 def owned_vector(scal, pieces, cols):
@@ -879,7 +927,7 @@
     return run(
         functools.partial(owned_vector_kernel, cols),
         "owned_vector",
-        shaped((rows, width + 128), BF),
+        shaped((rows, width), BF),
         (scal, pieces),
         1.5,
     )
@@ -901,14 +949,13 @@
                     ].astype(F32)
 
     def vector_of(piece):
-        high = piece[:, 4 * cols : 4 * cols + 128].astype(F32)
-        return high + piece[:, 4 * cols + 128 :].astype(F32)
+        return piece[:, 4 * cols :].astype(F32)
 
     halves = [vector_of(piece) for piece in pieces]
     table = (halves[0] + halves[1]) + (halves[2] + halves[3])
     rows = lax.broadcasted_iota(jnp.int32, (16, 128), 0)
     lanes = lax.broadcasted_iota(jnp.int32, (16, 128), 1)
-    unit = jnp.where((lanes == rows) | (lanes == rows + 16), 1.0, 0.0)
+    unit = jnp.where((lanes % 16 == rows) & (lanes < 64), 1.0, 0.0)
     vector = lax.dot_general(
         unit,
         table,
@@ -1097,8 +1144,7 @@
         owners = [device]
         for hop in range(1, count // 2 + 1):
             owners.append(RING[(place - hop) % count])
-            if hop < count // 2:
-                owners.append(RING[(place + hop) % count])
+            owners.append(RING[(place + hop) % count])
         table.append(owners)
     return np.asarray(table, np.int32)
 
@@ -1108,27 +1154,34 @@
 
 
 class Ring:
-    def __init__(self, block, count):
+    def __init__(self, block, count, halved=False):
         self.count = count
-        self.hops = count // 2 if count == len(RING) else 1
+        self.halved = halved
+        self.ringed = count == len(RING)
+        self.hops = count // 2 if self.ringed else 1
         self.front = self.rear = block
         self.pieces = [block]
         self.done = 0
 
+    def send(self, array, distance):
+        count = self.count
+        pairs = [(RING[i], RING[(i + distance) % count]) for i in range(count)]
+        return lax.ppermute(array, "dp", pairs)
+
     def hop(self, *others):
         self.done += 1
-        if self.count != len(RING):
+        if not self.ringed:
             self.pieces = [lax.all_gather(after(self.front, *others), "dp", axis=0, tiled=True)]
             return self
-        ahead = [(RING[i], RING[(i + 1) % self.count]) for i in range(self.count)]
-        back = [(target, source) for source, target in ahead]
-        last = self.done == self.hops
         if self.done > 1 or others:
             self.front, self.rear = lax.optimization_barrier((self.front, self.rear, *others))[:2]
-        self.front = lax.ppermute(self.front, "dp", ahead)
+        if self.done == self.hops and self.halved:
+            half = self.front.shape[0] // 2
+            self.front, self.rear = self.front[:half], self.rear[half:]
+        self.front = self.send(self.front, 1)
         self.pieces.append(self.front)
-        if not last:
-            self.rear = lax.ppermute(self.rear, "dp", back)
+        if self.done < self.hops or self.halved:
+            self.rear = self.send(self.rear, -1)
             self.pieces.append(self.rear)
         return self
 
@@ -1188,13 +1241,14 @@
     second = Ring(pack_forward(scal, feedforward_master, part), owners)
     second.hop(first.pieces[-1])
 
-    queries, keys, values, w_qkv, w_o, vec, seg_col, normed, hat = project(
+    queries, keys, values, w_qkv, w_o, vec, seg_col, normed, hat, ranges = project(
         scal, segments, x_all, first.pieces, cols
     )
     half = x_all.shape[0] // 2
     w_across = swap(w_o, 2)
     mixed_low, *kept = attend(
         scal,
+        ranges,
         after(queries, grad_across),
         keys,
         values,
@@ -1211,7 +1265,7 @@
     if ringed:
         second.hop(mixed_low)
     mixed_high = attend(
-        scal, after(queries, w_across), keys, values, segments, seg_col, per, half, half
+        scal, ranges, after(queries, w_across), keys, values, segments, seg_col, per, half, half
     )
     high_across = swap(after(mixed_high, low_across), 2)
     if ringed:
@@ -1259,14 +1313,17 @@
     grad_resid, grad_low, sums_resid = resid_back(
         scal, after(mine, send_branch), got, resid, cot_own, vec
     )
-    low_blocks = spread(grad_low)
+    low_across = swap(grad_low, 2)
     mine, send = merge(
         scal, keep_branch, swap(after(send_branch, grad_low), 1), lazy=(1,)
     )
-    low_blocks[0] = after(low_blocks[0], send)
+    table = vector_table(scal, far_sums, sums_resid)
+    low_across = after(low_across, send, table)
+    low_blocks = [grad_low, swap(grad_low, 1), low_across, swap(low_across, 1)]
     grad_mixed, grad_out = mixed_back(scal, low_blocks, far_mixed, far_rows)
-    grad_qkv, far_dh, far_sums_resid, far_grad_out = attend_back(
+    grad_qkv, far_dh, far_table, far_grad_out = attend_back(
         scal,
+        ranges,
         far_q,
         far_k,
         far_v,
@@ -1274,9 +1331,9 @@
         segments,
         far_col,
         per,
-        (grad_resid, sums_resid, grad_out),
-    )
-    got_branch = swap(send, 2)
+        (grad_resid, table, grad_out),
+    )
+    got_branch = swap(after(send, grad_mixed), 2)
     pack = query_grads(
         scal,
         after(far_normed[0], got_branch),
@@ -1284,8 +1341,7 @@
         far_grad_out,
         grad_qkv,
         far_weights,
-        far_sums,
-        far_sums_resid,
+        far_table,
     )
     owned_pack = exchange_owned(pack, owners)
     forward_parts = spread(owned_sum(scal, after(owned_ff, pack)))

time: 221 us -> 219 us (level)
  waiting for transfers between devices: 76 us -> 69.6 us
  starting transfers between devices: 44.2 us -> 47.1 us
    ppermute x30, waiting for transfers between devices: 38.8 us -> 33.3 us  [swap(): return lax.ppermute(part, 'head', [(i, i ^ bit) for i in range(4)])]
    ppermute x30, starting transfers between devices: 13.7 us -> 16.9 us  [swap(): return lax.ppermute(part, 'head', [(i, i ^ bit) for i in range(4)])]
    pallas_call x22 -> x23, Pallas kernels: 81.1 us -> 82.2 us  [run(): pl.pallas_call(body, out_shape=shapes + [pltpu.HBM(inputs[i].shape, input...]
  transfers between devices with their start and end apart: 47 -> 47, of which waited for: 25 -> 26; matrix products, arithmetic and copies ran while one was open for 0% -> 0% of each run, Pallas kernels for 31% -> 32%
where the time goes in v1:
time: 219 us; the launch traced here: 218 us
  Pallas kernels  96.6 us (44%)
  waiting for transfers between devices  69.6 us (32%)
  starting transfers between devices  47.1 us (22%)
  local copies, waits for them, and re-layouts  3.94 us (2%)
    pallas_call x23, Pallas kernels, run(): pl.pallas_call(body, out_shape=shapes + [pltpu.HBM(inputs[i].shape, input...  82.2 us
    ppermute x30, waiting for transfers between devices, swap(): return lax.ppermute(part, 'head', [(i, i ^ bit) for i in range(4)])  33.3 us
    ppermute x14, waiting for transfers between devices, send(): return lax.ppermute(array, 'dp', pairs)  23.4 us
    ppermute x30, starting transfers between devices, swap(): return lax.ppermute(part, 'head', [(i, i ^ bit) for i in range(4)])  16.9 us
    ppermute x14, starting transfers between devices, send(): return lax.ppermute(array, 'dp', pairs)  16.4 us
    pallas_call x1, Pallas kernels, adam(): pl.pallas_call(functools.partial(adam_kernel, counts), out_shape=out_shap...  12.8 us
    all_to_all x2, waiting for transfers between devices, exchange_owned(): return lax.all_to_all(blocks, 'dp', split_axis=0, concat_axis=0)  9.55 us
    all_to_all x2, starting transfers between devices, exchange_owned(): return lax.all_to_all(blocks, 'dp', split_axis=0, concat_axis=0)  9.32 us
  transfers between devices with their start and end apart: 47, of which 26 were waited for; matrix products, arithmetic and copies ran while one was open for 0% of the time, Pallas kernels for 32%

profile of v1, /device:TPU:0, one launch (start us, length us, event | category | flops | bytes accessed | tf_op | source)
XLA Modules:
  0.0 218.3 jit_solution(13724781399624001200)
XLA Ops:
  1.4 1.3 copy-done
  3.3 0.9 pack_attention.1.refs_3_
  4.2 3.0 %collective-permute-start.2 = (bf16[96,896]{1,0:T(8,128)(2,1)S(1)}, bf16[96,896]{1,0:T(8,128)(2,1)S(1)}, u32[]{:S(2)}, u32[]{:S(2)}) collective-permute-start(bf16[96,896]{1,0:T(8,128)(2,1)S(1)} %pack_attention.1.refs_3_), channel_id=1, source_target_pairs={{0,4},{8,0},{16,8},{24,16},{28,24},{20,28},{12,20},{4,12},{1,5},{9... | collective-permute-start | bytes 516104 | tf_op jit(solution)/shard_map/ppermute | solution.py:1169
  7.4 4.3 %collective-permute-done.2.refs_5_ = bf16[96,896]{1,0:T(8,128)(2,1)S(1)} collective-permute-done((bf16[96,896]{1,0:T(8,128)(2,1)S(1)}, bf16[96,896]{1,0:T(8,128)(2,1)S(1)}, u32[]{:S(2)}, u32[]{:S(2)}) %collective-permute-start.2) | collective-permute-done | bytes 172064 | tf_op jit(solution)/shard_map/ppermute | solution.py:1169
  11.7 1.4 collective-permute-done.1.refs_4_
  13.5 1.6 collective-permute-start.4
  15.1 1.5 collective-permute-start
  16.6 1.9 collective-permute-done.3.refs_6_
  18.9 1.7 collective-permute-start.5
  20.9 3.4 %collective-permute-done.5.refs_8_ = bf16[96,896]{1,0:T(8,128)(2,1)S(1)} collective-permute-done((bf16[96,896]{1,0:T(8,128)(2,1)S(1)}, bf16[96,896]{1,0:T(8,128)(2,1)S(1)}, u32[]{:S(2)}, u32[]{:S(2)}) %collective-permute-start.5) | collective-permute-done | bytes 172064 | tf_op jit(solution)/shard_map/ppermute | solution.py:1169
  24.3 1.7 collective-permute-done.6.refs_9_
  26.0 1.6 collective-permute-start.9
  28.1 1.5 collective-permute-start.11
  30.3 1.1 collective-permute-done.9.refs_10_
  31.4 1.6 collective-permute-start.22
  34.1 4.6 %project.1 = (bf16[1024,192]{1,0:T(8,128)(2,1)S(1)}, bf16[1024,192]{1,0:T(8,128)(2,1)S(1)}, bf16[1024,192]{1,0:T(8,128)(2,1)S(1)}, bf16[768,576]{1,0:T(8,128)(2,...) custom-call(s32[10]{0:T(128)S(1)} %dynamic-slice_bitcast_fusion.scal, ...), custom_call_target="tpu_custom_call" | custom-call | bytes 16200000 | tf_op jit(solution)/shard_map/project/pallas_call | solution.py:164
  39.1 1.5 collective-permute-start.10
  40.6 3.3 %attend.2 = (bf16[768,128]{1,0:T(8,128)(2,1)S(1)}, bf16[1024,192]{1,0:T(8,128)(2,1)}, bf16[1024,192]{1,0:T(8,128)(2,1)}, bf16[1024,192]{1,0:T(8,128)(2,1)}, s32[...) custom-call(s32[10]{0:T(128)S(1)} %dynamic-slice_bitcast_fusion.scal, ...), custom_call_target="tpu_custom_call" | custom-call | bytes 12600000 | tf_op jit(solution)/shard_map/attend/pallas_call | solution.py:164
  43.9 1.6 collective-permute-start.24
  46.5 0.8 collective-permute-done.10.refs_13_
  47.4 3.2 %attend.3.refs_4_ = bf16[768,128]{1,0:T(8,128)(2,1)S(1)} custom-call(s32[10]{0:T(128)S(1)} %dynamic-slice_bitcast_fusion.scal.refs_0_, s32[16]{0:T(128)S(1)} %get-tuple-element.142.refs_1_, bf16[1024,192]{1,0:T(8,128)(2,1)S(1)} %get-tuple-element.154.refs_2_, bf16[1024,192]{1,0:T(8,128)(2,1)S(1)} %get-tuple-element.145.refs_3_, ...), custom_call_target="tpu_custom_call" | custom-call | bytes 12600000 | tf_op jit(solution)/shard_map/attend/pallas_call | solution.py:164
  50.5 1.2 collective-permute-done.12.refs_7_
  51.7 1.4 collective-permute-start.13
  53.1 1.5 collective-permute-start.26
  55.1 2.2 %collective-permute-done.13.refs_8_ = bf16[768,128]{1,0:T(8,128)(2,1)S(1)} collective-permute-done((bf16[768,128]{1,0:T(8,128)(2,1)S(1)}, bf16[768,128]{1,0:T(8,128)(2,1)S(1)}, u32[]{:S(2)}, u32[]{:S(2)}) %collective-permute-start.13) | collective-permute-done | bytes 196640 | tf_op jit(solution)/shard_map/ppermute | solution.py:1120
  57.9 2.3 %collective-permute-done.26.refs_20_ = bf16[96,1536]{1,0:T(8,128)(2,1)S(1)} collective-permute-done((bf16[96,1536]{1,0:T(8,128)(2,1)S(1)}, bf16[96,1536]{1,0:T(8,128)(2,1)S(1)}, u32[]{:S(2)}, u32[]{:S(2)}) %collective-permute-start.26) | collective-permute-done | bytes 294944 | tf_op jit(solution)/shard_map/ppermute | solution.py:1169
  60.2 1.3 collective-permute-done.27.refs_21_
  62.0 1.5 collective-permute-start.28
  65.2 5.7 %collective-permute-done.28.refs_22_ = bf16[96,1536]{1,0:T(8,128)(2,1)S(1)} collective-permute-done((bf16[96,1536]{1,0:T(8,128)(2,1)S(1)}, bf16[96,1536]{1,0:T(8,128)(2,1)S(1)}, u32[]{:S(2)}, u32[]{:S(2)}) %collective-permute-start.28) | collective-permute-done | bytes 294944 | tf_op jit(solution)/shard_map/ppermute | solution.py:1169
  70.9 11.2 %forward_back.1 = (bf16[1024,768]{1,0:T(8,128)(2,1)S(1)}, bf16[1024,768]{1,0:T(8,128)(2,1)S(1)}, bf16[1024,768]{1,0:T(8,128)(2,1)S(1)}, f32[512,768]{1,0:T(8,128...) custom-call(s32[10]{0:T(128)S(1)} %dynamic-slice_bitcast_fusion.scal, ...), custom_call_target="tpu_custom_call" | custom-call | bytes 46800000 | tf_op jit(solution)/shard_map/forward_back/pallas_call | solution.py:164
  82.2 5.1 %forward_grads.1 = (bf16[768,1536]{1,0:T(8,128)(2,1)}, bf16[1024,768]{1,0:T(8,128)(2,1)}, f32[256,768]{1,0:T(8,128)}, f32[8,768]{1,0:T(8,128)}, bf16[192,768]{1,...) custom-call(s32[10]{0:T(128)S(1)} %dynamic-slice_bitcast_fusion.scal.refs_0_, ...), custom_call_target="tpu_custom_call" | custom-call | bytes 14400000 | tf_op jit(solution)/shard_map/forward_grads/pallas_call | solution.py:164
  87.4 4.7 %all-to-all-start.1 = ((bf16[8,96,1536]{2,1,0:T(8,128)(2,1)}), bf16[8,96,1536]{2,1,0:T(8,128)(2,1)}, u32[]{:S(2)}, u32[]{:S(2)}) async-start(bf16[8,96,1536]{2,1,0:T(8,128)(2,1)} %bitcast.2), calls=%async_computation.1 | async-start | bytes 4718592 | tf_op jit(solution)/shard_map/all_to_all | solution.py:1196
  92.8 1.7 collective-permute-start.30
  94.5 6.1 %branch_part.1 = (f32[512,768]{1,0:T(8,128)}, bf16[512,768]{1,0:T(8,128)(2,1)S(1)}, bf16[256,768]{1,0:T(8,128)(2,1)S(1)}) custom-call(s32[10]{0:T(128)S(1)} %dynamic-slice_bitcast_fusion.scal.refs_0_, bf16[1024,768]{1,0:T(8,128)(2,1)} %get-tuple-element.177.refs_1_, bf16[768,1536]{1,0:T(8,128)(2,1)} %get-tuple-element.184.refs_2_, bf16[256,768]{1,0:T(8,128)(2,1)} %refs_3_.4), custom_call_target="tpu_custom_call" | custom-call | bytes 10800000 | tf_op jit(solution)/shard_map/branch_part/pallas_call | solution.py:164
  100.6 3.5 %collective-permute-done.30.refs_2_ = bf16[256,768]{1,0:T(8,128)(2,1)S(1)} collective-permute-done((bf16[256,768]{1,0:T(8,128)(2,1)S(1)}, bf16[256,768]{1,0:T(8,128)(2,1)S(1)}, u32[]{:S(2)}, u32[]{:S(2)}) %collective-permute-start.30) | collective-permute-done | bytes 393248 | tf_op jit(solution)/shard_map/ppermute | solution.py:1120
  104.1 1.2 resid_back.1
  105.4 1.7 collective-permute-start.33
  107.2 1.7 vector_table.1.refs_9_
  108.9 2.1 merge.4
  111.0 5.9 %collective-permute-done.33.refs_3_ = bf16[256,768]{1,0:T(8,128)(2,1)S(1)} collective-permute-done((bf16[256,768]{1,0:T(8,128)(2,1)S(1)}, bf16[256,768]{1,0:T(8,128)(2,1)S(1)}, u32[]{:S(2)}, u32[]{:S(2)}) %collective-permute-start.33) | collective-permute-done | bytes 393248 | tf_op jit(solution)/shard_map/ppermute | solution.py:1120
  116.9 1.7 collective-permute-done.34.refs_4_
  118.6 4.3 %mixed_back.1 = (bf16[1024,192]{1,0:T(8,128)(2,1)S(1)}, bf16[768,192]{1,0:T(8,128)(2,1)S(1)}) custom-call(s32[10]{0:T(128)S(1)} %dynamic-slice_bitcast_fusion.scal.refs_0_, bf16[256,768]{1,0:T(8,128)(2,1)S(1)} %get-tuple-element.190.refs_1_, bf16[256,768]{1,0:T(8,128)(2,1)S(1)} %collective-permute-done.32.refs_2_, ...), custom_call_target="tpu_custom_call" | custom-call | bytes 9000000 | tf_op jit(solution)/shard_map/mixed_back/pallas_call | solution.py:164
  122.9 1.7 collective-permute-start.35
  124.6 12.1 %attend_back.1 = (bf16[1024,576]{1,0:T(8,128)(2,1)S(1)}, f32[256,768]{1,0:T(8,128)}, f32[768,128]{1,0:T(8,128)}, bf16[768,192]{1,0:T(8,128)(2,1)}) custom-call(s32[10]{0:T(128)S(1)} %dynamic-slice_bitcast_fusion.scal.refs_0_, s32[16]{0:T(128)S(1)} %get-tuple-element.142.refs_1_, bf16[1024,192]{1,0:T(8,128)(2,1)} %get-tuple-element.204.refs_2_, ...), custom_call_target="tpu_custom_call" | custom-call | bytes 57600000 | tf_op jit(solution)/shard_map/attend_back/pallas_call | solution.py:164
  136.7 0.7 copy-done.6
  137.4 8.1 %query_grads.1 = bf16[768,896]{1,0:T(8,128)(2,1)} custom-call(s32[10]{0:T(128)S(1)} %dynamic-slice_bitcast_fusion.scal.refs_0_, bf16[1024,768]{1,0:T(8,128)(2,1)} %get-tuple-element.202.refs_1_, bf16[1024,768]{1,0:T(8,128)(2,1)} %get-tuple-element.203.refs_2_, bf16[768,192]{1,0:T(8,128)(2,1)} %get-tuple-element.210.refs_3_, ...), custom_call_target="tpu_custom_call" | custom-call | bytes 14400000 | tf_op jit(solution)/shard_map/query_grads/pallas_call | solution.py:164
  145.6 1.1 all-to-all-done.1.refs_1_
  146.7 4.6 %all-to-all-start = ((bf16[8,96,896]{2,1,0:T(8,128)(2,1)}), bf16[8,96,896]{2,1,0:T(8,128)(2,1)S(1)}, u32[]{:S(2)}, u32[]{:S(2)}) async-start(bf16[8,96,896]{2,1,0:T(8,128)(2,1)} %bitcast.6), calls=%async_computation | async-start | bytes 2752512 | tf_op jit(solution)/shard_map/all_to_all | solution.py:1196
  151.3 3.9 %project_back.1 = (f32[512,768]{1,0:T(8,128)S(1)}, bf16[512,768]{1,0:T(8,128)(2,1)S(1)}) custom-call(s32[10]{0:T(128)S(1)} %dynamic-slice_bitcast_fusion.scal.refs_0_, bf16[1024,576]{1,0:T(8,128)(2,1)S(1)} %get-tuple-element.211.refs_4_.refs_1_, bf16[768,576]{1,0:T(8,128)(2,1)} %get-tuple-element.217.refs_5_.refs_2_), custom_call_target="tpu_custom_call" | custom-call | bytes 10800000 | tf_op jit(solution)/shard_map/project_back/pallas_call | solution.py:164
  155.3 2.5 %owned_sum.1.refs_1_ = bf16[96,1536]{1,0:T(8,128)(2,1)S(1)} custom-call(s32[10]{0:T(128)S(1)} %dynamic-slice_bitcast_fusion.scal.refs_0_, bf16[8,96,1536]{2,1,0:T(8,128)(2,1)} %all-to-all-done.1.refs_1_), custom_call_target="tpu_custom_call" | custom-call | bytes 5400000 | tf_op jit(solution)/shard_map/owned_sum/pallas_call | solution.py:164
  159.2 1.4 collective-permute-start.37
  160.7 7.0 %collective-permute-done.39.refs_3_ = bf16[96,1536]{1,0:T(8,128)(2,1)S(1)} collective-permute-done((bf16[96,1536]{1,0:T(8,128)(2,1)S(1)}, bf16[96,1536]{1,0:T(8,128)(2,1)S(1)}, u32[]{:S(2)}, u32[]{:S(2)}) %collective-permute-start.39) | collective-permute-done | bytes 294944 | tf_op jit(solution)/shard_map/ppermute | solution.py:1120
  167.7 2.7 %output_sum.1 = bf16[256,768]{1,0:T(8,128)(2,1)} custom-call(s32[10]{0:T(128)S(1)} %dynamic-slice_bitcast_fusion.scal.refs_0_, f32[256,768]{1,0:T(8,128)S(1)} %get-tuple-element.214.refs_1_, bf16[256,768]{1,0:T(8,128)(2,1)} %copy-done.6, f32[256,768]{1,0:T(8,128)} %get-tuple-element.215.refs_3_, f32[16,768]{1,0:T(8,128)} %get-tuple-element.216.refs_4_.refs_5_), custom_call_target="tpu_custom_call" | custom-call | bytes 2880000 | tf_op jit(solution)/shard_map/output_sum/pallas_call | solution.py:164
  170.4 1.6 squares_of.1
  172.0 3.8 %collective-permute-done.37.refs_2_ = bf16[256,768]{1,0:T(8,128)(2,1)} collective-permute-done((bf16[256,768]{1,0:T(8,128)(2,1)S(1)}, bf16[256,768]{1,0:T(8,128)(2,1)}, u32[]{:S(2)}, u32[]{:S(2)}) %collective-permute-start.37) | collective-permute-done | bytes 393248 | tf_op jit(solution)/shard_map/ppermute | solution.py:1120
  175.9 8.4 %all-to-all-done.refs_1_ = bf16[8,96,896]{2,1,0:T(8,128)(2,1)S(1)} async-done(((bf16[8,96,896]{2,1,0:T(8,128)(2,1)}), bf16[8,96,896]{2,1,0:T(8,128)(2,1)S(1)}, u32[]{:S(2)}, u32[]{:S(2)}) %all-to-all-start) | async-done | bytes 1376288 | tf_op jit(solution)/shard_map/all_to_all | solution.py:1196
  184.3 0.8 owned_vector.1.refs_1_
  185.8 4.7 %collective-permute-done.42.refs_3_ = bf16[96,896]{1,0:T(8,128)(2,1)S(1)} collective-permute-done((bf16[96,896]{1,0:T(8,128)(2,1)S(1)}, bf16[96,896]{1,0:T(8,128)(2,1)S(1)}, u32[]{:S(2)}, u32[]{:S(2)}) %collective-permute-start.42) | collective-permute-done | bytes 172064 | tf_op jit(solution)/shard_map/ppermute | solution.py:1120
  190.5 1.4 collective-permute-done.43.refs_4_
  191.9 1.8 join.1
  193.8 4.5 %all-to-all-start.2 = ((f32[8,8,128]{2,1,0:T(8,128)}), f32[8,8,128]{2,1,0:T(8,128)S(1)}, u32[]{:S(2)}, u32[]{:S(2)}) async-start(f32[8,8,128]{2,1,0:T(8,128)} %bitcast.3), calls=%async_computation.2 | async-start | bytes 65536 | tf_op jit(solution)/shard_map/all_to_all | solution.py:1359
  198.3 3.3 %input_back.1 = f32[256,768]{1,0:T(8,128)} custom-call(s32[10]{0:T(128)S(1)} %dynamic-slice_bitcast_fusion.scal.refs_0_, f32[256,768]{1,0:T(8,128)S(1)} %get-tuple-element.220.refs_1_, bf16[256,768]{1,0:T(8,128)(2,1)} %collective-permute-done.37.refs_2_, bf16[256,768]{1,0:T(8,128)(2,1)} %refs_3_.5, f32[256,768]{1,0:T(8,128)} %get-tuple-element.222.refs_4_, ...), custom_call_target="tpu_custom_call" | custom-call | bytes 3600000 | tf_op jit(solution)/shard_map/input_back/pallas_call | solution.py:164
  201.6 3.3 %all-to-all-done.2.total_ref = f32[8,8,128]{2,1,0:T(8,128)S(1)} async-done(((f32[8,8,128]{2,1,0:T(8,128)}), f32[8,8,128]{2,1,0:T(8,128)S(1)}, u32[]{:S(2)}, u32[]{:S(2)}) %all-to-all-start.2) | async-done | bytes 32800 | tf_op jit(solution)/shard_map/all_to_all | solution.py:1359
  205.0 12.8 %adam.1 = (f32[96,3072]{1,0:T(8,128)}, f32[96,6144]{1,0:T(8,128)}, f32[12,96]{1,0:T(8,128)}, f32[96,3072]{1,0:T(8,128)}, f32[96,6144]{1,0:T(8,128)}, /*index=5*/...) custom-call(s32[10]{0:T(128)S(1)} %dynamic-slice_bitcast_fusion.scal, ...), custom_call_target="tpu_custom_call" | custom-call | bytes 32400000 | tf_op jit(solution)/shard_map/adam/pallas_call | solution.py:1088
  (72 shorter events, 13.5 us)
Async XLA Ops:
  1.4 1.3 copy-start
  2.6 0.7 copy-start.5
  3.3 11.7 %copy-start.3 = (bf16[256,768]{1,0:T(8,128)(2,1)S(1)}, bf16[256,768]{1,0:T(8,128)(2,1)}, u32[]{:S(2)}) copy-start(bf16[256,768]{1,0:T(8,128)(2,1)} %refs_3_.5) | copy-start | bytes 1179652
  3.3 24.7 %copy-start.2 = (bf16[256,768]{1,0:T(8,128)(2,1)S(1)}, bf16[256,768]{1,0:T(8,128)(2,1)}, u32[]{:S(2)}) copy-start(bf16[256,768]{1,0:T(8,128)(2,1)} %refs_3_.4) | copy-start | bytes 1179652
  3.3 26.2 %copy-start.1 = (f32[96,6144]{1,0:T(8,128)S(1)}, f32[96,6144]{1,0:T(8,128)}, u32[]{:S(2)}) copy-start(f32[96,6144]{1,0:T(8,128)} %refs_8_.1) | copy-start | bytes 7077892
  4.2 7.5 %collective-permute-start.2 = (bf16[96,896]{1,0:T(8,128)(2,1)S(1)}, bf16[96,896]{1,0:T(8,128)(2,1)S(1)}, u32[]{:S(2)}, u32[]{:S(2)}) collective-permute-start(bf16[96,896]{1,0:T(8,128)(2,1)S(1)} %pack_attention.1.refs_3_), channel_id=1, source_target_pairs={{0,4},{8,0},{16,8},{24,16},{28,24},{20,28},{12,20},{4,12},{1,5},{9... | collective-permute-start | bytes 516104 | tf_op jit(solution)/shard_map/ppermute | solution.py:1169
  7.2 5.8 %collective-permute-start.1 = (bf16[96,896]{1,0:T(8,128)(2,1)S(1)}, bf16[96,896]{1,0:T(8,128)(2,1)S(1)}, u32[]{:S(2)}, u32[]{:S(2)}) collective-permute-start(bf16[96,896]{1,0:T(8,128)(2,1)S(1)} %pack_attention.1.refs_3_), channel_id=1, source_target_pairs={{0,8},{8,16},{16,24},{24,28},{28,20},{20,12},{12,4},{4,0},{1,9},{9... | collective-permute-start | bytes 516104 | tf_op jit(solution)/shard_map/ppermute | solution.py:1169
  13.0 5.4 %collective-permute-start.3 = (bf16[96,896]{1,0:T(8,128)(2,1)S(1)}, bf16[96,896]{1,0:T(8,128)(2,1)S(1)}, u32[]{:S(2)}, u32[]{:S(2)}) collective-permute-start(bf16[96,896]{1,0:T(8,128)(2,1)S(1)} %collective-permute-done.1.refs_4_), channel_id=1, source_target_pairs={{0,8},{8,16},{16,24},{24,28},{28,20},{20,12},{12,4},{4,0},{1,9},{9... | collective-permute-start | bytes 516104 | tf_op jit(solution)/shard_map/ppermute | solution.py:1169
  13.5 5.4 %collective-permute-start.4 = (bf16[96,896]{1,0:T(8,128)(2,1)S(1)}, bf16[96,896]{1,0:T(8,128)(2,1)S(1)}, u32[]{:S(2)}, u32[]{:S(2)}) collective-permute-start(bf16[96,896]{1,0:T(8,128)(2,1)S(1)} %collective-permute-done.2.refs_5_), channel_id=1, source_target_pairs={{0,4},{8,0},{16,8},{24,16},{28,24},{20,28},{12,20},{4,12},{1,5},{9... | collective-permute-start | bytes 516104 | tf_op jit(solution)/shard_map/ppermute | solution.py:1169
  15.1 12.5 %collective-permute-start = (bf16[256,768]{1,0:T(8,128)(2,1)S(1)}, bf16[256,768]{1,0:T(8,128)(2,1)S(1)}, u32[]{:S(2)}, u32[]{:S(2)}) collective-permute-start(bf16[256,768]{1,0:T(8,128)(2,1)S(1)} %copy-done.3), channel_id=1, source_target_pairs={{0,2},{1,3},{2,0},{3,1},{4,6},{5,7},{6,4},{7,5},{8,10},{9,11},{10,... | collective-permute-start | bytes 1179656 | tf_op jit(solution)/shard_map/ppermute | solution.py:1120
  18.9 5.4 %collective-permute-start.5 = (bf16[96,896]{1,0:T(8,128)(2,1)S(1)}, bf16[96,896]{1,0:T(8,128)(2,1)S(1)}, u32[]{:S(2)}, u32[]{:S(2)}) collective-permute-start(bf16[96,896]{1,0:T(8,128)(2,1)S(1)} %collective-permute-done.3.refs_6_), channel_id=1, source_target_pairs={{0,8},{8,16},{16,24},{24,28},{28,20},{20,12},{12,4},{4,0},{1,9},{9... | collective-permute-start | bytes 516104 | tf_op jit(solution)/shard_map/ppermute | solution.py:1169
  20.6 5.4 %collective-permute-start.6 = (bf16[96,896]{1,0:T(8,128)(2,1)S(1)}, bf16[96,896]{1,0:T(8,128)(2,1)S(1)}, u32[]{:S(2)}, u32[]{:S(2)}) collective-permute-start(bf16[96,896]{1,0:T(8,128)(2,1)S(1)} %collective-permute-done.4.refs_7_), channel_id=1, source_target_pairs={{0,4},{8,0},{16,8},{24,16},{28,24},{20,28},{12,20},{4,12},{1,5},{9... | collective-permute-start | bytes 516104 | tf_op jit(solution)/shard_map/ppermute | solution.py:1169
  26.0 5.4 %collective-permute-start.9 = (bf16[96,896]{1,0:T(8,128)(2,1)S(1)}, bf16[96,896]{1,0:T(8,128)(2,1)S(1)}, u32[]{:S(2)}, u32[]{:S(2)}) collective-permute-start(bf16[96,896]{1,0:T(8,128)(2,1)S(1)} %collective-permute-done.5.refs_8_), channel_id=1, source_target_pairs={{0,8},{8,16},{16,24},{24,28},{28,20},{20,12},{12,4},{4,0},{1,9},{9... | collective-permute-start | bytes 516104 | tf_op jit(solution)/shard_map/ppermute | solution.py:1169
  27.5 5.9 %collective-permute-start.7 = (bf16[256,768]{1,0:T(8,128)(2,1)S(1)}, bf16[256,768]{1,0:T(8,128)(2,1)S(1)}, u32[]{:S(2)}, u32[]{:S(2)}) collective-permute-start(bf16[256,768]{1,0:T(8,128)(2,1)S(1)} %copy-done.3), channel_id=1, source_target_pairs={{0,1},{1,0},{2,3},{3,2},{4,5},{5,4},{6,7},{7,6},{8,9},{9,8},{10,11... | collective-permute-start | bytes 1179656 | tf_op jit(solution)/shard_map/ppermute | solution.py:1120
  27.5 5.9 %collective-permute-start.8 = (bf16[256,768]{1,0:T(8,128)(2,1)S(1)}, bf16[256,768]{1,0:T(8,128)(2,1)S(1)}, u32[]{:S(2)}, u32[]{:S(2)}) collective-permute-start(bf16[256,768]{1,0:T(8,128)(2,1)S(1)} %collective-permute-done.refs_3_), channel_id=1, source_target_pairs={{0,1},{1,0},{2,3},{3,2},{4,5},{5,4},{6,7},{7,6},{8,9},{9,8},{10,11... | collective-permute-start | bytes 1179656 | tf_op jit(solution)/shard_map/ppermute | solution.py:1120
  28.1 11.0 %collective-permute-start.11 = (bf16[256,768]{1,0:T(8,128)(2,1)S(1)}, bf16[256,768]{1,0:T(8,128)(2,1)S(1)}, u32[]{:S(2)}, u32[]{:S(2)}) collective-permute-start(bf16[256,768]{1,0:T(8,128)(2,1)S(1)} %copy-done.2), channel_id=1, source_target_pairs={{0,2},{1,3},{2,0},{3,1},{4,6},{5,7},{6,4},{7,5},{8,10},{9,11},{10,... | collective-permute-start | bytes 1179656 | tf_op jit(solution)/shard_map/ppermute | solution.py:1120
  30.3 3.8 %copy-start.4 = (s32[1,1024]{1,0:T(1,128)S(1)}, s32[1,1024]{1,0:T(1,128)}, u32[]{:S(2)}) copy-start(s32[1,1024]{1,0:T(1,128)} %refs_6_.2) | copy-start | bytes 12292
  31.4 12.5 %collective-permute-start.22 = (bf16[96,1536]{1,0:T(8,128)(2,1)S(1)}, bf16[96,1536]{1,0:T(8,128)(2,1)S(1)}, u32[]{:S(2)}, u32[]{:S(2)}) collective-permute-start(bf16[96,1536]{1,0:T(8,128)(2,1)S(1)} %pack_forward.1.refs_15_), channel_id=1, source_target_pairs={{0,8},{8,16},{16,24},{24,28},{28,20},{20,12},{12,4},{4,0},{1,9},{9... | collective-permute-start | bytes 884744 | tf_op jit(solution)/shard_map/ppermute | solution.py:1169
  32.9 11.0 %collective-permute-start.23 = (bf16[96,1536]{1,0:T(8,128)(2,1)S(1)}, bf16[96,1536]{1,0:T(8,128)(2,1)S(1)}, u32[]{:S(2)}, u32[]{:S(2)}) collective-permute-start(bf16[96,1536]{1,0:T(8,128)(2,1)S(1)} %pack_forward.1.refs_15_), channel_id=1, source_target_pairs={{0,4},{8,0},{16,8},{24,16},{28,24},{20,28},{12,20},{4,12},{1,5},{9... | collective-permute-start | bytes 884744 | tf_op jit(solution)/shard_map/ppermute | solution.py:1169
  39.1 8.3 %collective-permute-start.10 = (bf16[1152,128]{1,0:T(8,128)(2,1)S(1)}, bf16[1152,128]{1,0:T(8,128)(2,1)S(1)}, u32[]{:S(2)}, u32[]{:S(2)}) collective-permute-start(bf16[1152,128]{1,0:T(8,128)(2,1)S(1)} %get-tuple-element.160.refs_11_), channel_id=1, source_target_pairs={{0,2},{1,3},{2,0},{3,1},{4,6},{5,7},{6,4},{7,5},{8,10},{9,11},{10,... | collective-permute-start | bytes 884744 | tf_op jit(solution)/shard_map/ppermute | solution.py:1120
  43.9 9.1 %collective-permute-start.24 = (bf16[96,1536]{1,0:T(8,128)(2,1)S(1)}, bf16[96,1536]{1,0:T(8,128)(2,1)S(1)}, u32[]{:S(2)}, u32[]{:S(2)}) collective-permute-start(bf16[96,1536]{1,0:T(8,128)(2,1)S(1)} %collective-permute-done.22.refs_16_), channel_id=1, source_target_pairs={{0,8},{8,16},{16,24},{24,28},{28,20},{20,12},{12,4},{4,0},{1,9},{9... | collective-permute-start | bytes 884744 | tf_op jit(solution)/shard_map/ppermute | solution.py:1169
  45.6 7.5 %collective-permute-start.25 = (bf16[96,1536]{1,0:T(8,128)(2,1)S(1)}, bf16[96,1536]{1,0:T(8,128)(2,1)S(1)}, u32[]{:S(2)}, u32[]{:S(2)}) collective-permute-start(bf16[96,1536]{1,0:T(8,128)(2,1)S(1)} %collective-permute-done.23.refs_17_), channel_id=1, source_target_pairs={{0,4},{8,0},{16,8},{24,16},{28,24},{20,28},{12,20},{4,12},{1,5},{9... | collective-permute-start | bytes 884744 | tf_op jit(solution)/shard_map/ppermute | solution.py:1169
  46.0 5.7 %collective-permute-start.12 = (bf16[768,128]{1,0:T(8,128)(2,1)S(1)}, bf16[768,128]{1,0:T(8,128)(2,1)S(1)}, u32[]{:S(2)}, u32[]{:S(2)}) collective-permute-start(bf16[768,128]{1,0:T(8,128)(2,1)S(1)} %get-tuple-element.158.refs_3_), channel_id=1, source_target_pairs={{0,2},{1,3},{2,0},{3,1},{4,6},{5,7},{6,4},{7,5},{8,10},{9,11},{10,... | collective-permute-start | bytes 589832 | tf_op jit(solution)/shard_map/ppermute | solution.py:1120
  51.7 5.7 %collective-permute-start.13 = (bf16[768,128]{1,0:T(8,128)(2,1)S(1)}, bf16[768,128]{1,0:T(8,128)(2,1)S(1)}, u32[]{:S(2)}, u32[]{:S(2)}) collective-permute-start(bf16[768,128]{1,0:T(8,128)(2,1)S(1)} %attend.3.refs_4_), channel_id=1, source_target_pairs={{0,2},{1,3},{2,0},{3,1},{4,6},{5,7},{6,4},{7,5},{8,10},{9,11},{10,... | collective-permute-start | bytes 589832 | tf_op jit(solution)/shard_map/ppermute | solution.py:1120
  53.1 7.1 %collective-permute-start.26 = (bf16[96,1536]{1,0:T(8,128)(2,1)S(1)}, bf16[96,1536]{1,0:T(8,128)(2,1)S(1)}, u32[]{:S(2)}, u32[]{:S(2)}) collective-permute-start(bf16[96,1536]{1,0:T(8,128)(2,1)S(1)} %collective-permute-done.24.refs_18_), channel_id=1, source_target_pairs={{0,8},{8,16},{16,24},{24,28},{28,20},{20,12},{12,4},{4,0},{1,9},{9... | collective-permute-start | bytes 884744 | tf_op jit(solution)/shard_map/ppermute | solution.py:1169
  54.6 6.8 %collective-permute-start.27 = (bf16[96,1536]{1,0:T(8,128)(2,1)S(1)}, bf16[96,1536]{1,0:T(8,128)(2,1)S(1)}, u32[]{:S(2)}, u32[]{:S(2)}) collective-permute-start(bf16[96,1536]{1,0:T(8,128)(2,1)S(1)} %collective-permute-done.25.refs_19_), channel_id=1, source_target_pairs={{0,4},{8,0},{16,8},{24,16},{28,24},{20,28},{12,20},{4,12},{1,5},{9... | collective-permute-start | bytes 884744 | tf_op jit(solution)/shard_map/ppermute | solution.py:1169
  57.4 6.1 %collective-permute-start.14 = (bf16[256,768]{1,0:T(8,128)(2,1)S(1)}, bf16[256,768]{1,0:T(8,128)(2,1)S(1)}, u32[]{:S(2)}, u32[]{:S(2)}) collective-permute-start(bf16[256,768]{1,0:T(8,128)(2,1)S(1)} %copy-done.2), channel_id=1, source_target_pairs={{0,1},{1,0},{2,3},{3,2},{4,5},{5,4},{6,7},{7,6},{8,9},{9,8},{10,11... | collective-permute-start | bytes 1179656 | tf_op jit(solution)/shard_map/ppermute | solution.py:1120
  57.4 6.1 %collective-permute-start.15 = (bf16[256,768]{1,0:T(8,128)(2,1)S(1)}, bf16[256,768]{1,0:T(8,128)(2,1)S(1)}, u32[]{:S(2)}, u32[]{:S(2)}) collective-permute-start(bf16[256,768]{1,0:T(8,128)(2,1)S(1)} %collective-permute-done.11.refs_3_), channel_id=1, source_target_pairs={{0,1},{1,0},{2,3},{3,2},{4,5},{5,4},{6,7},{7,6},{8,9},{9,8},{10,11... | collective-permute-start | bytes 1179656 | tf_op jit(solution)/shard_map/ppermute | solution.py:1120
  57.9 3.6 %collective-permute-start.17 = (bf16[768,128]{1,0:T(8,128)(2,1)S(1)}, bf16[768,128]{1,0:T(8,128)(2,1)S(1)}, u32[]{:S(2)}, u32[]{:S(2)}) collective-permute-start(bf16[768,128]{1,0:T(8,128)(2,1)S(1)} %attend.3.refs_4_), channel_id=1, source_target_pairs={{0,1},{1,0},{2,3},{3,2},{4,5},{5,4},{6,7},{7,6},{8,9},{9,8},{10,11... | collective-permute-start | bytes 589832 | tf_op jit(solution)/shard_map/ppermute | solution.py:1120
  60.1 1.8 collective-permute-start.16
  61.4 3.7 %collective-permute-start.20 = (bf16[1152,128]{1,0:T(8,128)(2,1)S(1)}, bf16[1152,128]{1,0:T(8,128)(2,1)S(1)}, u32[]{:S(2)}, u32[]{:S(2)}) collective-permute-start(bf16[1152,128]{1,0:T(8,128)(2,1)S(1)} %get-tuple-element.160.refs_11_), channel_id=1, source_target_pairs={{0,1},{1,0},{2,3},{3,2},{4,5},{5,4},{6,7},{7,6},{8,9},{9,8},{10,11... | collective-permute-start | bytes 884744 | tf_op jit(solution)/shard_map/ppermute | solution.py:1120
  61.5 3.7 %collective-permute-start.21 = (bf16[1152,128]{1,0:T(8,128)(2,1)S(1)}, bf16[1152,128]{1,0:T(8,128)(2,1)S(1)}, u32[]{:S(2)}, u32[]{:S(2)}) collective-permute-start(bf16[1152,128]{1,0:T(8,128)(2,1)S(1)} %collective-permute-done.10.refs_13_), channel_id=1, source_target_pairs={{0,1},{1,0},{2,3},{3,2},{4,5},{5,4},{6,7},{7,6},{8,9},{9,8},{10,11... | collective-permute-start | bytes 884744 | tf_op jit(solution)/shard_map/ppermute | solution.py:1120
  62.0 9.0 %collective-permute-start.28 = (bf16[96,1536]{1,0:T(8,128)(2,1)S(1)}, bf16[96,1536]{1,0:T(8,128)(2,1)S(1)}, u32[]{:S(2)}, u32[]{:S(2)}) collective-permute-start(bf16[96,1536]{1,0:T(8,128)(2,1)S(1)} %collective-permute-done.26.refs_20_), channel_id=1, source_target_pairs={{0,8},{8,16},{16,24},{24,28},{28,20},{20,12},{12,4},{4,0},{1,9},{9... | collective-permute-start | bytes 884744 | tf_op jit(solution)/shard_map/ppermute | solution.py:1169
  63.5 1.4 collective-permute-start.18
  63.5 1.7 collective-permute-start.19
  82.2 5.2 %collective-permute-start.29 = (bf16[512,768]{1,0:T(8,128)(2,1)S(1)}, bf16[512,768]{1,0:T(8,128)(2,1)S(1)}, u32[]{:S(2)}, u32[]{:S(2)}) collective-permute-start(bf16[512,768]{1,0:T(8,128)(2,1)S(1)} %get-tuple-element.181), channel_id=1, source_target_pairs={{0,1},{1,0},{2,3},{3,2},{4,5},{5,4},{6,7},{7,6},{8,9},{9,8},{10,11... | collective-permute-start | bytes 2359304 | tf_op jit(solution)/shard_map/ppermute | solution.py:1120
  87.4 59.3 %all-to-all-start.1 = ((bf16[8,96,1536]{2,1,0:T(8,128)(2,1)}), bf16[8,96,1536]{2,1,0:T(8,128)(2,1)}, u32[]{:S(2)}, u32[]{:S(2)}) async-start(bf16[8,96,1536]{2,1,0:T(8,128)(2,1)} %bitcast.2), calls=%async_computation.1 | async-start | bytes 4718592 | tf_op jit(solution)/shard_map/all_to_all | solution.py:1196
  92.8 11.3 %collective-permute-start.30 = (bf16[256,768]{1,0:T(8,128)(2,1)S(1)}, bf16[256,768]{1,0:T(8,128)(2,1)S(1)}, u32[]{:S(2)}, u32[]{:S(2)}) collective-permute-start(bf16[256,768]{1,0:T(8,128)(2,1)S(1)} %get-tuple-element.183), channel_id=1, source_target_pairs={{0,2},{1,3},{2,0},{3,1},{4,6},{5,7},{6,4},{7,5},{8,10},{9,11},{10,... | collective-permute-start | bytes 1179656 | tf_op jit(solution)/shard_map/ppermute | solution.py:1120
  105.3 3.6 %collective-permute-start.31 = (bf16[512,768]{1,0:T(8,128)(2,1)S(1)}, bf16[512,768]{1,0:T(8,128)(2,1)S(1)}, u32[]{:S(2)}, u32[]{:S(2)}) collective-permute-start(bf16[512,768]{1,0:T(8,128)(2,1)S(1)} %get-tuple-element.191), channel_id=1, source_target_pairs={{0,1},{1,0},{2,3},{3,2},{4,5},{5,4},{6,7},{7,6},{8,9},{9,8},{10,11... | collective-permute-start | bytes 2359304 | tf_op jit(solution)/shard_map/ppermute | solution.py:1120
  105.4 11.5 %collective-permute-start.33 = (bf16[256,768]{1,0:T(8,128)(2,1)S(1)}, bf16[256,768]{1,0:T(8,128)(2,1)S(1)}, u32[]{:S(2)}, u32[]{:S(2)}) collective-permute-start(bf16[256,768]{1,0:T(8,128)(2,1)S(1)} %get-tuple-element.190.refs_1_), channel_id=1, source_target_pairs={{0,2},{1,3},{2,0},{3,1},{4,6},{5,7},{6,4},{7,5},{8,10},{9,11},{10,... | collective-permute-start | bytes 1179656 | tf_op jit(solution)/shard_map/ppermute | solution.py:1120
  107.0 9.8 %collective-permute-start.32 = (bf16[256,768]{1,0:T(8,128)(2,1)S(1)}, bf16[256,768]{1,0:T(8,128)(2,1)S(1)}, u32[]{:S(2)}, u32[]{:S(2)}) collective-permute-start(bf16[256,768]{1,0:T(8,128)(2,1)S(1)} %get-tuple-element.190.refs_1_), channel_id=1, source_target_pairs={{0,1},{1,0},{2,3},{3,2},{4,5},{5,4},{6,7},{7,6},{8,9},{9,8},{10,11... | collective-permute-start | bytes 1179656 | tf_op jit(solution)/shard_map/ppermute | solution.py:1120
  116.9 1.7 collective-permute-start.34
  122.9 13.8 %collective-permute-start.35 = (bf16[256,768]{1,0:T(8,128)(2,1)S(1)}, bf16[256,768]{1,0:T(8,128)(2,1)S(1)}, u32[]{:S(2)}, u32[]{:S(2)}) collective-permute-start(bf16[256,768]{1,0:T(8,128)(2,1)S(1)} %get-tuple-element.201), channel_id=1, source_target_pairs={{0,2},{1,3},{2,0},{3,1},{4,6},{5,7},{6,4},{7,5},{8,10},{9,11},{10,... | collective-permute-start | bytes 1179656 | tf_op jit(solution)/shard_map/ppermute | solution.py:1120
  136.7 0.7 copy-start.6
  146.7 37.6 %all-to-all-start = ((bf16[8,96,896]{2,1,0:T(8,128)(2,1)}), bf16[8,96,896]{2,1,0:T(8,128)(2,1)S(1)}, u32[]{:S(2)}, u32[]{:S(2)}) async-start(bf16[8,96,896]{2,1,0:T(8,128)(2,1)} %bitcast.6), calls=%async_computation | async-start | bytes 2752512 | tf_op jit(solution)/shard_map/all_to_all | solution.py:1196
  155.2 3.3 %collective-permute-start.36 = (bf16[512,768]{1,0:T(8,128)(2,1)S(1)}, bf16[512,768]{1,0:T(8,128)(2,1)S(1)}, u32[]{:S(2)}, u32[]{:S(2)}) collective-permute-start(bf16[512,768]{1,0:T(8,128)(2,1)S(1)} %get-tuple-element.219), channel_id=1, source_target_pairs={{0,1},{1,0},{2,3},{3,2},{4,5},{5,4},{6,7},{7,6},{8,9},{9,8},{10,11... | collective-permute-start | bytes 2359304 | tf_op jit(solution)/shard_map/ppermute | solution.py:1120
  157.8 9.9 %collective-permute-start.39 = (bf16[96,1536]{1,0:T(8,128)(2,1)S(1)}, bf16[96,1536]{1,0:T(8,128)(2,1)S(1)}, u32[]{:S(2)}, u32[]{:S(2)}) collective-permute-start(bf16[96,1536]{1,0:T(8,128)(2,1)S(1)} %owned_sum.1.refs_1_), channel_id=1, source_target_pairs={{0,2},{1,3},{2,0},{3,1},{4,6},{5,7},{6,4},{7,5},{8,10},{9,11},{10,... | collective-permute-start | bytes 884744 | tf_op jit(solution)/shard_map/ppermute | solution.py:1120
  159.2 16.6 %collective-permute-start.37 = (bf16[256,768]{1,0:T(8,128)(2,1)S(1)}, bf16[256,768]{1,0:T(8,128)(2,1)}, u32[]{:S(2)}, u32[]{:S(2)}) collective-permute-start(bf16[256,768]{1,0:T(8,128)(2,1)S(1)} %get-tuple-element.221), channel_id=1, source_target_pairs={{0,2},{1,3},{2,0},{3,1},{4,6},{5,7},{6,4},{7,5},{8,10},{9,11},{10,... | collective-permute-start | bytes 1179656 | tf_op jit(solution)/shard_map/ppermute | solution.py:1120
  160.7 9.7 %collective-permute-start.38 = (bf16[96,1536]{1,0:T(8,128)(2,1)S(1)}, bf16[96,1536]{1,0:T(8,128)(2,1)S(1)}, u32[]{:S(2)}, u32[]{:S(2)}) collective-permute-start(bf16[96,1536]{1,0:T(8,128)(2,1)S(1)} %owned_sum.1.refs_1_), channel_id=1, source_target_pairs={{0,1},{1,0},{2,3},{3,2},{4,5},{5,4},{6,7},{7,6},{8,9},{9,8},{10,11... | collective-permute-start | bytes 884744 | tf_op jit(solution)/shard_map/ppermute | solution.py:1120
  167.7 2.7 %collective-permute-start.40 = (bf16[96,1536]{1,0:T(8,128)(2,1)S(1)}, bf16[96,1536]{1,0:T(8,128)(2,1)S(1)}, u32[]{:S(2)}, u32[]{:S(2)}) collective-permute-start(bf16[96,1536]{1,0:T(8,128)(2,1)S(1)} %collective-permute-done.39.refs_3_), channel_id=1, source_target_pairs={{0,1},{1,0},{2,3},{3,2},{4,5},{5,4},{6,7},{7,6},{8,9},{9,8},{10,11... | collective-permute-start | bytes 884744 | tf_op jit(solution)/shard_map/ppermute | solution.py:1120
  185.1 5.5 %collective-permute-start.42 = (bf16[96,896]{1,0:T(8,128)(2,1)S(1)}, bf16[96,896]{1,0:T(8,128)(2,1)S(1)}, u32[]{:S(2)}, u32[]{:S(2)}) collective-permute-start(bf16[96,896]{1,0:T(8,128)(2,1)S(1)} %owned_vector.1.refs_1_), channel_id=1, source_target_pairs={{0,2},{1,3},{2,0},{3,1},{4,6},{5,7},{6,4},{7,5},{8,10},{9,11},{10,... | collective-permute-start | bytes 516104 | tf_op jit(solution)/shard_map/ppermute | solution.py:1120
  185.8 4.7 %collective-permute-start.41 = (bf16[96,896]{1,0:T(8,128)(2,1)S(1)}, bf16[96,896]{1,0:T(8,128)(2,1)S(1)}, u32[]{:S(2)}, u32[]{:S(2)}) collective-permute-start(bf16[96,896]{1,0:T(8,128)(2,1)S(1)} %owned_vector.1.refs_1_), channel_id=1, source_target_pairs={{0,1},{1,0},{2,3},{3,2},{4,5},{5,4},{6,7},{7,6},{8,9},{9,8},{10,11... | collective-permute-start | bytes 516104 | tf_op jit(solution)/shard_map/ppermute | solution.py:1120
  190.5 1.4 collective-permute-start.43
  193.8 11.2 %all-to-all-start.2 = ((f32[8,8,128]{2,1,0:T(8,128)}), f32[8,8,128]{2,1,0:T(8,128)S(1)}, u32[]{:S(2)}, u32[]{:S(2)}) async-start(f32[8,8,128]{2,1,0:T(8,128)} %bitcast.3), calls=%async_computation.2 | async-start | bytes 65536 | tf_op jit(solution)/shard_map/all_to_all | solution.py:1359

commit v2 on v1

--- a/solution.py
+++ b/solution.py
@@ -215,7 +215,7 @@
         compiler_params=params(8),
         cost_estimate=cost(1.5),
         name="pack_attention",
-    )(scal, *[attention] * 4, vector)
+    )(scal, *[pin(attention)] * 4, pin(vector))
 
 
 def cast_kernel(scal, in_ref, out_ref):
@@ -774,18 +774,35 @@
     )
 
 
-def query_grads_kernel(cols, scal, *refs, ready):
+TERMS = 8
+
+
+def vector_places(count, rows, width):
+    each = width // rows
+    return [(i // each, (i % each) * rows) for i in range(2 * count)]
+
+
+def query_grads_kernel(cols, count, ringed, scal, *refs, ready):
     a_ref, hat_ref, out_ref, grad_ref, w_ref, table_ref, g_ref = refs
     width = a_ref.shape[1]
-    block = 256
+    owners = len(RING)
+    rows = width // owners
+    block = 4 * rows if ringed else 256
     ready(1)
 
-    def weights(i, carry):
-        lanes = pl.ds(pl.multiple_of(i * block, block), block)
-        g_ref[lanes, : 3 * cols] = dot_rows(a_ref[:, lanes], grad_ref[...]).astype(BF)
-        return carry
-
-    lax.fori_loop(0, width // block, weights, 0)
+    def place(first):
+        if not ringed:
+            return slice(first, first + block)
+        owner = first // rows
+        return slice(first + TERMS * owner, first + TERMS * owner + rows)
+
+    for first in range(0, width, block):
+        total = dot_rows(a_ref[:, first : first + block], grad_ref[...]).astype(BF)
+        if not ringed:
+            g_ref[place(first), : 3 * cols] = total
+        else:
+            for i in range(4):
+                g_ref[place(first + i * rows), : 3 * cols] = total[i * rows : (i + 1) * rows, :]
     row = lax.broadcasted_iota(jnp.int32, (8, 3 * cols), 0)
     rest = dot_rows(jnp.ones((a_ref.shape[0], 8), BF), grad_ref[...])
     terms = jnp.zeros((8, 3 * cols), F32)
@@ -796,10 +813,11 @@
     terms = terms.astype(BF)
     for position in (2, 3, 5, 6):
         ready(position)
-    lane = lax.broadcasted_iota(jnp.int32, (block, 128), 1)
+    chunk = 256
+    lane = lax.broadcasted_iota(jnp.int32, (chunk, 128), 1)
 
     def vectors(i, carry):
-        lanes = pl.ds(pl.multiple_of(i * block, block), block)
+        lanes = pl.ds(pl.multiple_of(i * chunk, chunk), chunk)
         weight = w_ref[lanes, :]
         product = dot_rows(hat_ref[:, lanes], grad_ref[...]) * weight.astype(F32)
         gain = jnp.sum(product, axis=1, keepdims=True)
@@ -808,8 +826,7 @@
         table_ref[lanes, :] = jnp.where(lane == 1, shift, table)
         return carry
 
-    lax.fori_loop(0, width // block, vectors, 0)
-    g_ref[:, 3 * cols : 4 * cols] = out_ref[...]
+    lax.fori_loop(0, width // chunk, vectors, 0)
     own = pl.ds(pl.multiple_of(scal[0] * cols, cols), cols)
     bias = table_ref[own, :]
     near = lax.broadcasted_iota(jnp.int32, (cols, 128), 1)
@@ -821,17 +838,34 @@
     total = table_ref[...]
     high = total.astype(BF)
     low = (total - high.astype(F32)).astype(BF)
-    g_ref[:, 4 * cols : 4 * cols + 16] = high[:, 0:16]
-    g_ref[:, 4 * cols + 16 : 4 * cols + 32] = low[:, 0:16]
-    g_ref[:, 4 * cols + 32 :] = jnp.zeros((width, 96), BF)
-
-
-def query_grads(scal, normed, hat, grad_out, grad, weights, table):
+    if not ringed:
+        g_ref[:, 3 * cols : 4 * cols] = out_ref[...]
+        g_ref[:, 4 * cols : 4 * cols + 16] = high[:, 0:16]
+        g_ref[:, 4 * cols + 16 : 4 * cols + 32] = low[:, 0:16]
+        g_ref[:, 4 * cols + 32 :] = jnp.zeros((width, 96), BF)
+        return
+    unit = unit_rows(16, 128)
+    lines = (dot_cols(unit, high), dot_cols(unit, low))
+    places = vector_places(count, rows, width)
+    for owner in range(owners):
+        first = owner * rows
+        g_ref[place(first), 3 * cols :] = out_ref[first : first + rows, :]
+        base = first + TERMS * owner + rows
+        g_ref[base : base + TERMS, :] = jnp.zeros((TERMS, width), BF)
+        for i, (line, start) in enumerate(places):
+            piece = lines[i // count][i % count : i % count + 1, first : first + rows]
+            g_ref[base + line : base + line + 1, start : start + rows] = piece.astype(BF)
+
+
+def query_grads(scal, normed, hat, grad_out, grad, weights, table, count, ringed):
     width, cols = grad_out.shape
+    shape = (width, 4 * cols + 128)
+    if ringed:
+        shape = (width + TERMS * len(RING), 4 * cols)
     return run(
-        functools.partial(query_grads_kernel, cols),
+        functools.partial(query_grads_kernel, cols, count, ringed),
         "query_grads",
-        shaped((width, 4 * cols + 128), BF),
+        shaped(shape, BF),
         (scal, normed, hat, grad_out, grad, weights, table),
         4.0,
         lazy=(1, 2, 3, 5, 6),
@@ -910,10 +944,19 @@
     return run(squares_kernel, "squares_of", outputs, (scal, *pieces), 1.0, save=range(1, 5))
 
 
-def owned_vector_kernel(cols, scal, in_ref, low_ref):
+def owned_vector_kernel(cols, ringed, scal, in_ref, low_ref):
     total = in_ref[0].astype(F32)
     for i in range(1, in_ref.shape[0]):
         total += in_ref[i].astype(F32)
+    if ringed:
+        rows = total.shape[0] - TERMS
+        low_ref[:rows, :] = total[:rows, :].astype(BF)
+        vector = total[rows:, :]
+        high = vector.astype(BF).astype(F32)
+        line = lax.broadcasted_iota(jnp.int32, vector.shape, 0)
+        rest = pltpu.roll(vector - high, 3, 0)
+        low_ref[rows:, :] = jnp.where(line < 3, high, rest).astype(BF)
+        return
     low_ref[:, : 4 * cols] = total[:, : 4 * cols].astype(BF)
     vector = total[:, 4 * cols :]
     high = vector.astype(BF).astype(F32)
@@ -922,67 +965,66 @@
     low_ref[:, 4 * cols :] = jnp.where(lane < 32, high, rest).astype(BF)
 
 
-def owned_vector(scal, pieces, cols):
-    _, rows, width = pieces.shape
+def owned_vector(scal, pieces, cols, ringed):
     return run(
-        functools.partial(owned_vector_kernel, cols),
+        functools.partial(owned_vector_kernel, cols, ringed),
         "owned_vector",
-        shaped((rows, width), BF),
+        shaped(pieces.shape[1:], BF),
         (scal, pieces),
         1.5,
     )
 
 
-def join_kernel(cols, count, scal, *refs):
-    pieces, forward_ref = refs[0:4], refs[4]
-    gradient_ref, vector_ref, squares_ref = refs[5:8]
-    width = gradient_ref.shape[1] // 4
-    for member in range(GROUPS):
-
-        @pl.when(scal[0] == member)
-        def _():
-            for i in range(4):
-                for k in range(GROUPS):
-                    start = i * width + (member ^ k) * cols
-                    gradient_ref[:, start : start + cols] = pieces[k][
-                        :, i * cols : (i + 1) * cols
-                    ].astype(F32)
-
-    def vector_of(piece):
-        return piece[:, 4 * cols :].astype(F32)
-
-    halves = [vector_of(piece) for piece in pieces]
-    table = (halves[0] + halves[1]) + (halves[2] + halves[3])
+def vector_sum(pieces, cols, count, ringed, held):
+    if ringed:
+        rows, width = pieces[0].shape
+        rows -= TERMS
+        parts = [piece[rows:, :].astype(F32) for piece in pieces]
+        lines = (parts[0] + parts[1]) + (parts[2] + parts[3])
+        lines = lines + pltpu.roll(lines, TERMS - 3, 0)
+        places = vector_places(count, rows, width)
+        for i in range(count):
+            total = jnp.zeros((1, rows), F32)
+            for line, start in (places[i], places[i + count]):
+                total += lines[line : line + 1, start : start + rows]
+            held[i : i + 1, :] = total
+        return held[...]
+    parts = [piece[:, 4 * cols :].astype(F32) for piece in pieces]
+    table = (parts[0] + parts[1]) + (parts[2] + parts[3])
     rows = lax.broadcasted_iota(jnp.int32, (16, 128), 0)
     lanes = lax.broadcasted_iota(jnp.int32, (16, 128), 1)
     unit = jnp.where((lanes % 16 == rows) & (lanes < 64), 1.0, 0.0)
-    vector = lax.dot_general(
+    return lax.dot_general(
         unit,
         table,
         (((1,), (1,)), ((), ())),
         preferred_element_type=F32,
         precision=lax.Precision.HIGHEST,
     )[:count]
-    vector_ref[...] = vector
-    gradient = gradient_ref[...]
-    total = jnp.sum(gradient * gradient) + jnp.sum(vector * vector)
+
+
+def join_kernel(cols, count, ringed, scal, *refs):
+    pieces, forward_ref, squares_ref, held = refs[0:4], refs[4], refs[5], refs[6]
+    rows = held.shape[1]
+    sums = []
+    for piece in pieces:
+        wide = piece[:rows, : 4 * cols].astype(F32)
+        sums.append(wide * wide)
+    vector = vector_sum(pieces, cols, count, ringed, held)
+    total = jnp.sum((sums[0] + sums[1]) + (sums[2] + sums[3])) + jnp.sum(vector * vector)
     total = forward_ref[...] + total
     for i in range(squares_ref.shape[0] // 8):
         squares_ref[8 * i : 8 * i + 8, :] = total
 
 
-def join(scal, pieces, squares, width, count, cols, owners):
-    rows = pieces[0].shape[0]
+def join(scal, pieces, squares, shape, cols, owners, ringed):
     return run(
-        functools.partial(join_kernel, cols, count),
+        functools.partial(join_kernel, cols, shape[0], ringed),
         "join",
-        (
-            shaped((rows, 4 * width), F32),
-            shaped((count, rows), F32),
-            shaped((8 * owners, 128), F32),
-        ),
+        shaped((8 * owners, 128), F32),
         (scal, *pieces, squares),
         1.5,
+        [pltpu.VMEM(shape, F32)],
     )
 
 
@@ -994,11 +1036,12 @@
     return norm, jnp.minimum(1.0, clip_limit / (norm + 1e-06))
 
 
-def adam_kernel(counts, scal, total_ref, attention_ref, vector_ref, *refs):
+def adam_kernel(counts, cols, ringed, scal, total_ref, *refs):
+    attention, refs = refs[0:4], refs[4:]
     pieces, sources, targets, norm_ref = refs[0:4], refs[4:16], refs[16:31], refs[31]
     held, copies = refs[32:44], refs[44:47]
     loads, stores = refs[47:50], refs[50:53]
-    grads, grad_loads = refs[53:57], refs[57]
+    grads, grad_loads, attention_ref, vector_ref = refs[53:57], refs[57], refs[58], refs[59]
     norm, factor = clip_factor(total_ref)
     norm_ref[...] = jnp.broadcast_to(norm, norm_ref.shape)
     decays = (weight_decay, weight_decay, 0.0)
@@ -1039,9 +1082,9 @@
             load(kind, i, state).wait()
         place = chunk(kind, i)
         if kind == 0:
-            gradient = attention_ref[place]
+            gradient = attention_ref[place].astype(F32)
         elif kind == 2:
-            gradient = vector_ref[...]
+            gradient = vector_sum(attention, cols, held[8].shape[0], ringed, vector_ref)
         else:
             size = held[4].shape[1] // counts[1]
             half = pl.ds(pl.multiple_of((i // GROUPS) * size, size), size)
@@ -1071,6 +1114,18 @@
         move.start()
     for kind in (1, 0, 2):
         every(kind, start)
+    width = attention_ref.shape[1] // 4
+    for member in range(GROUPS):
+
+        @pl.when(scal[0] == member)
+        def _():
+            for i in range(4):
+                for k in range(GROUPS):
+                    first = i * width + (member ^ k) * cols
+                    attention_ref[:, first : first + cols] = attention[k][
+                        : held[0].shape[0], i * cols : (i + 1) * cols
+                    ]
+
     for move in moves:
         move.wait()
     for kind in (1, 0, 2):
@@ -1079,27 +1134,28 @@
         every(kind, finish)
 
 
-def adam(scal, totals, attention_grad, vector_grad, forward_grads_by_member, states):
+def adam(scal, totals, attention_grads, forward_grads_by_member, states, cols, ringed):
     counts = (4, 2 * GROUPS, 1)
     kinds = [states[4 * kind].shape for kind in range(3)]
     out_shape = [pltpu.HBM(shape, F32) for _ in range(4) for shape in kinds]
     out_shape += [pltpu.HBM(shape, BF) for shape in kinds]
     out_shape += [shaped((8, 128), F32)]
     return pl.pallas_call(
-        functools.partial(adam_kernel, counts),
+        functools.partial(adam_kernel, counts, cols, ringed),
         out_shape=out_shape,
-        in_specs=[smem()] + [vmem()] * 3 + [far_space()] * 16,
+        in_specs=[smem()] + [vmem()] * 5 + [far_space()] * 16,
         out_specs=[far_space()] * 15 + [vmem()],
         scratch_shapes=[pltpu.VMEM(kinds[kind], F32) for kind in range(3) for _ in range(4)]
         + [pltpu.VMEM(shape, BF) for shape in kinds]
         + [pltpu.SemaphoreType.DMA((count, 4)) for count in counts]
         + [pltpu.SemaphoreType.DMA((count, 5)) for count in counts]
         + [pltpu.VMEM(item.shape, item.dtype) for item in forward_grads_by_member]
-        + [pltpu.SemaphoreType.DMA((GROUPS,))],
+        + [pltpu.SemaphoreType.DMA((GROUPS,))]
+        + [pltpu.VMEM(kinds[0], BF), pltpu.VMEM(kinds[2], F32)],
         compiler_params=params(32),
         cost_estimate=cost(9.0),
         name="adam",
-    )(scal, totals, attention_grad, vector_grad, *map(pin, forward_grads_by_member), *map(pin, states))
+    )(scal, totals, *attention_grads, *map(pin, forward_grads_by_member), *map(pin, states))
 
 
 def adam_update(master, moment, second, teacher, gradient, factor, decay_rate):
@@ -1244,6 +1300,8 @@
     queries, keys, values, w_qkv, w_o, vec, seg_col, normed, hat, ranges = project(
         scal, segments, x_all, first.pieces, cols
     )
+    if ringed:
+        second.hop(queries)
     half = x_all.shape[0] // 2
     w_across = swap(w_o, 2)
     mixed_low, *kept = attend(
@@ -1262,14 +1320,12 @@
     far_q, far_k, far_v, far_col, far_weights, far_vec, *far_normed = kept
     low_across = swap(mixed_low, 2)
     w_across = after(w_across, mixed_low)
-    if ringed:
-        second.hop(mixed_low)
     mixed_high = attend(
         scal, ranges, after(queries, w_across), keys, values, segments, seg_col, per, half, half
     )
-    high_across = swap(after(mixed_high, low_across), 2)
     if ringed:
         second.hop(mixed_high)
+    high_across = swap(after(mixed_high, low_across), 2)
     w_across, low_across, w_o, mixed_low, grad, grad_across = lax.optimization_barrier(
         (w_across, low_across, w_o, mixed_low, cotangent, grad_across, high_across)
     )[:6]
@@ -1333,28 +1389,31 @@
         per,
         (grad_resid, table, grad_out),
     )
-    got_branch = swap(after(send, grad_mixed), 2)
+    send_branch = send
     pack = query_grads(
         scal,
-        after(far_normed[0], got_branch),
+        far_normed[0],
         far_normed[1],
         far_grad_out,
         grad_qkv,
         far_weights,
         far_table,
+        vector_master.shape[0],
+        ringed,
     )
     owned_pack = exchange_owned(pack, owners)
     forward_parts = spread(owned_sum(scal, after(owned_ff, pack)))
     forward_squares, *forward_parts = squares_of(scal, forward_parts)
     keep, send = project_back(scal, grad_qkv, after(far_weights, pack))
     mine_input, send = merge(scal, keep, swap(send, 1))
-    block_output = output_sum(scal, after(mine, pack), got_branch, far_resid, far_vec)
+    got_branch = swap(after(send_branch, pack), 2)
+    block_output = output_sum(scal, mine, got_branch, far_resid, far_vec)
     got_input = swap(send, 2)
-    owned_pack = after(owned_pack, block_output, forward_squares, got_input)
+    owned_pack = after(owned_pack, forward_squares, got_input)
     input_gradient = input_back(scal, mine_input, got_input, tokens, far_dh, far_vec)
-    attention_parts = spread(owned_vector(scal, owned_pack, cols))
-    attention_grad, vector_grad, squares = join(
-        scal, attention_parts, forward_squares, width, vector_master.shape[0], cols, owners
+    attention_parts = spread(owned_vector(scal, owned_pack, cols, ringed))
+    squares = join(
+        scal, attention_parts, forward_squares, vector_master.shape, cols, owners, ringed
     )
     totals = lax.all_to_all(
         squares.reshape(owners, 8, 128), "dp", split_axis=0, concat_axis=0
@@ -1362,8 +1421,7 @@
     *results, norm = adam(
         scal,
         totals,
-        attention_grad,
-        vector_grad,
+        attention_parts,
         forward_parts,
         (
             attention_master,
@@ -1379,6 +1437,8 @@
             vector_second,
             vector_teacher,
         ),
+        cols,
+        ringed,
     )
     return (block_output, input_gradient, norm[0, 0], *results)
 

time: 219 us -> 216 us (0.986)
  waiting for transfers between devices: 69.6 us -> 66.8 us
  local copies, waits for them, and re-layouts: 3.94 us -> 1.23 us
    all_to_all x1, waiting for transfers between devices: 3.34 us -> 0.63 us  [local(): lax.all_to_all(squares.reshape(owners, 8, 128), 'dp', split_axis=0, conca...]
    unnamed x14 -> x8, local copies, waits for them, and re-layouts: 2.72 us -> 0.02 us
  transfers between devices with their start and end apart: 47 -> 47, of which waited for: 26 -> 25; matrix products, arithmetic and copies ran while one was open for 0% -> 0% of each run, Pallas kernels for 32% -> 33%
where the time goes in v2:
time: 216 us
  Pallas kernels  98 us (45%)
  waiting for transfers between devices  66.8 us (31%)
  starting transfers between devices  48.6 us (22%)
    pallas_call x23, Pallas kernels, run(): pl.pallas_call(body, out_shape=shapes + [pltpu.HBM(inputs[i].shape, input...  82.2 us
    ppermute x30, waiting for transfers between devices, swap(): return lax.ppermute(part, 'head', [(i, i ^ bit) for i in range(4)])  33.8 us
    ppermute x14, waiting for transfers between devices, send(): return lax.ppermute(array, 'dp', pairs)  22.4 us
    ppermute x30, starting transfers between devices, swap(): return lax.ppermute(part, 'head', [(i, i ^ bit) for i in range(4)])  17.3 us
    ppermute x14, starting transfers between devices, send(): return lax.ppermute(array, 'dp', pairs)  16.9 us
    pallas_call x1, Pallas kernels, adam(): pl.pallas_call(functools.partial(adam_kernel, counts, cols, ringed), out_...  12.8 us
    all_to_all x2, waiting for transfers between devices, exchange_owned(): return lax.all_to_all(blocks, 'dp', split_axis=0, concat_axis=0)  9.88 us
    all_to_all x2, starting transfers between devices, exchange_owned(): return lax.all_to_all(blocks, 'dp', split_axis=0, concat_axis=0)  9.04 us
  transfers between devices with their start and end apart: 47, of which 25 were waited for; matrix products, arithmetic and copies ran while one was open for 0% of the time, Pallas kernels for 33%

profile of v2, /device:TPU:0, one launch (start us, length us, event | category | flops | bytes accessed | tf_op | source)
XLA Modules:
  0.0 215.5 jit_solution(9089820192888882963)
XLA Ops:
  0.7 0.7 dynamic-slice_bitcast_fusion.scal.refs_0_
  1.4 2.2 %pack_attention.1.refs_3_ = bf16[96,896]{1,0:T(8,128)(2,1)S(1)} custom-call(s32[10]{0:T(128)S(1)} %dynamic-slice_bitcast_fusion.scal.refs_0_, f32[96,3072]{1,0:T(8,128)} %refs_8_.1, f32[96,3072]{1,0:T(8,128)} %refs_8_.1, f32[96,3072]{1,0:T(8,128)} %refs_8_.1, f32[96,3072]{1,0:T(8,128)} %refs_8_.1, f32[12,96]{1,0:T(8,128)} %refs_16_.1), custom_call_target="tpu_custom_call" | custom-call | bytes 5400000 | tf_op jit(solution)/shard_map/pack_attention/pallas_call | solution.py:206
  3.6 3.0 %collective-permute-start.2 = (bf16[96,896]{1,0:T(8,128)(2,1)S(1)}, bf16[96,896]{1,0:T(8,128)(2,1)S(1)}, u32[]{:S(2)}, u32[]{:S(2)}) collective-permute-start(bf16[96,896]{1,0:T(8,128)(2,1)S(1)} %pack_attention.1.refs_3_), channel_id=1, source_target_pairs={{0,4},{8,0},{16,8},{24,16},{28,24},{20,28},{12,20},{4,12},{1,5},{9... | collective-permute-start | bytes 516104 | tf_op jit(solution)/shard_map/ppermute | solution.py:1225
  6.8 4.3 %collective-permute-done.2.refs_5_ = bf16[96,896]{1,0:T(8,128)(2,1)S(1)} collective-permute-done((bf16[96,896]{1,0:T(8,128)(2,1)S(1)}, bf16[96,896]{1,0:T(8,128)(2,1)S(1)}, u32[]{:S(2)}, u32[]{:S(2)}) %collective-permute-start.2) | collective-permute-done | bytes 172064 | tf_op jit(solution)/shard_map/ppermute | solution.py:1225
  11.1 1.4 collective-permute-done.1.refs_4_
  12.9 1.6 collective-permute-start.4
  14.5 1.5 collective-permute-start
  16.0 1.9 collective-permute-done.3.refs_6_
  18.3 1.7 collective-permute-start.5
  20.3 3.4 %collective-permute-done.5.refs_8_ = bf16[96,896]{1,0:T(8,128)(2,1)S(1)} collective-permute-done((bf16[96,896]{1,0:T(8,128)(2,1)S(1)}, bf16[96,896]{1,0:T(8,128)(2,1)S(1)}, u32[]{:S(2)}, u32[]{:S(2)}) %collective-permute-start.5) | collective-permute-done | bytes 172064 | tf_op jit(solution)/shard_map/ppermute | solution.py:1225
  23.7 1.7 collective-permute-done.6.refs_9_
  25.4 1.6 collective-permute-start.9
  27.5 1.5 collective-permute-start.11
  29.0 0.7 pack_forward.1.refs_15_
  29.7 1.1 collective-permute-done.9.refs_10_
  30.8 1.6 collective-permute-start.22
  33.5 4.6 %project.1 = (bf16[1024,192]{1,0:T(8,128)(2,1)S(1)}, bf16[1024,192]{1,0:T(8,128)(2,1)S(1)}, bf16[1024,192]{1,0:T(8,128)(2,1)S(1)}, bf16[768,576]{1,0:T(8,128)(2,...) custom-call(s32[10]{0:T(128)S(1)} %dynamic-slice_bitcast_fusion.scal, ...), custom_call_target="tpu_custom_call" | custom-call | bytes 16200000 | tf_op jit(solution)/shard_map/project/pallas_call | solution.py:164
  38.0 1.6 collective-permute-start.10
  39.7 1.5 collective-permute-start.24
  41.7 3.3 %attend.2 = (bf16[768,128]{1,0:T(8,128)(2,1)S(1)}, bf16[1024,192]{1,0:T(8,128)(2,1)}, bf16[1024,192]{1,0:T(8,128)(2,1)}, bf16[1024,192]{1,0:T(8,128)(2,1)}, s32[...) custom-call(s32[10]{0:T(128)S(1)} %dynamic-slice_bitcast_fusion.scal, ...), custom_call_target="tpu_custom_call" | custom-call | bytes 12600000 | tf_op jit(solution)/shard_map/attend/pallas_call | solution.py:164
  45.1 0.9 collective-permute-start.12
  46.0 3.2 %attend.3.refs_4_ = bf16[768,128]{1,0:T(8,128)(2,1)S(1)} custom-call(s32[10]{0:T(128)S(1)} %dynamic-slice_bitcast_fusion.scal.refs_0_, s32[16]{0:T(128)S(1)} %get-tuple-element.137.refs_1_, bf16[1024,192]{1,0:T(8,128)(2,1)S(1)} %get-tuple-element.149.refs_2_, bf16[1024,192]{1,0:T(8,128)(2,1)S(1)} %get-tuple-element.140.refs_3_, ...), custom_call_target="tpu_custom_call" | custom-call | bytes 12600000 | tf_op jit(solution)/shard_map/attend/pallas_call | solution.py:164
  49.2 2.4 %collective-permute-done.12.refs_7_ = bf16[768,128]{1,0:T(8,128)(2,1)S(1)} collective-permute-done((bf16[768,128]{1,0:T(8,128)(2,1)S(1)}, bf16[768,128]{1,0:T(8,128)(2,1)S(1)}, u32[]{:S(2)}, u32[]{:S(2)}) %collective-permute-start.12) | collective-permute-done | bytes 196640 | tf_op jit(solution)/shard_map/ppermute | solution.py:1176
  52.1 1.6 collective-permute-start.26
  54.1 3.1 %collective-permute-done.13.refs_8_ = bf16[768,128]{1,0:T(8,128)(2,1)S(1)} collective-permute-done((bf16[768,128]{1,0:T(8,128)(2,1)S(1)}, bf16[768,128]{1,0:T(8,128)(2,1)S(1)}, u32[]{:S(2)}, u32[]{:S(2)}) %collective-permute-start.13) | collective-permute-done | bytes 196640 | tf_op jit(solution)/shard_map/ppermute | solution.py:1176
  57.7 1.1 collective-permute-done.26.refs_20_
  58.8 1.9 collective-permute-done.27.refs_21_
  61.3 2.0 collective-permute-start.28
  65.1 5.2 %collective-permute-done.28.refs_22_ = bf16[96,1536]{1,0:T(8,128)(2,1)S(1)} collective-permute-done((bf16[96,1536]{1,0:T(8,128)(2,1)S(1)}, bf16[96,1536]{1,0:T(8,128)(2,1)S(1)}, u32[]{:S(2)}, u32[]{:S(2)}) %collective-permute-start.28) | collective-permute-done | bytes 294944 | tf_op jit(solution)/shard_map/ppermute | solution.py:1225
  70.3 11.2 %forward_back.1 = (bf16[1024,768]{1,0:T(8,128)(2,1)S(1)}, bf16[1024,768]{1,0:T(8,128)(2,1)S(1)}, bf16[1024,768]{1,0:T(8,128)(2,1)S(1)}, f32[512,768]{1,0:T(8,128...) custom-call(s32[10]{0:T(128)S(1)} %dynamic-slice_bitcast_fusion.scal, ...), custom_call_target="tpu_custom_call" | custom-call | bytes 46800000 | tf_op jit(solution)/shard_map/forward_back/pallas_call | solution.py:164
  81.6 5.1 %forward_grads.1 = (bf16[768,1536]{1,0:T(8,128)(2,1)}, bf16[1024,768]{1,0:T(8,128)(2,1)}, f32[256,768]{1,0:T(8,128)}, f32[8,768]{1,0:T(8,128)}, bf16[192,768]{1,...) custom-call(s32[10]{0:T(128)S(1)} %dynamic-slice_bitcast_fusion.scal.refs_0_, ...), custom_call_target="tpu_custom_call" | custom-call | bytes 14400000 | tf_op jit(solution)/shard_map/forward_grads/pallas_call | solution.py:164
  86.7 5.4 %all-to-all-start.1 = ((bf16[8,96,1536]{2,1,0:T(8,128)(2,1)}), bf16[8,96,1536]{2,1,0:T(8,128)(2,1)}, u32[]{:S(2)}, u32[]{:S(2)}) async-start(bf16[8,96,1536]{2,1,0:T(8,128)(2,1)} %bitcast.2), calls=%async_computation.1 | async-start | bytes 4718592 | tf_op jit(solution)/shard_map/all_to_all | solution.py:1252
  92.8 1.7 collective-permute-start.30
  94.5 6.1 %branch_part.1 = (f32[512,768]{1,0:T(8,128)}, bf16[512,768]{1,0:T(8,128)(2,1)S(1)}, bf16[256,768]{1,0:T(8,128)(2,1)S(1)}) custom-call(s32[10]{0:T(128)S(1)} %dynamic-slice_bitcast_fusion.scal.refs_0_, bf16[1024,768]{1,0:T(8,128)(2,1)} %get-tuple-element.172.refs_1_, bf16[768,1536]{1,0:T(8,128)(2,1)} %get-tuple-element.179.refs_2_, bf16[256,768]{1,0:T(8,128)(2,1)} %refs_3_.4), custom_call_target="tpu_custom_call" | custom-call | bytes 10800000 | tf_op jit(solution)/shard_map/branch_part/pallas_call | solution.py:164
  100.6 3.5 %collective-permute-done.30.refs_2_ = bf16[256,768]{1,0:T(8,128)(2,1)S(1)} collective-permute-done((bf16[256,768]{1,0:T(8,128)(2,1)S(1)}, bf16[256,768]{1,0:T(8,128)(2,1)S(1)}, u32[]{:S(2)}, u32[]{:S(2)}) %collective-permute-start.30) | collective-permute-done | bytes 393248 | tf_op jit(solution)/shard_map/ppermute | solution.py:1176
  104.1 1.2 resid_back.1
  105.4 1.7 collective-permute-start.33
  107.2 1.7 vector_table.1.refs_9_
  108.9 2.9 %merge.4 = (f32[256,768]{1,0:T(8,128)S(1)}, bf16[256,768]{1,0:T(8,128)(2,1)}) custom-call(s32[10]{0:T(128)S(1)} %dynamic-slice_bitcast_fusion.scal.refs_0_, f32[512,768]{1,0:T(8,128)} %get-tuple-element.180.refs_1_, bf16[512,768]{1,0:T(8,128)(2,1)S(1)} %collective-permute-done.31.refs_2_), custom_call_target="tpu_custom_call" | custom-call | bytes 2520000 | tf_op jit(solution)/shard_map/merge/pallas_call | solution.py:164
  111.8 5.2 %collective-permute-done.33.refs_3_ = bf16[256,768]{1,0:T(8,128)(2,1)S(1)} collective-permute-done((bf16[256,768]{1,0:T(8,128)(2,1)S(1)}, bf16[256,768]{1,0:T(8,128)(2,1)S(1)}, u32[]{:S(2)}, u32[]{:S(2)}) %collective-permute-start.33) | collective-permute-done | bytes 393248 | tf_op jit(solution)/shard_map/ppermute | solution.py:1176
  116.9 1.7 collective-permute-done.34.refs_4_
  118.7 4.3 %mixed_back.1 = (bf16[1024,192]{1,0:T(8,128)(2,1)S(1)}, bf16[768,192]{1,0:T(8,128)(2,1)S(1)}) custom-call(s32[10]{0:T(128)S(1)} %dynamic-slice_bitcast_fusion.scal.refs_0_, bf16[256,768]{1,0:T(8,128)(2,1)S(1)} %get-tuple-element.185.refs_1_, bf16[256,768]{1,0:T(8,128)(2,1)S(1)} %collective-permute-done.32.refs_2_, ...), custom_call_target="tpu_custom_call" | custom-call | bytes 9000000 | tf_op jit(solution)/shard_map/mixed_back/pallas_call | solution.py:164
  122.9 12.1 %attend_back.1 = (bf16[1024,576]{1,0:T(8,128)(2,1)S(1)}, f32[256,768]{1,0:T(8,128)}, f32[768,128]{1,0:T(8,128)}, bf16[768,192]{1,0:T(8,128)(2,1)}) custom-call(s32[10]{0:T(128)S(1)} %dynamic-slice_bitcast_fusion.scal.refs_0_, s32[16]{0:T(128)S(1)} %get-tuple-element.137.refs_1_, bf16[1024,192]{1,0:T(8,128)(2,1)} %get-tuple-element.191.refs_2_, ...), custom_call_target="tpu_custom_call" | custom-call | bytes 57600000 | tf_op jit(solution)/shard_map/attend_back/pallas_call | solution.py:164
  135.1 7.7 %query_grads.1 = bf16[832,768]{1,0:T(8,128)(2,1)} custom-call(s32[10]{0:T(128)S(1)} %dynamic-slice_bitcast_fusion.scal.refs_0_, bf16[1024,768]{1,0:T(8,128)(2,1)} %get-tuple-element.189.refs_1_, bf16[1024,768]{1,0:T(8,128)(2,1)} %get-tuple-element.190.refs_2_, bf16[768,192]{1,0:T(8,128)(2,1)} %get-tuple-element.203.refs_3_, ...), custom_call_target="tpu_custom_call" | custom-call | bytes 14400000 | tf_op jit(solution)/shard_map/query_grads/pallas_call | solution.py:164
  142.8 3.9 %all-to-all-done.1.refs_1_ = bf16[8,96,1536]{2,1,0:T(8,128)(2,1)} async-done(((bf16[8,96,1536]{2,1,0:T(8,128)(2,1)}), bf16[8,96,1536]{2,1,0:T(8,128)(2,1)}, u32[]{:S(2)}, u32[]{:S(2)}) %all-to-all-start.1) | async-done | bytes 2359328 | tf_op jit(solution)/shard_map/all_to_all | solution.py:1252
  146.7 3.6 %all-to-all-start = ((bf16[8,104,768]{2,1,0:T(8,128)(2,1)}), bf16[8,104,768]{2,1,0:T(8,128)(2,1)S(1)}, u32[]{:S(2)}, u32[]{:S(2)}) async-start(bf16[8,104,768]{2,1,0:T(8,128)(2,1)} %bitcast.6), calls=%async_computation | async-start | bytes 2555904 | tf_op jit(solution)/shard_map/all_to_all | solution.py:1252
  150.4 3.9 %project_back.1 = (f32[512,768]{1,0:T(8,128)S(1)}, bf16[512,768]{1,0:T(8,128)(2,1)S(1)}) custom-call(s32[10]{0:T(128)S(1)} %dynamic-slice_bitcast_fusion.scal.refs_0_, bf16[1024,576]{1,0:T(8,128)(2,1)S(1)} %get-tuple-element.204.refs_4_.refs_1_, bf16[768,576]{1,0:T(8,128)(2,1)} %get-tuple-element.210.refs_5_.refs_2_), custom_call_target="tpu_custom_call" | custom-call | bytes 10800000 | tf_op jit(solution)/shard_map/project_back/pallas_call | solution.py:164
  154.4 2.5 %owned_sum.1.refs_1_ = bf16[96,1536]{1,0:T(8,128)(2,1)S(1)} custom-call(s32[10]{0:T(128)S(1)} %dynamic-slice_bitcast_fusion.scal.refs_0_, bf16[8,96,1536]{2,1,0:T(8,128)(2,1)} %all-to-all-done.1.refs_1_), custom_call_target="tpu_custom_call" | custom-call | bytes 5400000 | tf_op jit(solution)/shard_map/owned_sum/pallas_call | solution.py:164
  156.9 1.7 collective-permute-start.39
  158.6 0.7 merge.5
  159.8 7.0 %collective-permute-done.39.refs_3_ = bf16[96,1536]{1,0:T(8,128)(2,1)S(1)} collective-permute-done((bf16[96,1536]{1,0:T(8,128)(2,1)S(1)}, bf16[96,1536]{1,0:T(8,128)(2,1)S(1)}, u32[]{:S(2)}, u32[]{:S(2)}) %collective-permute-start.39) | collective-permute-done | bytes 294944 | tf_op jit(solution)/shard_map/ppermute | solution.py:1176
  166.8 1.6 collective-permute-start.35
  168.4 1.6 squares_of.1
  170.0 5.3 %collective-permute-done.37.refs_2_ = bf16[256,768]{1,0:T(8,128)(2,1)} collective-permute-done((bf16[256,768]{1,0:T(8,128)(2,1)S(1)}, bf16[256,768]{1,0:T(8,128)(2,1)}, u32[]{:S(2)}, u32[]{:S(2)}) %collective-permute-start.37) | collective-permute-done | bytes 393248 | tf_op jit(solution)/shard_map/ppermute | solution.py:1176
  175.3 6.0 %all-to-all-done.refs_1_ = bf16[8,104,768]{2,1,0:T(8,128)(2,1)S(1)} async-done(((bf16[8,104,768]{2,1,0:T(8,128)(2,1)}), bf16[8,104,768]{2,1,0:T(8,128)(2,1)S(1)}, u32[]{:S(2)}, u32[]{:S(2)}) %all-to-all-start) | async-done | bytes 1277984 | tf_op jit(solution)/shard_map/all_to_all | solution.py:1252
  181.3 0.7 owned_vector.1.refs_1_.refs_0_
  182.0 1.7 collective-permute-start.42
  183.6 3.7 %collective-permute-done.42.refs_3_.refs_2_ = bf16[104,768]{1,0:T(8,128)(2,1)S(1)} collective-permute-done((bf16[104,768]{1,0:T(8,128)(2,1)S(1)}, bf16[104,768]{1,0:T(8,128)(2,1)S(1)}, u32[]{:S(2)}, u32[]{:S(2)}) %collective-permute-start.42) | collective-permute-done | bytes 159776 | tf_op jit(solution)/shard_map/ppermute | solution.py:1176
  187.3 1.4 collective-permute-done.43.refs_4_.refs_3_
  188.7 1.5 join.1
  190.2 5.3 %all-to-all-start.2 = ((f32[8,8,128]{2,1,0:T(8,128)}), f32[8,8,128]{2,1,0:T(8,128)S(1)}, u32[]{:S(2)}, u32[]{:S(2)}) async-start(f32[8,8,128]{2,1,0:T(8,128)} %bitcast.3), calls=%async_computation.2 | async-start | bytes 65536 | tf_op jit(solution)/shard_map/all_to_all | solution.py:1418
  195.5 2.7 %output_sum.1 = bf16[256,768]{1,0:T(8,128)(2,1)} custom-call(s32[10]{0:T(128)S(1)} %dynamic-slice_bitcast_fusion.scal.refs_0_, f32[256,768]{1,0:T(8,128)S(1)} %get-tuple-element.187.refs_1_, bf16[256,768]{1,0:T(8,128)(2,1)} %collective-permute-done.35.refs_2_, f32[256,768]{1,0:T(8,128)} %get-tuple-element.208.refs_3_, ...), custom_call_target="tpu_custom_call" | custom-call | bytes 2880000 | tf_op jit(solution)/shard_map/output_sum/pallas_call | solution.py:164
  198.2 3.3 %input_back.1 = f32[256,768]{1,0:T(8,128)} custom-call(s32[10]{0:T(128)S(1)} %dynamic-slice_bitcast_fusion.scal.refs_0_, f32[256,768]{1,0:T(8,128)S(1)} %get-tuple-element.213.refs_1_, bf16[256,768]{1,0:T(8,128)(2,1)} %collective-permute-done.37.refs_2_, bf16[256,768]{1,0:T(8,128)(2,1)} %refs_3_.5, f32[256,768]{1,0:T(8,128)} %get-tuple-element.215.refs_4_, ...), custom_call_target="tpu_custom_call" | custom-call | bytes 3600000 | tf_op jit(solution)/shard_map/input_back/pallas_call | solution.py:164
  202.2 12.8 %adam.1 = (f32[96,3072]{1,0:T(8,128)}, f32[96,6144]{1,0:T(8,128)}, f32[12,96]{1,0:T(8,128)}, f32[96,3072]{1,0:T(8,128)}, f32[96,6144]{1,0:T(8,128)}, /*index=5*/...) custom-call(s32[10]{0:T(128)S(1)} %dynamic-slice_bitcast_fusion.scal, ...), custom_call_target="tpu_custom_call" | custom-call | bytes 32400000 | tf_op jit(solution)/shard_map/adam/pallas_call | solution.py:1143
  (66 shorter events, 10.1 us)
Async XLA Ops:
  1.4 13.1 %copy-start.2 = (bf16[256,768]{1,0:T(8,128)(2,1)S(1)}, bf16[256,768]{1,0:T(8,128)(2,1)}, u32[]{:S(2)}) copy-start(bf16[256,768]{1,0:T(8,128)(2,1)} %refs_3_.5) | copy-start | bytes 1179652
  1.4 26.1 %copy-start.1 = (bf16[256,768]{1,0:T(8,128)(2,1)S(1)}, bf16[256,768]{1,0:T(8,128)(2,1)}, u32[]{:S(2)}) copy-start(bf16[256,768]{1,0:T(8,128)(2,1)} %refs_3_.4) | copy-start | bytes 1179652
  1.4 27.6 %copy-start = (f32[96,6144]{1,0:T(8,128)S(1)}, f32[96,6144]{1,0:T(8,128)}, u32[]{:S(2)}) copy-start(f32[96,6144]{1,0:T(8,128)} %refs_12_.1) | copy-start | bytes 7077892
  3.6 7.4 %collective-permute-start.2 = (bf16[96,896]{1,0:T(8,128)(2,1)S(1)}, bf16[96,896]{1,0:T(8,128)(2,1)S(1)}, u32[]{:S(2)}, u32[]{:S(2)}) collective-permute-start(bf16[96,896]{1,0:T(8,128)(2,1)S(1)} %pack_attention.1.refs_3_), channel_id=1, source_target_pairs={{0,4},{8,0},{16,8},{24,16},{28,24},{20,28},{12,20},{4,12},{1,5},{9... | collective-permute-start | bytes 516104 | tf_op jit(solution)/shard_map/ppermute | solution.py:1225
  6.6 5.8 %collective-permute-start.1 = (bf16[96,896]{1,0:T(8,128)(2,1)S(1)}, bf16[96,896]{1,0:T(8,128)(2,1)S(1)}, u32[]{:S(2)}, u32[]{:S(2)}) collective-permute-start(bf16[96,896]{1,0:T(8,128)(2,1)S(1)} %pack_attention.1.refs_3_), channel_id=1, source_target_pairs={{0,8},{8,16},{16,24},{24,28},{28,20},{20,12},{12,4},{4,0},{1,9},{9... | collective-permute-start | bytes 516104 | tf_op jit(solution)/shard_map/ppermute | solution.py:1225
  12.4 5.4 %collective-permute-start.3 = (bf16[96,896]{1,0:T(8,128)(2,1)S(1)}, bf16[96,896]{1,0:T(8,128)(2,1)S(1)}, u32[]{:S(2)}, u32[]{:S(2)}) collective-permute-start(bf16[96,896]{1,0:T(8,128)(2,1)S(1)} %collective-permute-done.1.refs_4_), channel_id=1, source_target_pairs={{0,8},{8,16},{16,24},{24,28},{28,20},{20,12},{12,4},{4,0},{1,9},{9... | collective-permute-start | bytes 516104 | tf_op jit(solution)/shard_map/ppermute | solution.py:1225
  12.9 5.4 %collective-permute-start.4 = (bf16[96,896]{1,0:T(8,128)(2,1)S(1)}, bf16[96,896]{1,0:T(8,128)(2,1)S(1)}, u32[]{:S(2)}, u32[]{:S(2)}) collective-permute-start(bf16[96,896]{1,0:T(8,128)(2,1)S(1)} %collective-permute-done.2.refs_5_), channel_id=1, source_target_pairs={{0,4},{8,0},{16,8},{24,16},{28,24},{20,28},{12,20},{4,12},{1,5},{9... | collective-permute-start | bytes 516104 | tf_op jit(solution)/shard_map/ppermute | solution.py:1225
  14.5 12.5 %collective-permute-start = (bf16[256,768]{1,0:T(8,128)(2,1)S(1)}, bf16[256,768]{1,0:T(8,128)(2,1)S(1)}, u32[]{:S(2)}, u32[]{:S(2)}) collective-permute-start(bf16[256,768]{1,0:T(8,128)(2,1)S(1)} %copy-done.2), channel_id=1, source_target_pairs={{0,2},{1,3},{2,0},{3,1},{4,6},{5,7},{6,4},{7,5},{8,10},{9,11},{10,... | collective-permute-start | bytes 1179656 | tf_op jit(solution)/shard_map/ppermute | solution.py:1176
  18.3 5.4 %collective-permute-start.5 = (bf16[96,896]{1,0:T(8,128)(2,1)S(1)}, bf16[96,896]{1,0:T(8,128)(2,1)S(1)}, u32[]{:S(2)}, u32[]{:S(2)}) collective-permute-start(bf16[96,896]{1,0:T(8,128)(2,1)S(1)} %collective-permute-done.3.refs_6_), channel_id=1, source_target_pairs={{0,8},{8,16},{16,24},{24,28},{28,20},{20,12},{12,4},{4,0},{1,9},{9... | collective-permute-start | bytes 516104 | tf_op jit(solution)/shard_map/ppermute | solution.py:1225
  20.0 5.4 %collective-permute-start.6 = (bf16[96,896]{1,0:T(8,128)(2,1)S(1)}, bf16[96,896]{1,0:T(8,128)(2,1)S(1)}, u32[]{:S(2)}, u32[]{:S(2)}) collective-permute-start(bf16[96,896]{1,0:T(8,128)(2,1)S(1)} %collective-permute-done.4.refs_7_), channel_id=1, source_target_pairs={{0,4},{8,0},{16,8},{24,16},{28,24},{20,28},{12,20},{4,12},{1,5},{9... | collective-permute-start | bytes 516104 | tf_op jit(solution)/shard_map/ppermute | solution.py:1225
  25.4 5.4 %collective-permute-start.9 = (bf16[96,896]{1,0:T(8,128)(2,1)S(1)}, bf16[96,896]{1,0:T(8,128)(2,1)S(1)}, u32[]{:S(2)}, u32[]{:S(2)}) collective-permute-start(bf16[96,896]{1,0:T(8,128)(2,1)S(1)} %collective-permute-done.5.refs_8_), channel_id=1, source_target_pairs={{0,8},{8,16},{16,24},{24,28},{28,20},{20,12},{12,4},{4,0},{1,9},{9... | collective-permute-start | bytes 516104 | tf_op jit(solution)/shard_map/ppermute | solution.py:1225
  26.9 5.9 %collective-permute-start.7 = (bf16[256,768]{1,0:T(8,128)(2,1)S(1)}, bf16[256,768]{1,0:T(8,128)(2,1)S(1)}, u32[]{:S(2)}, u32[]{:S(2)}) collective-permute-start(bf16[256,768]{1,0:T(8,128)(2,1)S(1)} %copy-done.2), channel_id=1, source_target_pairs={{0,1},{1,0},{2,3},{3,2},{4,5},{5,4},{6,7},{7,6},{8,9},{9,8},{10,11... | collective-permute-start | bytes 1179656 | tf_op jit(solution)/shard_map/ppermute | solution.py:1176
  26.9 5.9 %collective-permute-start.8 = (bf16[256,768]{1,0:T(8,128)(2,1)S(1)}, bf16[256,768]{1,0:T(8,128)(2,1)S(1)}, u32[]{:S(2)}, u32[]{:S(2)}) collective-permute-start(bf16[256,768]{1,0:T(8,128)(2,1)S(1)} %collective-permute-done.refs_3_), channel_id=1, source_target_pairs={{0,1},{1,0},{2,3},{3,2},{4,5},{5,4},{6,7},{7,6},{8,9},{9,8},{10,11... | collective-permute-start | bytes 1179656 | tf_op jit(solution)/shard_map/ppermute | solution.py:1176
  27.5 14.3 %collective-permute-start.11 = (bf16[256,768]{1,0:T(8,128)(2,1)S(1)}, bf16[256,768]{1,0:T(8,128)(2,1)S(1)}, u32[]{:S(2)}, u32[]{:S(2)}) collective-permute-start(bf16[256,768]{1,0:T(8,128)(2,1)S(1)} %copy-done.1), channel_id=1, source_target_pairs={{0,2},{1,3},{2,0},{3,1},{4,6},{5,7},{6,4},{7,5},{8,10},{9,11},{10,... | collective-permute-start | bytes 1179656 | tf_op jit(solution)/shard_map/ppermute | solution.py:1176
  29.7 3.8 %copy-start.3 = (s32[1,1024]{1,0:T(1,128)S(1)}, s32[1,1024]{1,0:T(1,128)}, u32[]{:S(2)}) copy-start(s32[1,1024]{1,0:T(1,128)} %refs_6_.1) | copy-start | bytes 12292
  30.8 8.9 %collective-permute-start.22 = (bf16[96,1536]{1,0:T(8,128)(2,1)S(1)}, bf16[96,1536]{1,0:T(8,128)(2,1)S(1)}, u32[]{:S(2)}, u32[]{:S(2)}) collective-permute-start(bf16[96,1536]{1,0:T(8,128)(2,1)S(1)} %pack_forward.1.refs_15_), channel_id=1, source_target_pairs={{0,8},{8,16},{16,24},{24,28},{28,20},{20,12},{12,4},{4,0},{1,9},{9... | collective-permute-start | bytes 884744 | tf_op jit(solution)/shard_map/ppermute | solution.py:1225
  32.3 7.4 %collective-permute-start.23 = (bf16[96,1536]{1,0:T(8,128)(2,1)S(1)}, bf16[96,1536]{1,0:T(8,128)(2,1)S(1)}, u32[]{:S(2)}, u32[]{:S(2)}) collective-permute-start(bf16[96,1536]{1,0:T(8,128)(2,1)S(1)} %pack_forward.1.refs_15_), channel_id=1, source_target_pairs={{0,4},{8,0},{16,8},{24,16},{28,24},{20,28},{12,20},{4,12},{1,5},{9... | collective-permute-start | bytes 884744 | tf_op jit(solution)/shard_map/ppermute | solution.py:1225
  38.0 8.0 %collective-permute-start.10 = (bf16[1152,128]{1,0:T(8,128)(2,1)S(1)}, bf16[1152,128]{1,0:T(8,128)(2,1)S(1)}, u32[]{:S(2)}, u32[]{:S(2)}) collective-permute-start(bf16[1152,128]{1,0:T(8,128)(2,1)S(1)} %get-tuple-element.155.refs_11_), channel_id=1, source_target_pairs={{0,2},{1,3},{2,0},{3,1},{4,6},{5,7},{6,4},{7,5},{8,10},{9,11},{10,... | collective-permute-start | bytes 884744 | tf_op jit(solution)/shard_map/ppermute | solution.py:1176
  39.7 12.4 %collective-permute-start.24 = (bf16[96,1536]{1,0:T(8,128)(2,1)S(1)}, bf16[96,1536]{1,0:T(8,128)(2,1)S(1)}, u32[]{:S(2)}, u32[]{:S(2)}) collective-permute-start(bf16[96,1536]{1,0:T(8,128)(2,1)S(1)} %collective-permute-done.22.refs_16_), channel_id=1, source_target_pairs={{0,8},{8,16},{16,24},{24,28},{28,20},{20,12},{12,4},{4,0},{1,9},{9... | collective-permute-start | bytes 884744 | tf_op jit(solution)/shard_map/ppermute | solution.py:1225
  41.2 10.9 %collective-permute-start.25 = (bf16[96,1536]{1,0:T(8,128)(2,1)S(1)}, bf16[96,1536]{1,0:T(8,128)(2,1)S(1)}, u32[]{:S(2)}, u32[]{:S(2)}) collective-permute-start(bf16[96,1536]{1,0:T(8,128)(2,1)S(1)} %collective-permute-done.23.refs_17_), channel_id=1, source_target_pairs={{0,4},{8,0},{16,8},{24,16},{28,24},{20,28},{12,20},{4,12},{1,5},{9... | collective-permute-start | bytes 884744 | tf_op jit(solution)/shard_map/ppermute | solution.py:1225
  45.1 6.5 %collective-permute-start.12 = (bf16[768,128]{1,0:T(8,128)(2,1)S(1)}, bf16[768,128]{1,0:T(8,128)(2,1)S(1)}, u32[]{:S(2)}, u32[]{:S(2)}) collective-permute-start(bf16[768,128]{1,0:T(8,128)(2,1)S(1)} %get-tuple-element.153.refs_3_), channel_id=1, source_target_pairs={{0,2},{1,3},{2,0},{3,1},{4,6},{5,7},{6,4},{7,5},{8,10},{9,11},{10,... | collective-permute-start | bytes 589832 | tf_op jit(solution)/shard_map/ppermute | solution.py:1176
  51.5 5.7 %collective-permute-start.13 = (bf16[768,128]{1,0:T(8,128)(2,1)S(1)}, bf16[768,128]{1,0:T(8,128)(2,1)S(1)}, u32[]{:S(2)}, u32[]{:S(2)}) collective-permute-start(bf16[768,128]{1,0:T(8,128)(2,1)S(1)} %attend.3.refs_4_), channel_id=1, source_target_pairs={{0,2},{1,3},{2,0},{3,1},{4,6},{5,7},{6,4},{7,5},{8,10},{9,11},{10,... | collective-permute-start | bytes 589832 | tf_op jit(solution)/shard_map/ppermute | solution.py:1176
  52.1 6.7 %collective-permute-start.26 = (bf16[96,1536]{1,0:T(8,128)(2,1)S(1)}, bf16[96,1536]{1,0:T(8,128)(2,1)S(1)}, u32[]{:S(2)}, u32[]{:S(2)}) collective-permute-start(bf16[96,1536]{1,0:T(8,128)(2,1)S(1)} %collective-permute-done.24.refs_18_), channel_id=1, source_target_pairs={{0,8},{8,16},{16,24},{24,28},{28,20},{20,12},{12,4},{4,0},{1,9},{9... | collective-permute-start | bytes 884744 | tf_op jit(solution)/shard_map/ppermute | solution.py:1225
  53.7 7.1 %collective-permute-start.27 = (bf16[96,1536]{1,0:T(8,128)(2,1)S(1)}, bf16[96,1536]{1,0:T(8,128)(2,1)S(1)}, u32[]{:S(2)}, u32[]{:S(2)}) collective-permute-start(bf16[96,1536]{1,0:T(8,128)(2,1)S(1)} %collective-permute-done.25.refs_19_), channel_id=1, source_target_pairs={{0,4},{8,0},{16,8},{24,16},{28,24},{20,28},{12,20},{4,12},{1,5},{9... | collective-permute-start | bytes 884744 | tf_op jit(solution)/shard_map/ppermute | solution.py:1225
  57.2 6.1 %collective-permute-start.14 = (bf16[256,768]{1,0:T(8,128)(2,1)S(1)}, bf16[256,768]{1,0:T(8,128)(2,1)S(1)}, u32[]{:S(2)}, u32[]{:S(2)}) collective-permute-start(bf16[256,768]{1,0:T(8,128)(2,1)S(1)} %copy-done.1), channel_id=1, source_target_pairs={{0,1},{1,0},{2,3},{3,2},{4,5},{5,4},{6,7},{7,6},{8,9},{9,8},{10,11... | collective-permute-start | bytes 1179656 | tf_op jit(solution)/shard_map/ppermute | solution.py:1176
  57.2 6.1 %collective-permute-start.15 = (bf16[256,768]{1,0:T(8,128)(2,1)S(1)}, bf16[256,768]{1,0:T(8,128)(2,1)S(1)}, u32[]{:S(2)}, u32[]{:S(2)}) collective-permute-start(bf16[256,768]{1,0:T(8,128)(2,1)S(1)} %collective-permute-done.11.refs_3_), channel_id=1, source_target_pairs={{0,1},{1,0},{2,3},{3,2},{4,5},{5,4},{6,7},{7,6},{8,9},{9,8},{10,11... | collective-permute-start | bytes 1179656 | tf_op jit(solution)/shard_map/ppermute | solution.py:1176
  57.7 3.1 %collective-permute-start.17 = (bf16[768,128]{1,0:T(8,128)(2,1)S(1)}, bf16[768,128]{1,0:T(8,128)(2,1)S(1)}, u32[]{:S(2)}, u32[]{:S(2)}) collective-permute-start(bf16[768,128]{1,0:T(8,128)(2,1)S(1)} %attend.3.refs_4_), channel_id=1, source_target_pairs={{0,1},{1,0},{2,3},{3,2},{4,5},{5,4},{6,7},{7,6},{8,9},{9,8},{10,11... | collective-permute-start | bytes 589832 | tf_op jit(solution)/shard_map/ppermute | solution.py:1176
  58.8 2.5 %collective-permute-start.16 = (bf16[768,128]{1,0:T(8,128)(2,1)S(1)}, bf16[768,128]{1,0:T(8,128)(2,1)S(1)}, u32[]{:S(2)}, u32[]{:S(2)}) collective-permute-start(bf16[768,128]{1,0:T(8,128)(2,1)S(1)} %get-tuple-element.153.refs_3_), channel_id=1, source_target_pairs={{0,1},{1,0},{2,3},{3,2},{4,5},{5,4},{6,7},{7,6},{8,9},{9,8},{10,11... | collective-permute-start | bytes 589832 | tf_op jit(solution)/shard_map/ppermute | solution.py:1176
  60.8 4.3 %collective-permute-start.20 = (bf16[1152,128]{1,0:T(8,128)(2,1)S(1)}, bf16[1152,128]{1,0:T(8,128)(2,1)S(1)}, u32[]{:S(2)}, u32[]{:S(2)}) collective-permute-start(bf16[1152,128]{1,0:T(8,128)(2,1)S(1)} %get-tuple-element.155.refs_11_), channel_id=1, source_target_pairs={{0,1},{1,0},{2,3},{3,2},{4,5},{5,4},{6,7},{7,6},{8,9},{9,8},{10,11... | collective-permute-start | bytes 884744 | tf_op jit(solution)/shard_map/ppermute | solution.py:1176
  60.8 4.3 %collective-permute-start.21 = (bf16[1152,128]{1,0:T(8,128)(2,1)S(1)}, bf16[1152,128]{1,0:T(8,128)(2,1)S(1)}, u32[]{:S(2)}, u32[]{:S(2)}) collective-permute-start(bf16[1152,128]{1,0:T(8,128)(2,1)S(1)} %collective-permute-done.10.refs_13_), channel_id=1, source_target_pairs={{0,1},{1,0},{2,3},{3,2},{4,5},{5,4},{6,7},{7,6},{8,9},{9,8},{10,11... | collective-permute-start | bytes 884744 | tf_op jit(solution)/shard_map/ppermute | solution.py:1176
  61.3 9.0 %collective-permute-start.28 = (bf16[96,1536]{1,0:T(8,128)(2,1)S(1)}, bf16[96,1536]{1,0:T(8,128)(2,1)S(1)}, u32[]{:S(2)}, u32[]{:S(2)}) collective-permute-start(bf16[96,1536]{1,0:T(8,128)(2,1)S(1)} %collective-permute-done.26.refs_20_), channel_id=1, source_target_pairs={{0,8},{8,16},{16,24},{24,28},{28,20},{20,12},{12,4},{4,0},{1,9},{9... | collective-permute-start | bytes 884744 | tf_op jit(solution)/shard_map/ppermute | solution.py:1225
  63.3 1.4 collective-permute-start.18
  63.3 1.7 collective-permute-start.19
  81.5 5.2 %collective-permute-start.29 = (bf16[512,768]{1,0:T(8,128)(2,1)S(1)}, bf16[512,768]{1,0:T(8,128)(2,1)S(1)}, u32[]{:S(2)}, u32[]{:S(2)}) collective-permute-start(bf16[512,768]{1,0:T(8,128)(2,1)S(1)} %get-tuple-element.176), channel_id=1, source_target_pairs={{0,1},{1,0},{2,3},{3,2},{4,5},{5,4},{6,7},{7,6},{8,9},{9,8},{10,11... | collective-permute-start | bytes 2359304 | tf_op jit(solution)/shard_map/ppermute | solution.py:1176
  86.7 60.0 %all-to-all-start.1 = ((bf16[8,96,1536]{2,1,0:T(8,128)(2,1)}), bf16[8,96,1536]{2,1,0:T(8,128)(2,1)}, u32[]{:S(2)}, u32[]{:S(2)}) async-start(bf16[8,96,1536]{2,1,0:T(8,128)(2,1)} %bitcast.2), calls=%async_computation.1 | async-start | bytes 4718592 | tf_op jit(solution)/shard_map/all_to_all | solution.py:1252
  92.8 11.3 %collective-permute-start.30 = (bf16[256,768]{1,0:T(8,128)(2,1)S(1)}, bf16[256,768]{1,0:T(8,128)(2,1)S(1)}, u32[]{:S(2)}, u32[]{:S(2)}) collective-permute-start(bf16[256,768]{1,0:T(8,128)(2,1)S(1)} %get-tuple-element.178), channel_id=1, source_target_pairs={{0,2},{1,3},{2,0},{3,1},{4,6},{5,7},{6,4},{7,5},{8,10},{9,11},{10,... | collective-permute-start | bytes 1179656 | tf_op jit(solution)/shard_map/ppermute | solution.py:1176
  105.3 3.6 %collective-permute-start.31 = (bf16[512,768]{1,0:T(8,128)(2,1)S(1)}, bf16[512,768]{1,0:T(8,128)(2,1)S(1)}, u32[]{:S(2)}, u32[]{:S(2)}) collective-permute-start(bf16[512,768]{1,0:T(8,128)(2,1)S(1)} %get-tuple-element.186), channel_id=1, source_target_pairs={{0,1},{1,0},{2,3},{3,2},{4,5},{5,4},{6,7},{7,6},{8,9},{9,8},{10,11... | collective-permute-start | bytes 2359304 | tf_op jit(solution)/shard_map/ppermute | solution.py:1176
  105.4 11.5 %collective-permute-start.33 = (bf16[256,768]{1,0:T(8,128)(2,1)S(1)}, bf16[256,768]{1,0:T(8,128)(2,1)S(1)}, u32[]{:S(2)}, u32[]{:S(2)}) collective-permute-start(bf16[256,768]{1,0:T(8,128)(2,1)S(1)} %get-tuple-element.185.refs_1_), channel_id=1, source_target_pairs={{0,2},{1,3},{2,0},{3,1},{4,6},{5,7},{6,4},{7,5},{8,10},{9,11},{10,... | collective-permute-start | bytes 1179656 | tf_op jit(solution)/shard_map/ppermute | solution.py:1176
  107.1 9.9 %collective-permute-start.32 = (bf16[256,768]{1,0:T(8,128)(2,1)S(1)}, bf16[256,768]{1,0:T(8,128)(2,1)S(1)}, u32[]{:S(2)}, u32[]{:S(2)}) collective-permute-start(bf16[256,768]{1,0:T(8,128)(2,1)S(1)} %get-tuple-element.185.refs_1_), channel_id=1, source_target_pairs={{0,1},{1,0},{2,3},{3,2},{4,5},{5,4},{6,7},{7,6},{8,9},{9,8},{10,11... | collective-permute-start | bytes 1179656 | tf_op jit(solution)/shard_map/ppermute | solution.py:1176
  116.9 1.7 collective-permute-start.34
  146.7 34.5 %all-to-all-start = ((bf16[8,104,768]{2,1,0:T(8,128)(2,1)}), bf16[8,104,768]{2,1,0:T(8,128)(2,1)S(1)}, u32[]{:S(2)}, u32[]{:S(2)}) async-start(bf16[8,104,768]{2,1,0:T(8,128)(2,1)} %bitcast.6), calls=%async_computation | async-start | bytes 2555904 | tf_op jit(solution)/shard_map/all_to_all | solution.py:1252
  154.3 4.3 %collective-permute-start.36 = (bf16[512,768]{1,0:T(8,128)(2,1)S(1)}, bf16[512,768]{1,0:T(8,128)(2,1)S(1)}, u32[]{:S(2)}, u32[]{:S(2)}) collective-permute-start(bf16[512,768]{1,0:T(8,128)(2,1)S(1)} %get-tuple-element.212), channel_id=1, source_target_pairs={{0,1},{1,0},{2,3},{3,2},{4,5},{5,4},{6,7},{7,6},{8,9},{9,8},{10,11... | collective-permute-start | bytes 2359304 | tf_op jit(solution)/shard_map/ppermute | solution.py:1176
  156.9 9.9 %collective-permute-start.39 = (bf16[96,1536]{1,0:T(8,128)(2,1)S(1)}, bf16[96,1536]{1,0:T(8,128)(2,1)S(1)}, u32[]{:S(2)}, u32[]{:S(2)}) collective-permute-start(bf16[96,1536]{1,0:T(8,128)(2,1)S(1)} %owned_sum.1.refs_1_), channel_id=1, source_target_pairs={{0,2},{1,3},{2,0},{3,1},{4,6},{5,7},{6,4},{7,5},{8,10},{9,11},{10,... | collective-permute-start | bytes 884744 | tf_op jit(solution)/shard_map/ppermute | solution.py:1176
  159.3 16.0 %collective-permute-start.37 = (bf16[256,768]{1,0:T(8,128)(2,1)S(1)}, bf16[256,768]{1,0:T(8,128)(2,1)}, u32[]{:S(2)}, u32[]{:S(2)}) collective-permute-start(bf16[256,768]{1,0:T(8,128)(2,1)S(1)} %get-tuple-element.214), channel_id=1, source_target_pairs={{0,2},{1,3},{2,0},{3,1},{4,6},{5,7},{6,4},{7,5},{8,10},{9,11},{10,... | collective-permute-start | bytes 1179656 | tf_op jit(solution)/shard_map/ppermute | solution.py:1176
  159.8 8.6 %collective-permute-start.38 = (bf16[96,1536]{1,0:T(8,128)(2,1)S(1)}, bf16[96,1536]{1,0:T(8,128)(2,1)S(1)}, u32[]{:S(2)}, u32[]{:S(2)}) collective-permute-start(bf16[96,1536]{1,0:T(8,128)(2,1)S(1)} %owned_sum.1.refs_1_), channel_id=1, source_target_pairs={{0,1},{1,0},{2,3},{3,2},{4,5},{5,4},{6,7},{7,6},{8,9},{9,8},{10,11... | collective-permute-start | bytes 884744 | tf_op jit(solution)/shard_map/ppermute | solution.py:1176
  166.8 1.6 collective-permute-start.40
  166.8 28.7 %collective-permute-start.35 = (bf16[256,768]{1,0:T(8,128)(2,1)}, bf16[256,768]{1,0:T(8,128)(2,1)}, u32[]{:S(2)}, u32[]{:S(2)}) collective-permute-start(bf16[256,768]{1,0:T(8,128)(2,1)} %get-tuple-element.207), channel_id=1, source_target_pairs={{0,2},{1,3},{2,0},{3,1},{4,6},{5,7},{6,4},{7,5},{8,10},{9,11},{10,... | collective-permute-start | bytes 1179656 | tf_op jit(solution)/shard_map/ppermute | solution.py:1176
  182.0 5.3 %collective-permute-start.42 = (bf16[104,768]{1,0:T(8,128)(2,1)S(1)}, bf16[104,768]{1,0:T(8,128)(2,1)S(1)}, u32[]{:S(2)}, u32[]{:S(2)}) collective-permute-start(bf16[104,768]{1,0:T(8,128)(2,1)S(1)} %owned_vector.1.refs_1_.refs_0_), channel_id=1, source_target_pairs={{0,2},{1,3},{2,0},{3,1},{4,6},{5,7},{6,4},{7,5},{8,10},{9,11},{10,... | collective-permute-start | bytes 479240 | tf_op jit(solution)/shard_map/ppermute | solution.py:1176
  183.6 3.7 %collective-permute-start.41 = (bf16[104,768]{1,0:T(8,128)(2,1)S(1)}, bf16[104,768]{1,0:T(8,128)(2,1)S(1)}, u32[]{:S(2)}, u32[]{:S(2)}) collective-permute-start(bf16[104,768]{1,0:T(8,128)(2,1)S(1)} %owned_vector.1.refs_1_.refs_0_), channel_id=1, source_target_pairs={{0,1},{1,0},{2,3},{3,2},{4,5},{5,4},{6,7},{7,6},{8,9},{9,8},{10,11... | collective-permute-start | bytes 479240 | tf_op jit(solution)/shard_map/ppermute | solution.py:1176
  187.3 1.4 collective-permute-start.43
  190.2 12.0 %all-to-all-start.2 = ((f32[8,8,128]{2,1,0:T(8,128)}), f32[8,8,128]{2,1,0:T(8,128)S(1)}, u32[]{:S(2)}, u32[]{:S(2)}) async-start(f32[8,8,128]{2,1,0:T(8,128)} %bitcast.3), calls=%async_computation.2 | async-start | bytes 65536 | tf_op jit(solution)/shard_map/all_to_all | solution.py:1418

commit v3 on v2

--- a/solution.py
+++ b/solution.py
@@ -280,13 +280,25 @@
     return rows + rows * (columns - 128) // 128
 
 
-def project_kernel(count, cols, scal, seg_ref, x_ref, *refs):
+def segments_kernel(scal, seg_ref, col_ref, ranges_ref):
+    numbers = seg_ref[...]
+    key_ranges(numbers, ranges_ref)
+    lines = jnp.broadcast_to(numbers.astype(F32), (8, numbers.shape[1])).astype(BF)
+    col_ref[...] = dot_rows(lines, unit_rows(8, 128))[:, 0:1].astype(jnp.int32)
+
+
+def read_segments(scal, segments):
+    outputs = (shaped((segments.shape[1], 1), jnp.int32), shaped((16,), jnp.int32))
+    inputs = (scal, segments)
+    return run(
+        segments_kernel, "read_segments", outputs, inputs, 1.0, mebibytes=4, scalar_outputs=(1,)
+    )
+
+
+def project_kernel(count, cols, scal, x_ref, *refs):
     pieces = refs[:count]
-    q_ref, k_ref, v_ref, w_ref, wo_ref, vec_ref, col_ref, a_ref, hat_ref, ranges_ref = refs[
-        count : 10 + count
-    ]
-    weights, wq_ref, wk_ref, wv_ref = refs[10 + count : 14 + count]
-    key_ranges(seg_ref[...], ranges_ref)
+    q_ref, k_ref, v_ref, w_ref, wo_ref, vec_ref, a_ref, hat_ref = refs[count : 8 + count]
+    weights, wq_ref, wk_ref, wv_ref = refs[8 + count : 12 + count]
     place_rows(scal, pieces, weights)
     for i, ref in enumerate((wq_ref, wk_ref, wv_ref)):
         ref[...] = weights[:, i * cols : (i + 1) * cols]
@@ -300,8 +312,6 @@
     own = dot_cols(unit, weights[pl.ds(start, cols), 4 * cols :])
     query_bias, value_bias = own[2:3, :], own[3:4, :]
     gain, shift = vec_ref[0:1, :], vec_ref[1:2, :]
-    numbers = jnp.broadcast_to(seg_ref[...].astype(F32), (8, seg_ref.shape[1])).astype(BF)
-    col_ref[...] = dot_rows(numbers, unit_rows(8, 128))[:, 0:1].astype(jnp.int32)
     block = 256
 
     def step(i, carry):
@@ -318,23 +328,21 @@
     lax.fori_loop(0, x_ref.shape[0] // block, step, 0)
 
 
-def project(scal, segments, x_all, pieces, cols):
+def project(scal, x_all, pieces, cols):
     length, width = x_all.shape
     outputs = (
         (shaped((length, cols), BF),) * 3
         + (shaped((width, 3 * cols), BF),)
         + (shaped((folded_rows(width, cols), 128), BF),)
-        + (shaped((16, width), F32), shaped((length, 1), jnp.int32))
+        + (shaped((16, width), F32),)
         + (shaped((length, width), BF),) * 2
-        + (shaped((16,), jnp.int32),)
     )
     return run(
         functools.partial(project_kernel, len(pieces), cols),
         "project",
         outputs,
-        (scal, segments, x_all, *pieces),
+        (scal, x_all, *pieces),
         4.5,
-        scalar_outputs=(9,),
         scratch=[pltpu.VMEM((width, 4 * cols + 128), BF)] + [pltpu.VMEM((width, cols), BF)] * 3,
     )
 
@@ -1288,8 +1296,13 @@
     place = lax.axis_index("dp") * groups + lax.axis_index("head")
     scal = lax.dynamic_index_in_dim(jnp.asarray(table), place, 0, keepdims=False)
     first = Ring(pack_attention(scal, attention_master, vector_master, cols), owners)
-    first.rest()
     ringed = owners == len(RING)
+    first.hop()
+    if ringed:
+        first.hop()
+    seg_col, ranges = read_segments(scal, after(segments, *first.pieces[-2:]))
+    if ringed:
+        first.hop().hop(seg_col)
     early = first.pieces[-3:-1] if ringed else first.pieces
     token_across, grad_across = swap(tokens, 2), swap(cotangent, 2)
     token, token_across = lax.optimization_barrier((tokens, token_across, *early))[:2]
@@ -1297,11 +1310,9 @@
     second = Ring(pack_forward(scal, feedforward_master, part), owners)
     second.hop(first.pieces[-1])
 
-    queries, keys, values, w_qkv, w_o, vec, seg_col, normed, hat, ranges = project(
-        scal, segments, x_all, first.pieces, cols
-    )
-    if ringed:
-        second.hop(queries)
+    queries, keys, values, w_qkv, w_o, vec, normed, hat = project(
+        scal, x_all, first.pieces, cols
+    )
     half = x_all.shape[0] // 2
     w_across = swap(w_o, 2)
     mixed_low, *kept = attend(
@@ -1320,12 +1331,14 @@
     far_q, far_k, far_v, far_col, far_weights, far_vec, *far_normed = kept
     low_across = swap(mixed_low, 2)
     w_across = after(w_across, mixed_low)
+    if ringed:
+        second.hop(mixed_low)
     mixed_high = attend(
         scal, ranges, after(queries, w_across), keys, values, segments, seg_col, per, half, half
     )
     if ringed:
         second.hop(mixed_high)
-    high_across = swap(after(mixed_high, low_across), 2)
+    high_across = swap(mixed_high, 2)
     w_across, low_across, w_o, mixed_low, grad, grad_across = lax.optimization_barrier(
         (w_across, low_across, w_o, mixed_low, cotangent, grad_across, high_across)
     )[:6]
@@ -1389,10 +1402,10 @@
         per,
         (grad_resid, table, grad_out),
     )
-    send_branch = send
+    got_branch = swap(after(send, grad_mixed), 2)
     pack = query_grads(
         scal,
-        far_normed[0],
+        after(far_normed[0], got_branch),
         far_normed[1],
         far_grad_out,
         grad_qkv,
@@ -1406,10 +1419,9 @@
     forward_squares, *forward_parts = squares_of(scal, forward_parts)
     keep, send = project_back(scal, grad_qkv, after(far_weights, pack))
     mine_input, send = merge(scal, keep, swap(send, 1))
-    got_branch = swap(after(send_branch, pack), 2)
-    block_output = output_sum(scal, mine, got_branch, far_resid, far_vec)
+    block_output = output_sum(scal, after(mine, pack), got_branch, far_resid, far_vec)
     got_input = swap(send, 2)
-    owned_pack = after(owned_pack, forward_squares, got_input)
+    owned_pack = after(owned_pack, forward_squares, got_input, block_output)
     input_gradient = input_back(scal, mine_input, got_input, tokens, far_dh, far_vec)
     attention_parts = spread(owned_vector(scal, owned_pack, cols, ringed))
     squares = join(

time: 216 us -> 214 us (level)
  starting transfers between devices: 48.6 us -> 43.2 us
  waiting for transfers between devices: 66.8 us -> 69.8 us
    ppermute x30, starting transfers between devices: 17.3 us -> 14.4 us  [swap(): return lax.ppermute(part, 'head', [(i, i ^ bit) for i in range(4)])]
    all_to_all x1, waiting for transfers between devices: 0.63 us -> 3.33 us  [local(): lax.all_to_all(squares.reshape(owners, 8, 128), 'dp', split_axis=0, conca...]
    pallas_call x23 -> x24, Pallas kernels: 82.2 us -> 82.7 us  [run(): pl.pallas_call(body, out_shape=shapes + [pltpu.HBM(inputs[i].shape, input...]
where the time goes in v3:
time: 214 us
  Pallas kernels  98.5 us (46%)
  waiting for transfers between devices  69.8 us (33%)
  starting transfers between devices  43.2 us (20%)
    pallas_call x24, Pallas kernels, run(): pl.pallas_call(body, out_shape=shapes + [pltpu.HBM(inputs[i].shape, input...  82.7 us
    ppermute x30, waiting for transfers between devices, swap(): return lax.ppermute(part, 'head', [(i, i ^ bit) for i in range(4)])  34.8 us
    ppermute x14, waiting for transfers between devices, send(): return lax.ppermute(array, 'dp', pairs)  22.1 us
    ppermute x14, starting transfers between devices, send(): return lax.ppermute(array, 'dp', pairs)  16.4 us
    ppermute x30, starting transfers between devices, swap(): return lax.ppermute(part, 'head', [(i, i ^ bit) for i in range(4)])  14.4 us
    pallas_call x1, Pallas kernels, adam(): pl.pallas_call(functools.partial(adam_kernel, counts, cols, ringed), out_...  12.8 us
    all_to_all x2, waiting for transfers between devices, exchange_owned(): return lax.all_to_all(blocks, 'dp', split_axis=0, concat_axis=0)  9.55 us
    all_to_all x2, starting transfers between devices, exchange_owned(): return lax.all_to_all(blocks, 'dp', split_axis=0, concat_axis=0)  8 us
  transfers between devices with their start and end apart: 47, of which 25 were waited for; matrix products, arithmetic and copies ran while one was open for 0% of the time, Pallas kernels for 33%

profile of v3, /device:TPU:0, one launch (start us, length us, event | category | flops | bytes accessed | tf_op | source)
XLA Modules:
  0.0 213.7 jit_solution(771096547437522273)
XLA Ops:
  0.7 0.7 dynamic-slice_bitcast_fusion.scal.refs_0_
  1.4 2.3 %pack_attention.1.refs_2_ = bf16[96,896]{1,0:T(8,128)(2,1)S(1)} custom-call(s32[10]{0:T(128)S(1)} %dynamic-slice_bitcast_fusion.scal.refs_0_, f32[96,3072]{1,0:T(8,128)} %refs_8_.1, f32[96,3072]{1,0:T(8,128)} %refs_8_.1, f32[96,3072]{1,0:T(8,128)} %refs_8_.1, f32[96,3072]{1,0:T(8,128)} %refs_8_.1, f32[12,96]{1,0:T(8,128)} %refs_16_.1), custom_call_target="tpu_custom_call" | custom-call | bytes 5400000 | tf_op jit(solution)/shard_map/pack_attention/pallas_call | solution.py:206
  3.6 3.0 %collective-permute-start.2 = (bf16[96,896]{1,0:T(8,128)(2,1)S(1)}, bf16[96,896]{1,0:T(8,128)(2,1)S(1)}, u32[]{:S(2)}, u32[]{:S(2)}) collective-permute-start(bf16[96,896]{1,0:T(8,128)(2,1)S(1)} %pack_attention.1.refs_2_), channel_id=1, source_target_pairs={{0,4},{8,0},{16,8},{24,16},{28,24},{20,28},{12,20},{4,12},{1,5},{9... | collective-permute-start | bytes 516104 | tf_op jit(solution)/shard_map/ppermute | solution.py:1233
  6.8 4.3 %collective-permute-done.2.refs_4_ = bf16[96,896]{1,0:T(8,128)(2,1)S(1)} collective-permute-done((bf16[96,896]{1,0:T(8,128)(2,1)S(1)}, bf16[96,896]{1,0:T(8,128)(2,1)S(1)}, u32[]{:S(2)}, u32[]{:S(2)}) %collective-permute-start.2) | collective-permute-done | bytes 172064 | tf_op jit(solution)/shard_map/ppermute | solution.py:1233
  11.1 1.4 collective-permute-done.1.refs_3_
  12.9 1.6 collective-permute-start.4
  14.5 1.5 collective-permute-start
  16.0 1.9 collective-permute-done.3.refs_5_
  18.3 1.7 collective-permute-start.5
  20.3 1.9 read_segments.1
  22.2 1.5 collective-permute-done.5.refs_7_
  23.7 1.7 collective-permute-done.6.refs_8_
  25.4 1.6 collective-permute-start.9
  27.5 1.5 collective-permute-start.11
  29.0 0.7 pack_forward.1.refs_15_
  29.7 1.1 collective-permute-done.9.refs_9_
  30.8 1.6 collective-permute-start.22
  33.5 3.9 %project.1 = (bf16[1024,192]{1,0:T(8,128)(2,1)S(1)}, bf16[1024,192]{1,0:T(8,128)(2,1)S(1)}, bf16[1024,192]{1,0:T(8,128)(2,1)S(1)}, bf16[768,576]{1,0:T(8,128)(2,...) custom-call(s32[10]{0:T(128)S(1)} %dynamic-slice_bitcast_fusion.scal, ...), custom_call_target="tpu_custom_call" | custom-call | bytes 16200000 | tf_op jit(solution)/shard_map/project/pallas_call | solution.py:164
  37.4 1.1 collective-permute-done.11.refs_3_
  38.5 1.5 collective-permute-start.10
  40.0 3.3 %attend.2 = (bf16[768,128]{1,0:T(8,128)(2,1)S(1)}, bf16[1024,192]{1,0:T(8,128)(2,1)}, bf16[1024,192]{1,0:T(8,128)(2,1)}, bf16[1024,192]{1,0:T(8,128)(2,1)}, s32[...) custom-call(s32[10]{0:T(128)S(1)} %dynamic-slice_bitcast_fusion.scal, ...), custom_call_target="tpu_custom_call" | custom-call | bytes 12600000 | tf_op jit(solution)/shard_map/attend/pallas_call | solution.py:164
  43.4 1.6 collective-permute-start.24
  45.9 0.8 collective-permute-done.10.refs_13_
  46.8 3.1 %attend.3.refs_4_ = bf16[768,128]{1,0:T(8,128)(2,1)S(1)} custom-call(s32[10]{0:T(128)S(1)} %dynamic-slice_bitcast_fusion.scal.refs_0_, s32[16]{0:T(128)S(1)} %get-tuple-element.141.refs_1_, bf16[1024,192]{1,0:T(8,128)(2,1)S(1)} %get-tuple-element.152.refs_2_, bf16[1024,192]{1,0:T(8,128)(2,1)S(1)} %get-tuple-element.144.refs_3_, ...), custom_call_target="tpu_custom_call" | custom-call | bytes 12600000 | tf_op jit(solution)/shard_map/attend/pallas_call | solution.py:164
  49.9 2.5 %collective-permute-start.13 = (bf16[768,128]{1,0:T(8,128)(2,1)S(1)}, bf16[768,128]{1,0:T(8,128)(2,1)S(1)}, u32[]{:S(2)}, u32[]{:S(2)}) collective-permute-start(bf16[768,128]{1,0:T(8,128)(2,1)S(1)} %attend.3.refs_4_), channel_id=1, source_target_pairs={{0,2},{1,3},{2,0},{3,1},{4,6},{5,7},{6,4},{7,5},{8,10},{9,11},{10,... | collective-permute-start | bytes 589832 | tf_op jit(solution)/shard_map/ppermute | solution.py:1184
  52.5 1.5 collective-permute-start.26
  54.5 1.6 collective-permute-done.13.refs_8_
  56.6 2.6 %collective-permute-done.26.refs_20_ = bf16[96,1536]{1,0:T(8,128)(2,1)S(1)} collective-permute-done((bf16[96,1536]{1,0:T(8,128)(2,1)S(1)}, bf16[96,1536]{1,0:T(8,128)(2,1)S(1)}, u32[]{:S(2)}, u32[]{:S(2)}) %collective-permute-start.26) | collective-permute-done | bytes 294944 | tf_op jit(solution)/shard_map/ppermute | solution.py:1233
  59.2 1.5 collective-permute-done.27.refs_21_
  61.3 1.5 collective-permute-start.28
  64.5 5.7 %collective-permute-done.28.refs_22_ = bf16[96,1536]{1,0:T(8,128)(2,1)S(1)} collective-permute-done((bf16[96,1536]{1,0:T(8,128)(2,1)S(1)}, bf16[96,1536]{1,0:T(8,128)(2,1)S(1)}, u32[]{:S(2)}, u32[]{:S(2)}) %collective-permute-start.28) | collective-permute-done | bytes 294944 | tf_op jit(solution)/shard_map/ppermute | solution.py:1233
  70.2 11.2 %forward_back.1 = (bf16[1024,768]{1,0:T(8,128)(2,1)S(1)}, bf16[1024,768]{1,0:T(8,128)(2,1)S(1)}, bf16[1024,768]{1,0:T(8,128)(2,1)S(1)}, f32[512,768]{1,0:T(8,128...) custom-call(s32[10]{0:T(128)S(1)} %dynamic-slice_bitcast_fusion.scal, ...), custom_call_target="tpu_custom_call" | custom-call | bytes 46800000 | tf_op jit(solution)/shard_map/forward_back/pallas_call | solution.py:164
  81.5 5.1 %forward_grads.1 = (bf16[768,1536]{1,0:T(8,128)(2,1)}, bf16[1024,768]{1,0:T(8,128)(2,1)}, f32[256,768]{1,0:T(8,128)}, f32[8,768]{1,0:T(8,128)}, bf16[192,768]{1,...) custom-call(s32[10]{0:T(128)S(1)} %dynamic-slice_bitcast_fusion.scal.refs_0_, ...), custom_call_target="tpu_custom_call" | custom-call | bytes 14400000 | tf_op jit(solution)/shard_map/forward_grads/pallas_call | solution.py:164
  86.7 4.4 %all-to-all-start.1 = ((bf16[8,96,1536]{2,1,0:T(8,128)(2,1)}), bf16[8,96,1536]{2,1,0:T(8,128)(2,1)}, u32[]{:S(2)}, u32[]{:S(2)}) async-start(bf16[8,96,1536]{2,1,0:T(8,128)(2,1)} %bitcast.2), calls=%async_computation.1 | async-start | bytes 4718592 | tf_op jit(solution)/shard_map/all_to_all | solution.py:1260
  91.1 0.7 merge.3
  92.3 6.1 %branch_part.1 = (f32[512,768]{1,0:T(8,128)}, bf16[512,768]{1,0:T(8,128)(2,1)S(1)}, bf16[256,768]{1,0:T(8,128)(2,1)S(1)}) custom-call(s32[10]{0:T(128)S(1)} %dynamic-slice_bitcast_fusion.scal.refs_0_, bf16[1024,768]{1,0:T(8,128)(2,1)} %get-tuple-element.174.refs_1_, bf16[768,1536]{1,0:T(8,128)(2,1)} %get-tuple-element.181.refs_2_, bf16[256,768]{1,0:T(8,128)(2,1)} %refs_3_.4), custom_call_target="tpu_custom_call" | custom-call | bytes 10800000 | tf_op jit(solution)/shard_map/branch_part/pallas_call | solution.py:164
  98.4 4.9 %collective-permute-done.30.refs_2_ = bf16[256,768]{1,0:T(8,128)(2,1)S(1)} collective-permute-done((bf16[256,768]{1,0:T(8,128)(2,1)S(1)}, bf16[256,768]{1,0:T(8,128)(2,1)S(1)}, u32[]{:S(2)}, u32[]{:S(2)}) %collective-permute-start.30) | collective-permute-done | bytes 393248 | tf_op jit(solution)/shard_map/ppermute | solution.py:1184
  103.3 1.2 resid_back.1
  105.3 1.7 vector_table.1.refs_9_
  107.0 2.1 %merge.4 = (f32[256,768]{1,0:T(8,128)S(1)}, bf16[256,768]{1,0:T(8,128)(2,1)S(1)}) custom-call(s32[10]{0:T(128)S(1)} %dynamic-slice_bitcast_fusion.scal.refs_0_, f32[512,768]{1,0:T(8,128)} %get-tuple-element.182.refs_1_, bf16[512,768]{1,0:T(8,128)(2,1)S(1)} %collective-permute-done.31.refs_2_), custom_call_target="tpu_custom_call" | custom-call | bytes 2520000 | tf_op jit(solution)/shard_map/merge/pallas_call | solution.py:164
  109.2 7.0 %collective-permute-done.33.refs_3_ = bf16[256,768]{1,0:T(8,128)(2,1)S(1)} collective-permute-done((bf16[256,768]{1,0:T(8,128)(2,1)S(1)}, bf16[256,768]{1,0:T(8,128)(2,1)S(1)}, u32[]{:S(2)}, u32[]{:S(2)}) %collective-permute-start.33) | collective-permute-done | bytes 393248 | tf_op jit(solution)/shard_map/ppermute | solution.py:1184
  116.2 1.7 collective-permute-done.34.refs_4_
  117.9 4.3 %mixed_back.1 = (bf16[1024,192]{1,0:T(8,128)(2,1)S(1)}, bf16[768,192]{1,0:T(8,128)(2,1)S(1)}) custom-call(s32[10]{0:T(128)S(1)} %dynamic-slice_bitcast_fusion.scal.refs_0_, bf16[256,768]{1,0:T(8,128)(2,1)S(1)} %get-tuple-element.187.refs_1_, bf16[256,768]{1,0:T(8,128)(2,1)S(1)} %collective-permute-done.32.refs_2_, ...), custom_call_target="tpu_custom_call" | custom-call | bytes 9000000 | tf_op jit(solution)/shard_map/mixed_back/pallas_call | solution.py:164
  122.7 12.2 %attend_back.1 = (bf16[1024,576]{1,0:T(8,128)(2,1)S(1)}, f32[256,768]{1,0:T(8,128)}, f32[768,128]{1,0:T(8,128)}, bf16[768,192]{1,0:T(8,128)(2,1)}) custom-call(s32[10]{0:T(128)S(1)} %dynamic-slice_bitcast_fusion.scal.refs_0_, s32[16]{0:T(128)S(1)} %get-tuple-element.141.refs_1_, bf16[1024,192]{1,0:T(8,128)(2,1)} %get-tuple-element.201.refs_2_, ...), custom_call_target="tpu_custom_call" | custom-call | bytes 57600000 | tf_op jit(solution)/shard_map/attend_back/pallas_call | solution.py:164
  134.9 7.8 %query_grads.1 = bf16[832,768]{1,0:T(8,128)(2,1)} custom-call(s32[10]{0:T(128)S(1)} %dynamic-slice_bitcast_fusion.scal.refs_0_, bf16[1024,768]{1,0:T(8,128)(2,1)} %get-tuple-element.199.refs_1_, bf16[1024,768]{1,0:T(8,128)(2,1)} %get-tuple-element.200.refs_2_, bf16[768,192]{1,0:T(8,128)(2,1)} %get-tuple-element.207.refs_3_, ...), custom_call_target="tpu_custom_call" | custom-call | bytes 14400000 | tf_op jit(solution)/shard_map/query_grads/pallas_call | solution.py:164
  142.7 3.2 %all-to-all-done.1.refs_1_ = bf16[8,96,1536]{2,1,0:T(8,128)(2,1)} async-done(((bf16[8,96,1536]{2,1,0:T(8,128)(2,1)}), bf16[8,96,1536]{2,1,0:T(8,128)(2,1)}, u32[]{:S(2)}, u32[]{:S(2)}) %all-to-all-start.1) | async-done | bytes 2359328 | tf_op jit(solution)/shard_map/all_to_all | solution.py:1260
  145.9 3.6 %all-to-all-start = ((bf16[8,104,768]{2,1,0:T(8,128)(2,1)}), bf16[8,104,768]{2,1,0:T(8,128)(2,1)S(1)}, u32[]{:S(2)}, u32[]{:S(2)}) async-start(bf16[8,104,768]{2,1,0:T(8,128)(2,1)} %bitcast.6), calls=%async_computation | async-start | bytes 2555904 | tf_op jit(solution)/shard_map/all_to_all | solution.py:1260
  149.5 3.9 %project_back.1 = (f32[512,768]{1,0:T(8,128)S(1)}, bf16[512,768]{1,0:T(8,128)(2,1)S(1)}) custom-call(s32[10]{0:T(128)S(1)} %dynamic-slice_bitcast_fusion.scal.refs_0_, bf16[1024,576]{1,0:T(8,128)(2,1)S(1)} %get-tuple-element.208.refs_4_.refs_1_, bf16[768,576]{1,0:T(8,128)(2,1)} %get-tuple-element.214.refs_5_.refs_2_), custom_call_target="tpu_custom_call" | custom-call | bytes 10800000 | tf_op jit(solution)/shard_map/project_back/pallas_call | solution.py:164
  153.5 2.5 %owned_sum.1.refs_1_ = bf16[96,1536]{1,0:T(8,128)(2,1)S(1)} custom-call(s32[10]{0:T(128)S(1)} %dynamic-slice_bitcast_fusion.scal.refs_0_, bf16[8,96,1536]{2,1,0:T(8,128)(2,1)} %all-to-all-done.1.refs_1_), custom_call_target="tpu_custom_call" | custom-call | bytes 5400000 | tf_op jit(solution)/shard_map/owned_sum/pallas_call | solution.py:164
  156.6 0.7 merge.5
  157.3 1.6 collective-permute-start.37
  158.9 7.0 %collective-permute-done.39.refs_3_ = bf16[96,1536]{1,0:T(8,128)(2,1)S(1)} collective-permute-done((bf16[96,1536]{1,0:T(8,128)(2,1)S(1)}, bf16[96,1536]{1,0:T(8,128)(2,1)S(1)}, u32[]{:S(2)}, u32[]{:S(2)}) %collective-permute-start.39) | collective-permute-done | bytes 294944 | tf_op jit(solution)/shard_map/ppermute | solution.py:1184
  165.9 2.7 %output_sum.1 = bf16[256,768]{1,0:T(8,128)(2,1)} custom-call(s32[10]{0:T(128)S(1)} %dynamic-slice_bitcast_fusion.scal.refs_0_, f32[256,768]{1,0:T(8,128)S(1)} %get-tuple-element.211.refs_1_, bf16[256,768]{1,0:T(8,128)(2,1)} %copy-done.4, f32[256,768]{1,0:T(8,128)} %get-tuple-element.212.refs_3_, f32[16,768]{1,0:T(8,128)} %get-tuple-element.213.refs_4_.refs_5_), custom_call_target="tpu_custom_call" | custom-call | bytes 2880000 | tf_op jit(solution)/shard_map/output_sum/pallas_call | solution.py:164
  168.6 1.6 squares_of.1
  170.2 3.8 %collective-permute-done.37.refs_2_ = bf16[256,768]{1,0:T(8,128)(2,1)} collective-permute-done((bf16[256,768]{1,0:T(8,128)(2,1)S(1)}, bf16[256,768]{1,0:T(8,128)(2,1)}, u32[]{:S(2)}, u32[]{:S(2)}) %collective-permute-start.37) | collective-permute-done | bytes 393248 | tf_op jit(solution)/shard_map/ppermute | solution.py:1184
  174.0 6.4 %all-to-all-done.refs_1_ = bf16[8,104,768]{2,1,0:T(8,128)(2,1)S(1)} async-done(((bf16[8,104,768]{2,1,0:T(8,128)(2,1)}), bf16[8,104,768]{2,1,0:T(8,128)(2,1)S(1)}, u32[]{:S(2)}, u32[]{:S(2)}) %all-to-all-start) | async-done | bytes 1277984 | tf_op jit(solution)/shard_map/all_to_all | solution.py:1260
  180.4 0.7 owned_vector.1.refs_1_.refs_0_
  181.7 4.8 %collective-permute-done.42.refs_3_.refs_2_ = bf16[104,768]{1,0:T(8,128)(2,1)S(1)} collective-permute-done((bf16[104,768]{1,0:T(8,128)(2,1)S(1)}, bf16[104,768]{1,0:T(8,128)(2,1)S(1)}, u32[]{:S(2)}, u32[]{:S(2)}) %collective-permute-start.42) | collective-permute-done | bytes 159776 | tf_op jit(solution)/shard_map/ppermute | solution.py:1184
  186.5 1.4 collective-permute-done.43.refs_4_.refs_3_
  187.9 1.5 join.1
  189.3 4.4 %all-to-all-start.2 = ((f32[8,8,128]{2,1,0:T(8,128)}), f32[8,8,128]{2,1,0:T(8,128)S(1)}, u32[]{:S(2)}, u32[]{:S(2)}) async-start(f32[8,8,128]{2,1,0:T(8,128)} %bitcast.3), calls=%async_computation.2 | async-start | bytes 65536 | tf_op jit(solution)/shard_map/all_to_all | solution.py:1430
  193.7 3.3 %input_back.1 = f32[256,768]{1,0:T(8,128)} custom-call(s32[10]{0:T(128)S(1)} %dynamic-slice_bitcast_fusion.scal.refs_0_, f32[256,768]{1,0:T(8,128)S(1)} %get-tuple-element.217.refs_1_, bf16[256,768]{1,0:T(8,128)(2,1)} %collective-permute-done.37.refs_2_, bf16[256,768]{1,0:T(8,128)(2,1)} %refs_3_.5, f32[256,768]{1,0:T(8,128)} %get-tuple-element.219.refs_4_, ...), custom_call_target="tpu_custom_call" | custom-call | bytes 3600000 | tf_op jit(solution)/shard_map/input_back/pallas_call | solution.py:164
  197.1 3.3 %all-to-all-done.2.total_ref = f32[8,8,128]{2,1,0:T(8,128)S(1)} async-done(((f32[8,8,128]{2,1,0:T(8,128)}), f32[8,8,128]{2,1,0:T(8,128)S(1)}, u32[]{:S(2)}, u32[]{:S(2)}) %all-to-all-start.2) | async-done | bytes 32800 | tf_op jit(solution)/shard_map/all_to_all | solution.py:1430
  200.4 12.8 %adam.1 = (f32[96,3072]{1,0:T(8,128)}, f32[96,6144]{1,0:T(8,128)}, f32[12,96]{1,0:T(8,128)}, f32[96,3072]{1,0:T(8,128)}, f32[96,6144]{1,0:T(8,128)}, /*index=5*/...) custom-call(s32[10]{0:T(128)S(1)} %dynamic-slice_bitcast_fusion.scal, ...), custom_call_target="tpu_custom_call" | custom-call | bytes 32400000 | tf_op jit(solution)/shard_map/adam/pallas_call | solution.py:1151
  (69 shorter events, 10.9 us)
Async XLA Ops:
  1.4 13.1 %copy-start.2 = (bf16[256,768]{1,0:T(8,128)(2,1)S(1)}, bf16[256,768]{1,0:T(8,128)(2,1)}, u32[]{:S(2)}) copy-start(bf16[256,768]{1,0:T(8,128)(2,1)} %refs_3_.5) | copy-start | bytes 1179652
  1.4 19.0 %copy-start.3 = (s32[1,1024]{1,0:T(1,128)S(1)}, s32[1,1024]{1,0:T(1,128)}, u32[]{:S(2)}) copy-start(s32[1,1024]{1,0:T(1,128)} %refs_6_.1) | copy-start | bytes 12292
  1.4 26.1 %copy-start.1 = (bf16[256,768]{1,0:T(8,128)(2,1)S(1)}, bf16[256,768]{1,0:T(8,128)(2,1)}, u32[]{:S(2)}) copy-start(bf16[256,768]{1,0:T(8,128)(2,1)} %refs_3_.4) | copy-start | bytes 1179652
  1.4 27.6 %copy-start = (f32[96,6144]{1,0:T(8,128)S(1)}, f32[96,6144]{1,0:T(8,128)}, u32[]{:S(2)}) copy-start(f32[96,6144]{1,0:T(8,128)} %refs_12_.1) | copy-start | bytes 7077892
  3.6 7.4 %collective-permute-start.2 = (bf16[96,896]{1,0:T(8,128)(2,1)S(1)}, bf16[96,896]{1,0:T(8,128)(2,1)S(1)}, u32[]{:S(2)}, u32[]{:S(2)}) collective-permute-start(bf16[96,896]{1,0:T(8,128)(2,1)S(1)} %pack_attention.1.refs_2_), channel_id=1, source_target_pairs={{0,4},{8,0},{16,8},{24,16},{28,24},{20,28},{12,20},{4,12},{1,5},{9... | collective-permute-start | bytes 516104 | tf_op jit(solution)/shard_map/ppermute | solution.py:1233
  6.6 5.8 %collective-permute-start.1 = (bf16[96,896]{1,0:T(8,128)(2,1)S(1)}, bf16[96,896]{1,0:T(8,128)(2,1)S(1)}, u32[]{:S(2)}, u32[]{:S(2)}) collective-permute-start(bf16[96,896]{1,0:T(8,128)(2,1)S(1)} %pack_attention.1.refs_2_), channel_id=1, source_target_pairs={{0,8},{8,16},{16,24},{24,28},{28,20},{20,12},{12,4},{4,0},{1,9},{9... | collective-permute-start | bytes 516104 | tf_op jit(solution)/shard_map/ppermute | solution.py:1233
  12.5 5.4 %collective-permute-start.3 = (bf16[96,896]{1,0:T(8,128)(2,1)S(1)}, bf16[96,896]{1,0:T(8,128)(2,1)S(1)}, u32[]{:S(2)}, u32[]{:S(2)}) collective-permute-start(bf16[96,896]{1,0:T(8,128)(2,1)S(1)} %collective-permute-done.1.refs_3_), channel_id=1, source_target_pairs={{0,8},{8,16},{16,24},{24,28},{28,20},{20,12},{12,4},{4,0},{1,9},{9... | collective-permute-start | bytes 516104 | tf_op jit(solution)/shard_map/ppermute | solution.py:1233
  12.9 5.4 %collective-permute-start.4 = (bf16[96,896]{1,0:T(8,128)(2,1)S(1)}, bf16[96,896]{1,0:T(8,128)(2,1)S(1)}, u32[]{:S(2)}, u32[]{:S(2)}) collective-permute-start(bf16[96,896]{1,0:T(8,128)(2,1)S(1)} %collective-permute-done.2.refs_4_), channel_id=1, source_target_pairs={{0,4},{8,0},{16,8},{24,16},{28,24},{20,28},{12,20},{4,12},{1,5},{9... | collective-permute-start | bytes 516104 | tf_op jit(solution)/shard_map/ppermute | solution.py:1233
  14.5 12.5 %collective-permute-start = (bf16[256,768]{1,0:T(8,128)(2,1)S(1)}, bf16[256,768]{1,0:T(8,128)(2,1)S(1)}, u32[]{:S(2)}, u32[]{:S(2)}) collective-permute-start(bf16[256,768]{1,0:T(8,128)(2,1)S(1)} %copy-done.2), channel_id=1, source_target_pairs={{0,2},{1,3},{2,0},{3,1},{4,6},{5,7},{6,4},{7,5},{8,10},{9,11},{10,... | collective-permute-start | bytes 1179656 | tf_op jit(solution)/shard_map/ppermute | solution.py:1184
  18.3 5.4 %collective-permute-start.5 = (bf16[96,896]{1,0:T(8,128)(2,1)S(1)}, bf16[96,896]{1,0:T(8,128)(2,1)S(1)}, u32[]{:S(2)}, u32[]{:S(2)}) collective-permute-start(bf16[96,896]{1,0:T(8,128)(2,1)S(1)} %collective-permute-done.3.refs_5_), channel_id=1, source_target_pairs={{0,8},{8,16},{16,24},{24,28},{28,20},{20,12},{12,4},{4,0},{1,9},{9... | collective-permute-start | bytes 516104 | tf_op jit(solution)/shard_map/ppermute | solution.py:1233
  20.0 5.4 %collective-permute-start.6 = (bf16[96,896]{1,0:T(8,128)(2,1)S(1)}, bf16[96,896]{1,0:T(8,128)(2,1)S(1)}, u32[]{:S(2)}, u32[]{:S(2)}) collective-permute-start(bf16[96,896]{1,0:T(8,128)(2,1)S(1)} %collective-permute-done.4.refs_6_), channel_id=1, source_target_pairs={{0,4},{8,0},{16,8},{24,16},{28,24},{20,28},{12,20},{4,12},{1,5},{9... | collective-permute-start | bytes 516104 | tf_op jit(solution)/shard_map/ppermute | solution.py:1233
  25.4 5.4 %collective-permute-start.9 = (bf16[96,896]{1,0:T(8,128)(2,1)S(1)}, bf16[96,896]{1,0:T(8,128)(2,1)S(1)}, u32[]{:S(2)}, u32[]{:S(2)}) collective-permute-start(bf16[96,896]{1,0:T(8,128)(2,1)S(1)} %collective-permute-done.5.refs_7_), channel_id=1, source_target_pairs={{0,8},{8,16},{16,24},{24,28},{28,20},{20,12},{12,4},{4,0},{1,9},{9... | collective-permute-start | bytes 516104 | tf_op jit(solution)/shard_map/ppermute | solution.py:1233
  27.0 5.9 %collective-permute-start.7 = (bf16[256,768]{1,0:T(8,128)(2,1)S(1)}, bf16[256,768]{1,0:T(8,128)(2,1)S(1)}, u32[]{:S(2)}, u32[]{:S(2)}) collective-permute-start(bf16[256,768]{1,0:T(8,128)(2,1)S(1)} %copy-done.2), channel_id=1, source_target_pairs={{0,1},{1,0},{2,3},{3,2},{4,5},{5,4},{6,7},{7,6},{8,9},{9,8},{10,11... | collective-permute-start | bytes 1179656 | tf_op jit(solution)/shard_map/ppermute | solution.py:1184
  27.0 5.9 %collective-permute-start.8 = (bf16[256,768]{1,0:T(8,128)(2,1)S(1)}, bf16[256,768]{1,0:T(8,128)(2,1)S(1)}, u32[]{:S(2)}, u32[]{:S(2)}) collective-permute-start(bf16[256,768]{1,0:T(8,128)(2,1)S(1)} %collective-permute-done.refs_3_), channel_id=1, source_target_pairs={{0,1},{1,0},{2,3},{3,2},{4,5},{5,4},{6,7},{7,6},{8,9},{9,8},{10,11... | collective-permute-start | bytes 1179656 | tf_op jit(solution)/shard_map/ppermute | solution.py:1184
  27.5 11.0 %collective-permute-start.11 = (bf16[256,768]{1,0:T(8,128)(2,1)S(1)}, bf16[256,768]{1,0:T(8,128)(2,1)S(1)}, u32[]{:S(2)}, u32[]{:S(2)}) collective-permute-start(bf16[256,768]{1,0:T(8,128)(2,1)S(1)} %copy-done.1), channel_id=1, source_target_pairs={{0,2},{1,3},{2,0},{3,1},{4,6},{5,7},{6,4},{7,5},{8,10},{9,11},{10,... | collective-permute-start | bytes 1179656 | tf_op jit(solution)/shard_map/ppermute | solution.py:1184
  30.8 12.5 %collective-permute-start.22 = (bf16[96,1536]{1,0:T(8,128)(2,1)S(1)}, bf16[96,1536]{1,0:T(8,128)(2,1)S(1)}, u32[]{:S(2)}, u32[]{:S(2)}) collective-permute-start(bf16[96,1536]{1,0:T(8,128)(2,1)S(1)} %pack_forward.1.refs_15_), channel_id=1, source_target_pairs={{0,8},{8,16},{16,24},{24,28},{28,20},{20,12},{12,4},{4,0},{1,9},{9... | collective-permute-start | bytes 884744 | tf_op jit(solution)/shard_map/ppermute | solution.py:1233
  32.4 11.0 %collective-permute-start.23 = (bf16[96,1536]{1,0:T(8,128)(2,1)S(1)}, bf16[96,1536]{1,0:T(8,128)(2,1)S(1)}, u32[]{:S(2)}, u32[]{:S(2)}) collective-permute-start(bf16[96,1536]{1,0:T(8,128)(2,1)S(1)} %pack_forward.1.refs_15_), channel_id=1, source_target_pairs={{0,4},{8,0},{16,8},{24,16},{28,24},{20,28},{12,20},{4,12},{1,5},{9... | collective-permute-start | bytes 884744 | tf_op jit(solution)/shard_map/ppermute | solution.py:1233
  38.5 8.3 %collective-permute-start.10 = (bf16[1152,128]{1,0:T(8,128)(2,1)S(1)}, bf16[1152,128]{1,0:T(8,128)(2,1)S(1)}, u32[]{:S(2)}, u32[]{:S(2)}) collective-permute-start(bf16[1152,128]{1,0:T(8,128)(2,1)S(1)} %get-tuple-element.157.refs_11_), channel_id=1, source_target_pairs={{0,2},{1,3},{2,0},{3,1},{4,6},{5,7},{6,4},{7,5},{8,10},{9,11},{10,... | collective-permute-start | bytes 884744 | tf_op jit(solution)/shard_map/ppermute | solution.py:1184
  43.4 9.1 %collective-permute-start.24 = (bf16[96,1536]{1,0:T(8,128)(2,1)S(1)}, bf16[96,1536]{1,0:T(8,128)(2,1)S(1)}, u32[]{:S(2)}, u32[]{:S(2)}) collective-permute-start(bf16[96,1536]{1,0:T(8,128)(2,1)S(1)} %collective-permute-done.22.refs_16_), channel_id=1, source_target_pairs={{0,8},{8,16},{16,24},{24,28},{28,20},{20,12},{12,4},{4,0},{1,9},{9... | collective-permute-start | bytes 884744 | tf_op jit(solution)/shard_map/ppermute | solution.py:1233
  45.0 7.5 %collective-permute-start.25 = (bf16[96,1536]{1,0:T(8,128)(2,1)S(1)}, bf16[96,1536]{1,0:T(8,128)(2,1)S(1)}, u32[]{:S(2)}, u32[]{:S(2)}) collective-permute-start(bf16[96,1536]{1,0:T(8,128)(2,1)S(1)} %collective-permute-done.23.refs_17_), channel_id=1, source_target_pairs={{0,4},{8,0},{16,8},{24,16},{28,24},{20,28},{12,20},{4,12},{1,5},{9... | collective-permute-start | bytes 884744 | tf_op jit(solution)/shard_map/ppermute | solution.py:1233
  45.4 9.1 %collective-permute-start.12 = (bf16[768,128]{1,0:T(8,128)(2,1)S(1)}, bf16[768,128]{1,0:T(8,128)(2,1)S(1)}, u32[]{:S(2)}, u32[]{:S(2)}) collective-permute-start(bf16[768,128]{1,0:T(8,128)(2,1)S(1)} %get-tuple-element.155.refs_3_), channel_id=1, source_target_pairs={{0,2},{1,3},{2,0},{3,1},{4,6},{5,7},{6,4},{7,5},{8,10},{9,11},{10,... | collective-permute-start | bytes 589832 | tf_op jit(solution)/shard_map/ppermute | solution.py:1184
  49.9 6.2 %collective-permute-start.13 = (bf16[768,128]{1,0:T(8,128)(2,1)S(1)}, bf16[768,128]{1,0:T(8,128)(2,1)S(1)}, u32[]{:S(2)}, u32[]{:S(2)}) collective-permute-start(bf16[768,128]{1,0:T(8,128)(2,1)S(1)} %attend.3.refs_4_), channel_id=1, source_target_pairs={{0,2},{1,3},{2,0},{3,1},{4,6},{5,7},{6,4},{7,5},{8,10},{9,11},{10,... | collective-permute-start | bytes 589832 | tf_op jit(solution)/shard_map/ppermute | solution.py:1184
  52.5 6.7 %collective-permute-start.26 = (bf16[96,1536]{1,0:T(8,128)(2,1)S(1)}, bf16[96,1536]{1,0:T(8,128)(2,1)S(1)}, u32[]{:S(2)}, u32[]{:S(2)}) collective-permute-start(bf16[96,1536]{1,0:T(8,128)(2,1)S(1)} %collective-permute-done.24.refs_18_), channel_id=1, source_target_pairs={{0,8},{8,16},{16,24},{24,28},{28,20},{20,12},{12,4},{4,0},{1,9},{9... | collective-permute-start | bytes 884744 | tf_op jit(solution)/shard_map/ppermute | solution.py:1233
  54.0 6.7 %collective-permute-start.27 = (bf16[96,1536]{1,0:T(8,128)(2,1)S(1)}, bf16[96,1536]{1,0:T(8,128)(2,1)S(1)}, u32[]{:S(2)}, u32[]{:S(2)}) collective-permute-start(bf16[96,1536]{1,0:T(8,128)(2,1)S(1)} %collective-permute-done.25.refs_19_), channel_id=1, source_target_pairs={{0,4},{8,0},{16,8},{24,16},{28,24},{20,28},{12,20},{4,12},{1,5},{9... | collective-permute-start | bytes 884744 | tf_op jit(solution)/shard_map/ppermute | solution.py:1233
  56.1 6.7 %collective-permute-start.14 = (bf16[256,768]{1,0:T(8,128)(2,1)S(1)}, bf16[256,768]{1,0:T(8,128)(2,1)S(1)}, u32[]{:S(2)}, u32[]{:S(2)}) collective-permute-start(bf16[256,768]{1,0:T(8,128)(2,1)S(1)} %copy-done.1), channel_id=1, source_target_pairs={{0,1},{1,0},{2,3},{3,2},{4,5},{5,4},{6,7},{7,6},{8,9},{9,8},{10,11... | collective-permute-start | bytes 1179656 | tf_op jit(solution)/shard_map/ppermute | solution.py:1184
  56.1 6.7 %collective-permute-start.15 = (bf16[256,768]{1,0:T(8,128)(2,1)S(1)}, bf16[256,768]{1,0:T(8,128)(2,1)S(1)}, u32[]{:S(2)}, u32[]{:S(2)}) collective-permute-start(bf16[256,768]{1,0:T(8,128)(2,1)S(1)} %collective-permute-done.11.refs_3_), channel_id=1, source_target_pairs={{0,1},{1,0},{2,3},{3,2},{4,5},{5,4},{6,7},{7,6},{8,9},{9,8},{10,11... | collective-permute-start | bytes 1179656 | tf_op jit(solution)/shard_map/ppermute | solution.py:1184
  56.6 4.2 %collective-permute-start.17 = (bf16[768,128]{1,0:T(8,128)(2,1)S(1)}, bf16[768,128]{1,0:T(8,128)(2,1)S(1)}, u32[]{:S(2)}, u32[]{:S(2)}) collective-permute-start(bf16[768,128]{1,0:T(8,128)(2,1)S(1)} %attend.3.refs_4_), channel_id=1, source_target_pairs={{0,1},{1,0},{2,3},{3,2},{4,5},{5,4},{6,7},{7,6},{8,9},{9,8},{10,11... | collective-permute-start | bytes 589832 | tf_op jit(solution)/shard_map/ppermute | solution.py:1184
  59.2 2.0 collective-permute-start.19
  60.7 3.7 %collective-permute-start.20 = (bf16[1152,128]{1,0:T(8,128)(2,1)S(1)}, bf16[1152,128]{1,0:T(8,128)(2,1)S(1)}, u32[]{:S(2)}, u32[]{:S(2)}) collective-permute-start(bf16[1152,128]{1,0:T(8,128)(2,1)S(1)} %get-tuple-element.157.refs_11_), channel_id=1, source_target_pairs={{0,1},{1,0},{2,3},{3,2},{4,5},{5,4},{6,7},{7,6},{8,9},{9,8},{10,11... | collective-permute-start | bytes 884744 | tf_op jit(solution)/shard_map/ppermute | solution.py:1184
  60.8 3.7 %collective-permute-start.21 = (bf16[1152,128]{1,0:T(8,128)(2,1)S(1)}, bf16[1152,128]{1,0:T(8,128)(2,1)S(1)}, u32[]{:S(2)}, u32[]{:S(2)}) collective-permute-start(bf16[1152,128]{1,0:T(8,128)(2,1)S(1)} %collective-permute-done.10.refs_13_), channel_id=1, source_target_pairs={{0,1},{1,0},{2,3},{3,2},{4,5},{5,4},{6,7},{7,6},{8,9},{9,8},{10,11... | collective-permute-start | bytes 884744 | tf_op jit(solution)/shard_map/ppermute | solution.py:1184
  61.3 9.0 %collective-permute-start.28 = (bf16[96,1536]{1,0:T(8,128)(2,1)S(1)}, bf16[96,1536]{1,0:T(8,128)(2,1)S(1)}, u32[]{:S(2)}, u32[]{:S(2)}) collective-permute-start(bf16[96,1536]{1,0:T(8,128)(2,1)S(1)} %collective-permute-done.26.refs_20_), channel_id=1, source_target_pairs={{0,8},{8,16},{16,24},{24,28},{28,20},{20,12},{12,4},{4,0},{1,9},{9... | collective-permute-start | bytes 884744 | tf_op jit(solution)/shard_map/ppermute | solution.py:1233
  62.8 1.4 collective-permute-start.16
  62.8 1.7 collective-permute-start.18
  81.5 5.2 %collective-permute-start.29 = (bf16[512,768]{1,0:T(8,128)(2,1)S(1)}, bf16[512,768]{1,0:T(8,128)(2,1)S(1)}, u32[]{:S(2)}, u32[]{:S(2)}) collective-permute-start(bf16[512,768]{1,0:T(8,128)(2,1)S(1)} %get-tuple-element.178), channel_id=1, source_target_pairs={{0,1},{1,0},{2,3},{3,2},{4,5},{5,4},{6,7},{7,6},{8,9},{9,8},{10,11... | collective-permute-start | bytes 2359304 | tf_op jit(solution)/shard_map/ppermute | solution.py:1184
  86.7 59.2 %all-to-all-start.1 = ((bf16[8,96,1536]{2,1,0:T(8,128)(2,1)}), bf16[8,96,1536]{2,1,0:T(8,128)(2,1)}, u32[]{:S(2)}, u32[]{:S(2)}) async-start(bf16[8,96,1536]{2,1,0:T(8,128)(2,1)} %bitcast.2), calls=%async_computation.1 | async-start | bytes 4718592 | tf_op jit(solution)/shard_map/all_to_all | solution.py:1260
  91.8 11.6 %collective-permute-start.30 = (bf16[256,768]{1,0:T(8,128)(2,1)S(1)}, bf16[256,768]{1,0:T(8,128)(2,1)S(1)}, u32[]{:S(2)}, u32[]{:S(2)}) collective-permute-start(bf16[256,768]{1,0:T(8,128)(2,1)S(1)} %get-tuple-element.180), channel_id=1, source_target_pairs={{0,2},{1,3},{2,0},{3,1},{4,6},{5,7},{6,4},{7,5},{8,10},{9,11},{10,... | collective-permute-start | bytes 1179656 | tf_op jit(solution)/shard_map/ppermute | solution.py:1184
  104.6 2.5 %collective-permute-start.31 = (bf16[512,768]{1,0:T(8,128)(2,1)S(1)}, bf16[512,768]{1,0:T(8,128)(2,1)S(1)}, u32[]{:S(2)}, u32[]{:S(2)}) collective-permute-start(bf16[512,768]{1,0:T(8,128)(2,1)S(1)} %get-tuple-element.188), channel_id=1, source_target_pairs={{0,1},{1,0},{2,3},{3,2},{4,5},{5,4},{6,7},{7,6},{8,9},{9,8},{10,11... | collective-permute-start | bytes 2359304 | tf_op jit(solution)/shard_map/ppermute | solution.py:1184
  104.6 11.5 %collective-permute-start.33 = (bf16[256,768]{1,0:T(8,128)(2,1)S(1)}, bf16[256,768]{1,0:T(8,128)(2,1)S(1)}, u32[]{:S(2)}, u32[]{:S(2)}) collective-permute-start(bf16[256,768]{1,0:T(8,128)(2,1)S(1)} %get-tuple-element.187.refs_1_), channel_id=1, source_target_pairs={{0,2},{1,3},{2,0},{3,1},{4,6},{5,7},{6,4},{7,5},{8,10},{9,11},{10,... | collective-permute-start | bytes 1179656 | tf_op jit(solution)/shard_map/ppermute | solution.py:1184
  105.2 11.0 %collective-permute-start.32 = (bf16[256,768]{1,0:T(8,128)(2,1)S(1)}, bf16[256,768]{1,0:T(8,128)(2,1)S(1)}, u32[]{:S(2)}, u32[]{:S(2)}) collective-permute-start(bf16[256,768]{1,0:T(8,128)(2,1)S(1)} %get-tuple-element.187.refs_1_), channel_id=1, source_target_pairs={{0,1},{1,0},{2,3},{3,2},{4,5},{5,4},{6,7},{7,6},{8,9},{9,8},{10,11... | collective-permute-start | bytes 1179656 | tf_op jit(solution)/shard_map/ppermute | solution.py:1184
  116.2 1.7 collective-permute-start.34
  122.2 12.7 %collective-permute-start.35 = (bf16[256,768]{1,0:T(8,128)(2,1)S(1)}, bf16[256,768]{1,0:T(8,128)(2,1)S(1)}, u32[]{:S(2)}, u32[]{:S(2)}) collective-permute-start(bf16[256,768]{1,0:T(8,128)(2,1)S(1)} %get-tuple-element.198), channel_id=1, source_target_pairs={{0,2},{1,3},{2,0},{3,1},{4,6},{5,7},{6,4},{7,5},{8,10},{9,11},{10,... | collective-permute-start | bytes 1179656 | tf_op jit(solution)/shard_map/ppermute | solution.py:1184
  134.9 7.8 %copy-start.4 = (bf16[256,768]{1,0:T(8,128)(2,1)}, bf16[256,768]{1,0:T(8,128)(2,1)S(1)}, u32[]{:S(2)}) copy-start(bf16[256,768]{1,0:T(8,128)(2,1)S(1)} %collective-permute-done.35.refs_2_) | copy-start | bytes 1179652
  145.9 34.5 %all-to-all-start = ((bf16[8,104,768]{2,1,0:T(8,128)(2,1)}), bf16[8,104,768]{2,1,0:T(8,128)(2,1)S(1)}, u32[]{:S(2)}, u32[]{:S(2)}) async-start(bf16[8,104,768]{2,1,0:T(8,128)(2,1)} %bitcast.6), calls=%async_computation | async-start | bytes 2555904 | tf_op jit(solution)/shard_map/all_to_all | solution.py:1260
  153.4 3.1 %collective-permute-start.36 = (bf16[512,768]{1,0:T(8,128)(2,1)S(1)}, bf16[512,768]{1,0:T(8,128)(2,1)S(1)}, u32[]{:S(2)}, u32[]{:S(2)}) collective-permute-start(bf16[512,768]{1,0:T(8,128)(2,1)S(1)} %get-tuple-element.216), channel_id=1, source_target_pairs={{0,1},{1,0},{2,3},{3,2},{4,5},{5,4},{6,7},{7,6},{8,9},{9,8},{10,11... | collective-permute-start | bytes 2359304 | tf_op jit(solution)/shard_map/ppermute | solution.py:1184
  156.0 9.9 %collective-permute-start.39 = (bf16[96,1536]{1,0:T(8,128)(2,1)S(1)}, bf16[96,1536]{1,0:T(8,128)(2,1)S(1)}, u32[]{:S(2)}, u32[]{:S(2)}) collective-permute-start(bf16[96,1536]{1,0:T(8,128)(2,1)S(1)} %owned_sum.1.refs_1_), channel_id=1, source_target_pairs={{0,2},{1,3},{2,0},{3,1},{4,6},{5,7},{6,4},{7,5},{8,10},{9,11},{10,... | collective-permute-start | bytes 884744 | tf_op jit(solution)/shard_map/ppermute | solution.py:1184
  157.3 16.8 %collective-permute-start.37 = (bf16[256,768]{1,0:T(8,128)(2,1)S(1)}, bf16[256,768]{1,0:T(8,128)(2,1)}, u32[]{:S(2)}, u32[]{:S(2)}) collective-permute-start(bf16[256,768]{1,0:T(8,128)(2,1)S(1)} %get-tuple-element.218), channel_id=1, source_target_pairs={{0,2},{1,3},{2,0},{3,1},{4,6},{5,7},{6,4},{7,5},{8,10},{9,11},{10,... | collective-permute-start | bytes 1179656 | tf_op jit(solution)/shard_map/ppermute | solution.py:1184
  158.9 9.7 %collective-permute-start.38 = (bf16[96,1536]{1,0:T(8,128)(2,1)S(1)}, bf16[96,1536]{1,0:T(8,128)(2,1)S(1)}, u32[]{:S(2)}, u32[]{:S(2)}) collective-permute-start(bf16[96,1536]{1,0:T(8,128)(2,1)S(1)} %owned_sum.1.refs_1_), channel_id=1, source_target_pairs={{0,1},{1,0},{2,3},{3,2},{4,5},{5,4},{6,7},{7,6},{8,9},{9,8},{10,11... | collective-permute-start | bytes 884744 | tf_op jit(solution)/shard_map/ppermute | solution.py:1184
  165.9 2.7 %collective-permute-start.40 = (bf16[96,1536]{1,0:T(8,128)(2,1)S(1)}, bf16[96,1536]{1,0:T(8,128)(2,1)S(1)}, u32[]{:S(2)}, u32[]{:S(2)}) collective-permute-start(bf16[96,1536]{1,0:T(8,128)(2,1)S(1)} %collective-permute-done.39.refs_3_), channel_id=1, source_target_pairs={{0,1},{1,0},{2,3},{3,2},{4,5},{5,4},{6,7},{7,6},{8,9},{9,8},{10,11... | collective-permute-start | bytes 884744 | tf_op jit(solution)/shard_map/ppermute | solution.py:1184
  181.1 5.3 %collective-permute-start.42 = (bf16[104,768]{1,0:T(8,128)(2,1)S(1)}, bf16[104,768]{1,0:T(8,128)(2,1)S(1)}, u32[]{:S(2)}, u32[]{:S(2)}) collective-permute-start(bf16[104,768]{1,0:T(8,128)(2,1)S(1)} %owned_vector.1.refs_1_.refs_0_), channel_id=1, source_target_pairs={{0,2},{1,3},{2,0},{3,1},{4,6},{5,7},{6,4},{7,5},{8,10},{9,11},{10,... | collective-permute-start | bytes 479240 | tf_op jit(solution)/shard_map/ppermute | solution.py:1184
  181.7 4.8 %collective-permute-start.41 = (bf16[104,768]{1,0:T(8,128)(2,1)S(1)}, bf16[104,768]{1,0:T(8,128)(2,1)S(1)}, u32[]{:S(2)}, u32[]{:S(2)}) collective-permute-start(bf16[104,768]{1,0:T(8,128)(2,1)S(1)} %owned_vector.1.refs_1_.refs_0_), channel_id=1, source_target_pairs={{0,1},{1,0},{2,3},{3,2},{4,5},{5,4},{6,7},{7,6},{8,9},{9,8},{10,11... | collective-permute-start | bytes 479240 | tf_op jit(solution)/shard_map/ppermute | solution.py:1184
  186.5 1.4 collective-permute-start.43
  189.3 11.1 %all-to-all-start.2 = ((f32[8,8,128]{2,1,0:T(8,128)}), f32[8,8,128]{2,1,0:T(8,128)S(1)}, u32[]{:S(2)}, u32[]{:S(2)}) async-start(f32[8,8,128]{2,1,0:T(8,128)} %bitcast.3), calls=%async_computation.2 | async-start | bytes 65536 | tf_op jit(solution)/shard_map/all_to_all | solution.py:1430

commit v4 on v3

--- a/solution.py
+++ b/solution.py
@@ -1143,7 +1143,7 @@
 
 
 def adam(scal, totals, attention_grads, forward_grads_by_member, states, cols, ringed):
-    counts = (4, 2 * GROUPS, 1)
+    counts = (8, 2 * GROUPS, 1)
     kinds = [states[4 * kind].shape for kind in range(3)]
     out_shape = [pltpu.HBM(shape, F32) for _ in range(4) for shape in kinds]
     out_shape += [pltpu.HBM(shape, BF) for shape in kinds]

time: 214 us -> 215 us (level)
  no operation moved by 1% of the time
where the time goes in v4:
time: 215 us; the launch traced here: 214 us
  Pallas kernels  98.6 us (46%)
  waiting for transfers between devices  69.9 us (33%)
  starting transfers between devices  43.2 us (20%)
    pallas_call x24, Pallas kernels, run(): pl.pallas_call(body, out_shape=shapes + [pltpu.HBM(inputs[i].shape, input...  82.6 us
    ppermute x30, waiting for transfers between devices, swap(): return lax.ppermute(part, 'head', [(i, i ^ bit) for i in range(4)])  34.8 us
    ppermute x14, waiting for transfers between devices, send(): return lax.ppermute(array, 'dp', pairs)  22.1 us
    ppermute x14, starting transfers between devices, send(): return lax.ppermute(array, 'dp', pairs)  16.4 us
    ppermute x30, starting transfers between devices, swap(): return lax.ppermute(part, 'head', [(i, i ^ bit) for i in range(4)])  14.4 us
    pallas_call x1, Pallas kernels, adam(): pl.pallas_call(functools.partial(adam_kernel, counts, cols, ringed), out_...  13 us
    all_to_all x2, waiting for transfers between devices, exchange_owned(): return lax.all_to_all(blocks, 'dp', split_axis=0, concat_axis=0)  9.6 us
    all_to_all x2, starting transfers between devices, exchange_owned(): return lax.all_to_all(blocks, 'dp', split_axis=0, concat_axis=0)  8 us
  transfers between devices with their start and end apart: 47, of which 25 were waited for; matrix products, arithmetic and copies ran while one was open for 0% of the time, Pallas kernels for 33%

profile of v4, /device:TPU:0, one launch (start us, length us, event | category | flops | bytes accessed | tf_op | source)
XLA Modules:
  0.0 213.9 jit_solution(5884283640514865634)
XLA Ops:
  0.7 0.7 dynamic-slice_bitcast_fusion.scal.refs_0_
  1.4 2.3 %pack_attention.1.refs_2_ = bf16[96,896]{1,0:T(8,128)(2,1)S(1)} custom-call(s32[10]{0:T(128)S(1)} %dynamic-slice_bitcast_fusion.scal.refs_0_, f32[96,3072]{1,0:T(8,128)} %refs_8_.1, f32[96,3072]{1,0:T(8,128)} %refs_8_.1, f32[96,3072]{1,0:T(8,128)} %refs_8_.1, f32[96,3072]{1,0:T(8,128)} %refs_8_.1, f32[12,96]{1,0:T(8,128)} %refs_16_.1), custom_call_target="tpu_custom_call" | custom-call | bytes 5400000 | tf_op jit(solution)/shard_map/pack_attention/pallas_call | solution.py:206
  3.6 3.0 %collective-permute-start.2 = (bf16[96,896]{1,0:T(8,128)(2,1)S(1)}, bf16[96,896]{1,0:T(8,128)(2,1)S(1)}, u32[]{:S(2)}, u32[]{:S(2)}) collective-permute-start(bf16[96,896]{1,0:T(8,128)(2,1)S(1)} %pack_attention.1.refs_2_), channel_id=1, source_target_pairs={{0,4},{8,0},{16,8},{24,16},{28,24},{20,28},{12,20},{4,12},{1,5},{9... | collective-permute-start | bytes 516104 | tf_op jit(solution)/shard_map/ppermute | solution.py:1233
  6.8 4.3 %collective-permute-done.2.refs_4_ = bf16[96,896]{1,0:T(8,128)(2,1)S(1)} collective-permute-done((bf16[96,896]{1,0:T(8,128)(2,1)S(1)}, bf16[96,896]{1,0:T(8,128)(2,1)S(1)}, u32[]{:S(2)}, u32[]{:S(2)}) %collective-permute-start.2) | collective-permute-done | bytes 172064 | tf_op jit(solution)/shard_map/ppermute | solution.py:1233
  11.1 1.4 collective-permute-done.1.refs_3_
  12.9 1.6 collective-permute-start.4
  14.5 1.5 collective-permute-start
  16.0 1.9 collective-permute-done.3.refs_5_
  18.3 1.7 collective-permute-start.5
  20.3 1.9 read_segments.1
  22.2 1.5 collective-permute-done.5.refs_7_
  23.7 1.7 collective-permute-done.6.refs_8_
  25.4 1.6 collective-permute-start.9
  27.5 1.5 collective-permute-start.11
  29.0 0.7 pack_forward.1.refs_15_
  29.7 1.1 collective-permute-done.9.refs_9_
  30.8 1.6 collective-permute-start.22
  33.5 3.9 %project.1 = (bf16[1024,192]{1,0:T(8,128)(2,1)S(1)}, bf16[1024,192]{1,0:T(8,128)(2,1)S(1)}, bf16[1024,192]{1,0:T(8,128)(2,1)S(1)}, bf16[768,576]{1,0:T(8,128)(2,...) custom-call(s32[10]{0:T(128)S(1)} %dynamic-slice_bitcast_fusion.scal, ...), custom_call_target="tpu_custom_call" | custom-call | bytes 16200000 | tf_op jit(solution)/shard_map/project/pallas_call | solution.py:164
  37.4 1.1 collective-permute-done.11.refs_3_
  38.5 1.5 collective-permute-start.10
  40.0 3.3 %attend.2 = (bf16[768,128]{1,0:T(8,128)(2,1)S(1)}, bf16[1024,192]{1,0:T(8,128)(2,1)}, bf16[1024,192]{1,0:T(8,128)(2,1)}, bf16[1024,192]{1,0:T(8,128)(2,1)}, s32[...) custom-call(s32[10]{0:T(128)S(1)} %dynamic-slice_bitcast_fusion.scal, ...), custom_call_target="tpu_custom_call" | custom-call | bytes 12600000 | tf_op jit(solution)/shard_map/attend/pallas_call | solution.py:164
  43.4 1.6 collective-permute-start.24
  45.9 0.8 collective-permute-done.10.refs_13_
  46.8 3.1 %attend.3.refs_4_ = bf16[768,128]{1,0:T(8,128)(2,1)S(1)} custom-call(s32[10]{0:T(128)S(1)} %dynamic-slice_bitcast_fusion.scal.refs_0_, s32[16]{0:T(128)S(1)} %get-tuple-element.141.refs_1_, bf16[1024,192]{1,0:T(8,128)(2,1)S(1)} %get-tuple-element.152.refs_2_, bf16[1024,192]{1,0:T(8,128)(2,1)S(1)} %get-tuple-element.144.refs_3_, ...), custom_call_target="tpu_custom_call" | custom-call | bytes 12600000 | tf_op jit(solution)/shard_map/attend/pallas_call | solution.py:164
  49.9 2.5 %collective-permute-start.13 = (bf16[768,128]{1,0:T(8,128)(2,1)S(1)}, bf16[768,128]{1,0:T(8,128)(2,1)S(1)}, u32[]{:S(2)}, u32[]{:S(2)}) collective-permute-start(bf16[768,128]{1,0:T(8,128)(2,1)S(1)} %attend.3.refs_4_), channel_id=1, source_target_pairs={{0,2},{1,3},{2,0},{3,1},{4,6},{5,7},{6,4},{7,5},{8,10},{9,11},{10,... | collective-permute-start | bytes 589832 | tf_op jit(solution)/shard_map/ppermute | solution.py:1184
  52.5 1.5 collective-permute-start.26
  54.5 1.6 collective-permute-done.13.refs_8_
  56.6 2.6 %collective-permute-done.26.refs_20_ = bf16[96,1536]{1,0:T(8,128)(2,1)S(1)} collective-permute-done((bf16[96,1536]{1,0:T(8,128)(2,1)S(1)}, bf16[96,1536]{1,0:T(8,128)(2,1)S(1)}, u32[]{:S(2)}, u32[]{:S(2)}) %collective-permute-start.26) | collective-permute-done | bytes 294944 | tf_op jit(solution)/shard_map/ppermute | solution.py:1233
  59.2 1.5 collective-permute-done.27.refs_21_
  61.3 1.5 collective-permute-start.28
  64.5 5.7 %collective-permute-done.28.refs_22_ = bf16[96,1536]{1,0:T(8,128)(2,1)S(1)} collective-permute-done((bf16[96,1536]{1,0:T(8,128)(2,1)S(1)}, bf16[96,1536]{1,0:T(8,128)(2,1)S(1)}, u32[]{:S(2)}, u32[]{:S(2)}) %collective-permute-start.28) | collective-permute-done | bytes 294944 | tf_op jit(solution)/shard_map/ppermute | solution.py:1233
  70.2 11.2 %forward_back.1 = (bf16[1024,768]{1,0:T(8,128)(2,1)S(1)}, bf16[1024,768]{1,0:T(8,128)(2,1)S(1)}, bf16[1024,768]{1,0:T(8,128)(2,1)S(1)}, f32[512,768]{1,0:T(8,128...) custom-call(s32[10]{0:T(128)S(1)} %dynamic-slice_bitcast_fusion.scal, ...), custom_call_target="tpu_custom_call" | custom-call | bytes 46800000 | tf_op jit(solution)/shard_map/forward_back/pallas_call | solution.py:164
  81.5 5.1 %forward_grads.1 = (bf16[768,1536]{1,0:T(8,128)(2,1)}, bf16[1024,768]{1,0:T(8,128)(2,1)}, f32[256,768]{1,0:T(8,128)}, f32[8,768]{1,0:T(8,128)}, bf16[192,768]{1,...) custom-call(s32[10]{0:T(128)S(1)} %dynamic-slice_bitcast_fusion.scal.refs_0_, ...), custom_call_target="tpu_custom_call" | custom-call | bytes 14400000 | tf_op jit(solution)/shard_map/forward_grads/pallas_call | solution.py:164
  86.7 4.4 %all-to-all-start.1 = ((bf16[8,96,1536]{2,1,0:T(8,128)(2,1)}), bf16[8,96,1536]{2,1,0:T(8,128)(2,1)}, u32[]{:S(2)}, u32[]{:S(2)}) async-start(bf16[8,96,1536]{2,1,0:T(8,128)(2,1)} %bitcast.2), calls=%async_computation.1 | async-start | bytes 4718592 | tf_op jit(solution)/shard_map/all_to_all | solution.py:1260
  91.1 0.7 merge.3
  92.3 6.1 %branch_part.1 = (f32[512,768]{1,0:T(8,128)}, bf16[512,768]{1,0:T(8,128)(2,1)S(1)}, bf16[256,768]{1,0:T(8,128)(2,1)S(1)}) custom-call(s32[10]{0:T(128)S(1)} %dynamic-slice_bitcast_fusion.scal.refs_0_, bf16[1024,768]{1,0:T(8,128)(2,1)} %get-tuple-element.174.refs_1_, bf16[768,1536]{1,0:T(8,128)(2,1)} %get-tuple-element.181.refs_2_, bf16[256,768]{1,0:T(8,128)(2,1)} %refs_3_.4), custom_call_target="tpu_custom_call" | custom-call | bytes 10800000 | tf_op jit(solution)/shard_map/branch_part/pallas_call | solution.py:164
  98.4 4.9 %collective-permute-done.30.refs_2_ = bf16[256,768]{1,0:T(8,128)(2,1)S(1)} collective-permute-done((bf16[256,768]{1,0:T(8,128)(2,1)S(1)}, bf16[256,768]{1,0:T(8,128)(2,1)S(1)}, u32[]{:S(2)}, u32[]{:S(2)}) %collective-permute-start.30) | collective-permute-done | bytes 393248 | tf_op jit(solution)/shard_map/ppermute | solution.py:1184
  103.3 1.2 resid_back.1
  105.3 1.7 vector_table.1.refs_9_
  107.0 2.1 %merge.4 = (f32[256,768]{1,0:T(8,128)S(1)}, bf16[256,768]{1,0:T(8,128)(2,1)S(1)}) custom-call(s32[10]{0:T(128)S(1)} %dynamic-slice_bitcast_fusion.scal.refs_0_, f32[512,768]{1,0:T(8,128)} %get-tuple-element.182.refs_1_, bf16[512,768]{1,0:T(8,128)(2,1)S(1)} %collective-permute-done.31.refs_2_), custom_call_target="tpu_custom_call" | custom-call | bytes 2520000 | tf_op jit(solution)/shard_map/merge/pallas_call | solution.py:164
  109.2 7.0 %collective-permute-done.33.refs_3_ = bf16[256,768]{1,0:T(8,128)(2,1)S(1)} collective-permute-done((bf16[256,768]{1,0:T(8,128)(2,1)S(1)}, bf16[256,768]{1,0:T(8,128)(2,1)S(1)}, u32[]{:S(2)}, u32[]{:S(2)}) %collective-permute-start.33) | collective-permute-done | bytes 393248 | tf_op jit(solution)/shard_map/ppermute | solution.py:1184
  116.2 1.7 collective-permute-done.34.refs_4_
  117.9 4.3 %mixed_back.1 = (bf16[1024,192]{1,0:T(8,128)(2,1)S(1)}, bf16[768,192]{1,0:T(8,128)(2,1)S(1)}) custom-call(s32[10]{0:T(128)S(1)} %dynamic-slice_bitcast_fusion.scal.refs_0_, bf16[256,768]{1,0:T(8,128)(2,1)S(1)} %get-tuple-element.187.refs_1_, bf16[256,768]{1,0:T(8,128)(2,1)S(1)} %collective-permute-done.32.refs_2_, ...), custom_call_target="tpu_custom_call" | custom-call | bytes 9000000 | tf_op jit(solution)/shard_map/mixed_back/pallas_call | solution.py:164
  122.7 12.1 %attend_back.1 = (bf16[1024,576]{1,0:T(8,128)(2,1)S(1)}, f32[256,768]{1,0:T(8,128)}, f32[768,128]{1,0:T(8,128)}, bf16[768,192]{1,0:T(8,128)(2,1)}) custom-call(s32[10]{0:T(128)S(1)} %dynamic-slice_bitcast_fusion.scal.refs_0_, s32[16]{0:T(128)S(1)} %get-tuple-element.141.refs_1_, bf16[1024,192]{1,0:T(8,128)(2,1)} %get-tuple-element.201.refs_2_, ...), custom_call_target="tpu_custom_call" | custom-call | bytes 57600000 | tf_op jit(solution)/shard_map/attend_back/pallas_call | solution.py:164
  134.9 7.7 %query_grads.1 = bf16[832,768]{1,0:T(8,128)(2,1)} custom-call(s32[10]{0:T(128)S(1)} %dynamic-slice_bitcast_fusion.scal.refs_0_, bf16[1024,768]{1,0:T(8,128)(2,1)} %get-tuple-element.199.refs_1_, bf16[1024,768]{1,0:T(8,128)(2,1)} %get-tuple-element.200.refs_2_, bf16[768,192]{1,0:T(8,128)(2,1)} %get-tuple-element.207.refs_3_, ...), custom_call_target="tpu_custom_call" | custom-call | bytes 14400000 | tf_op jit(solution)/shard_map/query_grads/pallas_call | solution.py:164
  142.6 3.2 %all-to-all-done.1.refs_1_ = bf16[8,96,1536]{2,1,0:T(8,128)(2,1)} async-done(((bf16[8,96,1536]{2,1,0:T(8,128)(2,1)}), bf16[8,96,1536]{2,1,0:T(8,128)(2,1)}, u32[]{:S(2)}, u32[]{:S(2)}) %all-to-all-start.1) | async-done | bytes 2359328 | tf_op jit(solution)/shard_map/all_to_all | solution.py:1260
  145.9 3.6 %all-to-all-start = ((bf16[8,104,768]{2,1,0:T(8,128)(2,1)}), bf16[8,104,768]{2,1,0:T(8,128)(2,1)S(1)}, u32[]{:S(2)}, u32[]{:S(2)}) async-start(bf16[8,104,768]{2,1,0:T(8,128)(2,1)} %bitcast.6), calls=%async_computation | async-start | bytes 2555904 | tf_op jit(solution)/shard_map/all_to_all | solution.py:1260
  149.5 3.9 %project_back.1 = (f32[512,768]{1,0:T(8,128)S(1)}, bf16[512,768]{1,0:T(8,128)(2,1)S(1)}) custom-call(s32[10]{0:T(128)S(1)} %dynamic-slice_bitcast_fusion.scal.refs_0_, bf16[1024,576]{1,0:T(8,128)(2,1)S(1)} %get-tuple-element.208.refs_4_.refs_1_, bf16[768,576]{1,0:T(8,128)(2,1)} %get-tuple-element.214.refs_5_.refs_2_), custom_call_target="tpu_custom_call" | custom-call | bytes 10800000 | tf_op jit(solution)/shard_map/project_back/pallas_call | solution.py:164
  153.5 2.5 %owned_sum.1.refs_1_ = bf16[96,1536]{1,0:T(8,128)(2,1)S(1)} custom-call(s32[10]{0:T(128)S(1)} %dynamic-slice_bitcast_fusion.scal.refs_0_, bf16[8,96,1536]{2,1,0:T(8,128)(2,1)} %all-to-all-done.1.refs_1_), custom_call_target="tpu_custom_call" | custom-call | bytes 5400000 | tf_op jit(solution)/shard_map/owned_sum/pallas_call | solution.py:164
  156.6 0.7 merge.5
  157.3 1.6 collective-permute-start.37
  158.9 7.0 %collective-permute-done.39.refs_3_ = bf16[96,1536]{1,0:T(8,128)(2,1)S(1)} collective-permute-done((bf16[96,1536]{1,0:T(8,128)(2,1)S(1)}, bf16[96,1536]{1,0:T(8,128)(2,1)S(1)}, u32[]{:S(2)}, u32[]{:S(2)}) %collective-permute-start.39) | collective-permute-done | bytes 294944 | tf_op jit(solution)/shard_map/ppermute | solution.py:1184
  165.9 2.7 %output_sum.1 = bf16[256,768]{1,0:T(8,128)(2,1)} custom-call(s32[10]{0:T(128)S(1)} %dynamic-slice_bitcast_fusion.scal.refs_0_, f32[256,768]{1,0:T(8,128)S(1)} %get-tuple-element.211.refs_1_, bf16[256,768]{1,0:T(8,128)(2,1)} %copy-done.4, f32[256,768]{1,0:T(8,128)} %get-tuple-element.212.refs_3_, f32[16,768]{1,0:T(8,128)} %get-tuple-element.213.refs_4_.refs_5_), custom_call_target="tpu_custom_call" | custom-call | bytes 2880000 | tf_op jit(solution)/shard_map/output_sum/pallas_call | solution.py:164
  168.6 1.6 squares_of.1
  170.2 3.8 %collective-permute-done.37.refs_2_ = bf16[256,768]{1,0:T(8,128)(2,1)} collective-permute-done((bf16[256,768]{1,0:T(8,128)(2,1)S(1)}, bf16[256,768]{1,0:T(8,128)(2,1)}, u32[]{:S(2)}, u32[]{:S(2)}) %collective-permute-start.37) | collective-permute-done | bytes 393248 | tf_op jit(solution)/shard_map/ppermute | solution.py:1184
  174.0 6.4 %all-to-all-done.refs_1_ = bf16[8,104,768]{2,1,0:T(8,128)(2,1)S(1)} async-done(((bf16[8,104,768]{2,1,0:T(8,128)(2,1)}), bf16[8,104,768]{2,1,0:T(8,128)(2,1)S(1)}, u32[]{:S(2)}, u32[]{:S(2)}) %all-to-all-start) | async-done | bytes 1277984 | tf_op jit(solution)/shard_map/all_to_all | solution.py:1260
  180.4 0.7 owned_vector.1.refs_1_.refs_0_
  181.7 4.8 %collective-permute-done.42.refs_3_.refs_2_ = bf16[104,768]{1,0:T(8,128)(2,1)S(1)} collective-permute-done((bf16[104,768]{1,0:T(8,128)(2,1)S(1)}, bf16[104,768]{1,0:T(8,128)(2,1)S(1)}, u32[]{:S(2)}, u32[]{:S(2)}) %collective-permute-start.42) | collective-permute-done | bytes 159776 | tf_op jit(solution)/shard_map/ppermute | solution.py:1184
  186.5 1.4 collective-permute-done.43.refs_4_.refs_3_
  187.9 1.5 join.1
  189.3 4.4 %all-to-all-start.2 = ((f32[8,8,128]{2,1,0:T(8,128)}), f32[8,8,128]{2,1,0:T(8,128)S(1)}, u32[]{:S(2)}, u32[]{:S(2)}) async-start(f32[8,8,128]{2,1,0:T(8,128)} %bitcast.3), calls=%async_computation.2 | async-start | bytes 65536 | tf_op jit(solution)/shard_map/all_to_all | solution.py:1430
  193.7 3.3 %input_back.1 = f32[256,768]{1,0:T(8,128)} custom-call(s32[10]{0:T(128)S(1)} %dynamic-slice_bitcast_fusion.scal.refs_0_, f32[256,768]{1,0:T(8,128)S(1)} %get-tuple-element.217.refs_1_, bf16[256,768]{1,0:T(8,128)(2,1)} %collective-permute-done.37.refs_2_, bf16[256,768]{1,0:T(8,128)(2,1)} %refs_3_.5, f32[256,768]{1,0:T(8,128)} %get-tuple-element.219.refs_4_, ...), custom_call_target="tpu_custom_call" | custom-call | bytes 3600000 | tf_op jit(solution)/shard_map/input_back/pallas_call | solution.py:164
  197.1 3.3 %all-to-all-done.2.total_ref = f32[8,8,128]{2,1,0:T(8,128)S(1)} async-done(((f32[8,8,128]{2,1,0:T(8,128)}), f32[8,8,128]{2,1,0:T(8,128)S(1)}, u32[]{:S(2)}, u32[]{:S(2)}) %all-to-all-start.2) | async-done | bytes 32800 | tf_op jit(solution)/shard_map/all_to_all | solution.py:1430
  200.4 13.0 %adam.1 = (f32[96,3072]{1,0:T(8,128)}, f32[96,6144]{1,0:T(8,128)}, f32[12,96]{1,0:T(8,128)}, f32[96,3072]{1,0:T(8,128)}, f32[96,6144]{1,0:T(8,128)}, /*index=5*/...) custom-call(s32[10]{0:T(128)S(1)} %dynamic-slice_bitcast_fusion.scal, ...), custom_call_target="tpu_custom_call" | custom-call | bytes 32400000 | tf_op jit(solution)/shard_map/adam/pallas_call | solution.py:1151
  (69 shorter events, 10.9 us)
Async XLA Ops:
  1.4 13.1 %copy-start.2 = (bf16[256,768]{1,0:T(8,128)(2,1)S(1)}, bf16[256,768]{1,0:T(8,128)(2,1)}, u32[]{:S(2)}) copy-start(bf16[256,768]{1,0:T(8,128)(2,1)} %refs_3_.5) | copy-start | bytes 1179652
  1.4 19.0 %copy-start.3 = (s32[1,1024]{1,0:T(1,128)S(1)}, s32[1,1024]{1,0:T(1,128)}, u32[]{:S(2)}) copy-start(s32[1,1024]{1,0:T(1,128)} %refs_6_.1) | copy-start | bytes 12292
  1.4 26.1 %copy-start.1 = (bf16[256,768]{1,0:T(8,128)(2,1)S(1)}, bf16[256,768]{1,0:T(8,128)(2,1)}, u32[]{:S(2)}) copy-start(bf16[256,768]{1,0:T(8,128)(2,1)} %refs_3_.4) | copy-start | bytes 1179652
  1.4 27.6 %copy-start = (f32[96,6144]{1,0:T(8,128)S(1)}, f32[96,6144]{1,0:T(8,128)}, u32[]{:S(2)}) copy-start(f32[96,6144]{1,0:T(8,128)} %refs_12_.1) | copy-start | bytes 7077892
  3.6 7.4 %collective-permute-start.2 = (bf16[96,896]{1,0:T(8,128)(2,1)S(1)}, bf16[96,896]{1,0:T(8,128)(2,1)S(1)}, u32[]{:S(2)}, u32[]{:S(2)}) collective-permute-start(bf16[96,896]{1,0:T(8,128)(2,1)S(1)} %pack_attention.1.refs_2_), channel_id=1, source_target_pairs={{0,4},{8,0},{16,8},{24,16},{28,24},{20,28},{12,20},{4,12},{1,5},{9... | collective-permute-start | bytes 516104 | tf_op jit(solution)/shard_map/ppermute | solution.py:1233
  6.6 5.8 %collective-permute-start.1 = (bf16[96,896]{1,0:T(8,128)(2,1)S(1)}, bf16[96,896]{1,0:T(8,128)(2,1)S(1)}, u32[]{:S(2)}, u32[]{:S(2)}) collective-permute-start(bf16[96,896]{1,0:T(8,128)(2,1)S(1)} %pack_attention.1.refs_2_), channel_id=1, source_target_pairs={{0,8},{8,16},{16,24},{24,28},{28,20},{20,12},{12,4},{4,0},{1,9},{9... | collective-permute-start | bytes 516104 | tf_op jit(solution)/shard_map/ppermute | solution.py:1233
  12.5 5.4 %collective-permute-start.3 = (bf16[96,896]{1,0:T(8,128)(2,1)S(1)}, bf16[96,896]{1,0:T(8,128)(2,1)S(1)}, u32[]{:S(2)}, u32[]{:S(2)}) collective-permute-start(bf16[96,896]{1,0:T(8,128)(2,1)S(1)} %collective-permute-done.1.refs_3_), channel_id=1, source_target_pairs={{0,8},{8,16},{16,24},{24,28},{28,20},{20,12},{12,4},{4,0},{1,9},{9... | collective-permute-start | bytes 516104 | tf_op jit(solution)/shard_map/ppermute | solution.py:1233
  12.9 5.4 %collective-permute-start.4 = (bf16[96,896]{1,0:T(8,128)(2,1)S(1)}, bf16[96,896]{1,0:T(8,128)(2,1)S(1)}, u32[]{:S(2)}, u32[]{:S(2)}) collective-permute-start(bf16[96,896]{1,0:T(8,128)(2,1)S(1)} %collective-permute-done.2.refs_4_), channel_id=1, source_target_pairs={{0,4},{8,0},{16,8},{24,16},{28,24},{20,28},{12,20},{4,12},{1,5},{9... | collective-permute-start | bytes 516104 | tf_op jit(solution)/shard_map/ppermute | solution.py:1233
  14.5 12.5 %collective-permute-start = (bf16[256,768]{1,0:T(8,128)(2,1)S(1)}, bf16[256,768]{1,0:T(8,128)(2,1)S(1)}, u32[]{:S(2)}, u32[]{:S(2)}) collective-permute-start(bf16[256,768]{1,0:T(8,128)(2,1)S(1)} %copy-done.2), channel_id=1, source_target_pairs={{0,2},{1,3},{2,0},{3,1},{4,6},{5,7},{6,4},{7,5},{8,10},{9,11},{10,... | collective-permute-start | bytes 1179656 | tf_op jit(solution)/shard_map/ppermute | solution.py:1184
  18.3 5.4 %collective-permute-start.5 = (bf16[96,896]{1,0:T(8,128)(2,1)S(1)}, bf16[96,896]{1,0:T(8,128)(2,1)S(1)}, u32[]{:S(2)}, u32[]{:S(2)}) collective-permute-start(bf16[96,896]{1,0:T(8,128)(2,1)S(1)} %collective-permute-done.3.refs_5_), channel_id=1, source_target_pairs={{0,8},{8,16},{16,24},{24,28},{28,20},{20,12},{12,4},{4,0},{1,9},{9... | collective-permute-start | bytes 516104 | tf_op jit(solution)/shard_map/ppermute | solution.py:1233
  20.0 5.4 %collective-permute-start.6 = (bf16[96,896]{1,0:T(8,128)(2,1)S(1)}, bf16[96,896]{1,0:T(8,128)(2,1)S(1)}, u32[]{:S(2)}, u32[]{:S(2)}) collective-permute-start(bf16[96,896]{1,0:T(8,128)(2,1)S(1)} %collective-permute-done.4.refs_6_), channel_id=1, source_target_pairs={{0,4},{8,0},{16,8},{24,16},{28,24},{20,28},{12,20},{4,12},{1,5},{9... | collective-permute-start | bytes 516104 | tf_op jit(solution)/shard_map/ppermute | solution.py:1233
  25.4 5.4 %collective-permute-start.9 = (bf16[96,896]{1,0:T(8,128)(2,1)S(1)}, bf16[96,896]{1,0:T(8,128)(2,1)S(1)}, u32[]{:S(2)}, u32[]{:S(2)}) collective-permute-start(bf16[96,896]{1,0:T(8,128)(2,1)S(1)} %collective-permute-done.5.refs_7_), channel_id=1, source_target_pairs={{0,8},{8,16},{16,24},{24,28},{28,20},{20,12},{12,4},{4,0},{1,9},{9... | collective-permute-start | bytes 516104 | tf_op jit(solution)/shard_map/ppermute | solution.py:1233
  27.0 5.9 %collective-permute-start.7 = (bf16[256,768]{1,0:T(8,128)(2,1)S(1)}, bf16[256,768]{1,0:T(8,128)(2,1)S(1)}, u32[]{:S(2)}, u32[]{:S(2)}) collective-permute-start(bf16[256,768]{1,0:T(8,128)(2,1)S(1)} %copy-done.2), channel_id=1, source_target_pairs={{0,1},{1,0},{2,3},{3,2},{4,5},{5,4},{6,7},{7,6},{8,9},{9,8},{10,11... | collective-permute-start | bytes 1179656 | tf_op jit(solution)/shard_map/ppermute | solution.py:1184
  27.0 5.9 %collective-permute-start.8 = (bf16[256,768]{1,0:T(8,128)(2,1)S(1)}, bf16[256,768]{1,0:T(8,128)(2,1)S(1)}, u32[]{:S(2)}, u32[]{:S(2)}) collective-permute-start(bf16[256,768]{1,0:T(8,128)(2,1)S(1)} %collective-permute-done.refs_3_), channel_id=1, source_target_pairs={{0,1},{1,0},{2,3},{3,2},{4,5},{5,4},{6,7},{7,6},{8,9},{9,8},{10,11... | collective-permute-start | bytes 1179656 | tf_op jit(solution)/shard_map/ppermute | solution.py:1184
  27.5 11.0 %collective-permute-start.11 = (bf16[256,768]{1,0:T(8,128)(2,1)S(1)}, bf16[256,768]{1,0:T(8,128)(2,1)S(1)}, u32[]{:S(2)}, u32[]{:S(2)}) collective-permute-start(bf16[256,768]{1,0:T(8,128)(2,1)S(1)} %copy-done.1), channel_id=1, source_target_pairs={{0,2},{1,3},{2,0},{3,1},{4,6},{5,7},{6,4},{7,5},{8,10},{9,11},{10,... | collective-permute-start | bytes 1179656 | tf_op jit(solution)/shard_map/ppermute | solution.py:1184
  30.8 12.5 %collective-permute-start.22 = (bf16[96,1536]{1,0:T(8,128)(2,1)S(1)}, bf16[96,1536]{1,0:T(8,128)(2,1)S(1)}, u32[]{:S(2)}, u32[]{:S(2)}) collective-permute-start(bf16[96,1536]{1,0:T(8,128)(2,1)S(1)} %pack_forward.1.refs_15_), channel_id=1, source_target_pairs={{0,8},{8,16},{16,24},{24,28},{28,20},{20,12},{12,4},{4,0},{1,9},{9... | collective-permute-start | bytes 884744 | tf_op jit(solution)/shard_map/ppermute | solution.py:1233
  32.4 11.0 %collective-permute-start.23 = (bf16[96,1536]{1,0:T(8,128)(2,1)S(1)}, bf16[96,1536]{1,0:T(8,128)(2,1)S(1)}, u32[]{:S(2)}, u32[]{:S(2)}) collective-permute-start(bf16[96,1536]{1,0:T(8,128)(2,1)S(1)} %pack_forward.1.refs_15_), channel_id=1, source_target_pairs={{0,4},{8,0},{16,8},{24,16},{28,24},{20,28},{12,20},{4,12},{1,5},{9... | collective-permute-start | bytes 884744 | tf_op jit(solution)/shard_map/ppermute | solution.py:1233
  38.5 8.3 %collective-permute-start.10 = (bf16[1152,128]{1,0:T(8,128)(2,1)S(1)}, bf16[1152,128]{1,0:T(8,128)(2,1)S(1)}, u32[]{:S(2)}, u32[]{:S(2)}) collective-permute-start(bf16[1152,128]{1,0:T(8,128)(2,1)S(1)} %get-tuple-element.157.refs_11_), channel_id=1, source_target_pairs={{0,2},{1,3},{2,0},{3,1},{4,6},{5,7},{6,4},{7,5},{8,10},{9,11},{10,... | collective-permute-start | bytes 884744 | tf_op jit(solution)/shard_map/ppermute | solution.py:1184
  43.4 9.1 %collective-permute-start.24 = (bf16[96,1536]{1,0:T(8,128)(2,1)S(1)}, bf16[96,1536]{1,0:T(8,128)(2,1)S(1)}, u32[]{:S(2)}, u32[]{:S(2)}) collective-permute-start(bf16[96,1536]{1,0:T(8,128)(2,1)S(1)} %collective-permute-done.22.refs_16_), channel_id=1, source_target_pairs={{0,8},{8,16},{16,24},{24,28},{28,20},{20,12},{12,4},{4,0},{1,9},{9... | collective-permute-start | bytes 884744 | tf_op jit(solution)/shard_map/ppermute | solution.py:1233
  45.0 7.5 %collective-permute-start.25 = (bf16[96,1536]{1,0:T(8,128)(2,1)S(1)}, bf16[96,1536]{1,0:T(8,128)(2,1)S(1)}, u32[]{:S(2)}, u32[]{:S(2)}) collective-permute-start(bf16[96,1536]{1,0:T(8,128)(2,1)S(1)} %collective-permute-done.23.refs_17_), channel_id=1, source_target_pairs={{0,4},{8,0},{16,8},{24,16},{28,24},{20,28},{12,20},{4,12},{1,5},{9... | collective-permute-start | bytes 884744 | tf_op jit(solution)/shard_map/ppermute | solution.py:1233
  45.4 9.1 %collective-permute-start.12 = (bf16[768,128]{1,0:T(8,128)(2,1)S(1)}, bf16[768,128]{1,0:T(8,128)(2,1)S(1)}, u32[]{:S(2)}, u32[]{:S(2)}) collective-permute-start(bf16[768,128]{1,0:T(8,128)(2,1)S(1)} %get-tuple-element.155.refs_3_), channel_id=1, source_target_pairs={{0,2},{1,3},{2,0},{3,1},{4,6},{5,7},{6,4},{7,5},{8,10},{9,11},{10,... | collective-permute-start | bytes 589832 | tf_op jit(solution)/shard_map/ppermute | solution.py:1184
  49.9 6.2 %collective-permute-start.13 = (bf16[768,128]{1,0:T(8,128)(2,1)S(1)}, bf16[768,128]{1,0:T(8,128)(2,1)S(1)}, u32[]{:S(2)}, u32[]{:S(2)}) collective-permute-start(bf16[768,128]{1,0:T(8,128)(2,1)S(1)} %attend.3.refs_4_), channel_id=1, source_target_pairs={{0,2},{1,3},{2,0},{3,1},{4,6},{5,7},{6,4},{7,5},{8,10},{9,11},{10,... | collective-permute-start | bytes 589832 | tf_op jit(solution)/shard_map/ppermute | solution.py:1184
  52.5 6.7 %collective-permute-start.26 = (bf16[96,1536]{1,0:T(8,128)(2,1)S(1)}, bf16[96,1536]{1,0:T(8,128)(2,1)S(1)}, u32[]{:S(2)}, u32[]{:S(2)}) collective-permute-start(bf16[96,1536]{1,0:T(8,128)(2,1)S(1)} %collective-permute-done.24.refs_18_), channel_id=1, source_target_pairs={{0,8},{8,16},{16,24},{24,28},{28,20},{20,12},{12,4},{4,0},{1,9},{9... | collective-permute-start | bytes 884744 | tf_op jit(solution)/shard_map/ppermute | solution.py:1233
  54.0 6.7 %collective-permute-start.27 = (bf16[96,1536]{1,0:T(8,128)(2,1)S(1)}, bf16[96,1536]{1,0:T(8,128)(2,1)S(1)}, u32[]{:S(2)}, u32[]{:S(2)}) collective-permute-start(bf16[96,1536]{1,0:T(8,128)(2,1)S(1)} %collective-permute-done.25.refs_19_), channel_id=1, source_target_pairs={{0,4},{8,0},{16,8},{24,16},{28,24},{20,28},{12,20},{4,12},{1,5},{9... | collective-permute-start | bytes 884744 | tf_op jit(solution)/shard_map/ppermute | solution.py:1233
  56.1 6.7 %collective-permute-start.14 = (bf16[256,768]{1,0:T(8,128)(2,1)S(1)}, bf16[256,768]{1,0:T(8,128)(2,1)S(1)}, u32[]{:S(2)}, u32[]{:S(2)}) collective-permute-start(bf16[256,768]{1,0:T(8,128)(2,1)S(1)} %copy-done.1), channel_id=1, source_target_pairs={{0,1},{1,0},{2,3},{3,2},{4,5},{5,4},{6,7},{7,6},{8,9},{9,8},{10,11... | collective-permute-start | bytes 1179656 | tf_op jit(solution)/shard_map/ppermute | solution.py:1184
  56.1 6.7 %collective-permute-start.15 = (bf16[256,768]{1,0:T(8,128)(2,1)S(1)}, bf16[256,768]{1,0:T(8,128)(2,1)S(1)}, u32[]{:S(2)}, u32[]{:S(2)}) collective-permute-start(bf16[256,768]{1,0:T(8,128)(2,1)S(1)} %collective-permute-done.11.refs_3_), channel_id=1, source_target_pairs={{0,1},{1,0},{2,3},{3,2},{4,5},{5,4},{6,7},{7,6},{8,9},{9,8},{10,11... | collective-permute-start | bytes 1179656 | tf_op jit(solution)/shard_map/ppermute | solution.py:1184
  56.6 4.2 %collective-permute-start.17 = (bf16[768,128]{1,0:T(8,128)(2,1)S(1)}, bf16[768,128]{1,0:T(8,128)(2,1)S(1)}, u32[]{:S(2)}, u32[]{:S(2)}) collective-permute-start(bf16[768,128]{1,0:T(8,128)(2,1)S(1)} %attend.3.refs_4_), channel_id=1, source_target_pairs={{0,1},{1,0},{2,3},{3,2},{4,5},{5,4},{6,7},{7,6},{8,9},{9,8},{10,11... | collective-permute-start | bytes 589832 | tf_op jit(solution)/shard_map/ppermute | solution.py:1184
  59.2 2.0 collective-permute-start.19
  60.7 3.7 %collective-permute-start.20 = (bf16[1152,128]{1,0:T(8,128)(2,1)S(1)}, bf16[1152,128]{1,0:T(8,128)(2,1)S(1)}, u32[]{:S(2)}, u32[]{:S(2)}) collective-permute-start(bf16[1152,128]{1,0:T(8,128)(2,1)S(1)} %get-tuple-element.157.refs_11_), channel_id=1, source_target_pairs={{0,1},{1,0},{2,3},{3,2},{4,5},{5,4},{6,7},{7,6},{8,9},{9,8},{10,11... | collective-permute-start | bytes 884744 | tf_op jit(solution)/shard_map/ppermute | solution.py:1184
  60.8 3.7 %collective-permute-start.21 = (bf16[1152,128]{1,0:T(8,128)(2,1)S(1)}, bf16[1152,128]{1,0:T(8,128)(2,1)S(1)}, u32[]{:S(2)}, u32[]{:S(2)}) collective-permute-start(bf16[1152,128]{1,0:T(8,128)(2,1)S(1)} %collective-permute-done.10.refs_13_), channel_id=1, source_target_pairs={{0,1},{1,0},{2,3},{3,2},{4,5},{5,4},{6,7},{7,6},{8,9},{9,8},{10,11... | collective-permute-start | bytes 884744 | tf_op jit(solution)/shard_map/ppermute | solution.py:1184
  61.3 9.0 %collective-permute-start.28 = (bf16[96,1536]{1,0:T(8,128)(2,1)S(1)}, bf16[96,1536]{1,0:T(8,128)(2,1)S(1)}, u32[]{:S(2)}, u32[]{:S(2)}) collective-permute-start(bf16[96,1536]{1,0:T(8,128)(2,1)S(1)} %collective-permute-done.26.refs_20_), channel_id=1, source_target_pairs={{0,8},{8,16},{16,24},{24,28},{28,20},{20,12},{12,4},{4,0},{1,9},{9... | collective-permute-start | bytes 884744 | tf_op jit(solution)/shard_map/ppermute | solution.py:1233
  62.8 1.4 collective-permute-start.16
  62.8 1.7 collective-permute-start.18
  81.5 5.2 %collective-permute-start.29 = (bf16[512,768]{1,0:T(8,128)(2,1)S(1)}, bf16[512,768]{1,0:T(8,128)(2,1)S(1)}, u32[]{:S(2)}, u32[]{:S(2)}) collective-permute-start(bf16[512,768]{1,0:T(8,128)(2,1)S(1)} %get-tuple-element.178), channel_id=1, source_target_pairs={{0,1},{1,0},{2,3},{3,2},{4,5},{5,4},{6,7},{7,6},{8,9},{9,8},{10,11... | collective-permute-start | bytes 2359304 | tf_op jit(solution)/shard_map/ppermute | solution.py:1184
  86.7 59.2 %all-to-all-start.1 = ((bf16[8,96,1536]{2,1,0:T(8,128)(2,1)}), bf16[8,96,1536]{2,1,0:T(8,128)(2,1)}, u32[]{:S(2)}, u32[]{:S(2)}) async-start(bf16[8,96,1536]{2,1,0:T(8,128)(2,1)} %bitcast.2), calls=%async_computation.1 | async-start | bytes 4718592 | tf_op jit(solution)/shard_map/all_to_all | solution.py:1260
  91.8 11.6 %collective-permute-start.30 = (bf16[256,768]{1,0:T(8,128)(2,1)S(1)}, bf16[256,768]{1,0:T(8,128)(2,1)S(1)}, u32[]{:S(2)}, u32[]{:S(2)}) collective-permute-start(bf16[256,768]{1,0:T(8,128)(2,1)S(1)} %get-tuple-element.180), channel_id=1, source_target_pairs={{0,2},{1,3},{2,0},{3,1},{4,6},{5,7},{6,4},{7,5},{8,10},{9,11},{10,... | collective-permute-start | bytes 1179656 | tf_op jit(solution)/shard_map/ppermute | solution.py:1184
  104.6 2.5 %collective-permute-start.31 = (bf16[512,768]{1,0:T(8,128)(2,1)S(1)}, bf16[512,768]{1,0:T(8,128)(2,1)S(1)}, u32[]{:S(2)}, u32[]{:S(2)}) collective-permute-start(bf16[512,768]{1,0:T(8,128)(2,1)S(1)} %get-tuple-element.188), channel_id=1, source_target_pairs={{0,1},{1,0},{2,3},{3,2},{4,5},{5,4},{6,7},{7,6},{8,9},{9,8},{10,11... | collective-permute-start | bytes 2359304 | tf_op jit(solution)/shard_map/ppermute | solution.py:1184
  104.6 11.5 %collective-permute-start.33 = (bf16[256,768]{1,0:T(8,128)(2,1)S(1)}, bf16[256,768]{1,0:T(8,128)(2,1)S(1)}, u32[]{:S(2)}, u32[]{:S(2)}) collective-permute-start(bf16[256,768]{1,0:T(8,128)(2,1)S(1)} %get-tuple-element.187.refs_1_), channel_id=1, source_target_pairs={{0,2},{1,3},{2,0},{3,1},{4,6},{5,7},{6,4},{7,5},{8,10},{9,11},{10,... | collective-permute-start | bytes 1179656 | tf_op jit(solution)/shard_map/ppermute | solution.py:1184
  105.2 11.0 %collective-permute-start.32 = (bf16[256,768]{1,0:T(8,128)(2,1)S(1)}, bf16[256,768]{1,0:T(8,128)(2,1)S(1)}, u32[]{:S(2)}, u32[]{:S(2)}) collective-permute-start(bf16[256,768]{1,0:T(8,128)(2,1)S(1)} %get-tuple-element.187.refs_1_), channel_id=1, source_target_pairs={{0,1},{1,0},{2,3},{3,2},{4,5},{5,4},{6,7},{7,6},{8,9},{9,8},{10,11... | collective-permute-start | bytes 1179656 | tf_op jit(solution)/shard_map/ppermute | solution.py:1184
  116.2 1.7 collective-permute-start.34
  122.2 12.7 %collective-permute-start.35 = (bf16[256,768]{1,0:T(8,128)(2,1)S(1)}, bf16[256,768]{1,0:T(8,128)(2,1)S(1)}, u32[]{:S(2)}, u32[]{:S(2)}) collective-permute-start(bf16[256,768]{1,0:T(8,128)(2,1)S(1)} %get-tuple-element.198), channel_id=1, source_target_pairs={{0,2},{1,3},{2,0},{3,1},{4,6},{5,7},{6,4},{7,5},{8,10},{9,11},{10,... | collective-permute-start | bytes 1179656 | tf_op jit(solution)/shard_map/ppermute | solution.py:1184
  134.9 7.8 %copy-start.4 = (bf16[256,768]{1,0:T(8,128)(2,1)}, bf16[256,768]{1,0:T(8,128)(2,1)S(1)}, u32[]{:S(2)}) copy-start(bf16[256,768]{1,0:T(8,128)(2,1)S(1)} %collective-permute-done.35.refs_2_) | copy-start | bytes 1179652
  145.9 34.5 %all-to-all-start = ((bf16[8,104,768]{2,1,0:T(8,128)(2,1)}), bf16[8,104,768]{2,1,0:T(8,128)(2,1)S(1)}, u32[]{:S(2)}, u32[]{:S(2)}) async-start(bf16[8,104,768]{2,1,0:T(8,128)(2,1)} %bitcast.6), calls=%async_computation | async-start | bytes 2555904 | tf_op jit(solution)/shard_map/all_to_all | solution.py:1260
  153.4 3.1 %collective-permute-start.36 = (bf16[512,768]{1,0:T(8,128)(2,1)S(1)}, bf16[512,768]{1,0:T(8,128)(2,1)S(1)}, u32[]{:S(2)}, u32[]{:S(2)}) collective-permute-start(bf16[512,768]{1,0:T(8,128)(2,1)S(1)} %get-tuple-element.216), channel_id=1, source_target_pairs={{0,1},{1,0},{2,3},{3,2},{4,5},{5,4},{6,7},{7,6},{8,9},{9,8},{10,11... | collective-permute-start | bytes 2359304 | tf_op jit(solution)/shard_map/ppermute | solution.py:1184
  156.0 9.9 %collective-permute-start.39 = (bf16[96,1536]{1,0:T(8,128)(2,1)S(1)}, bf16[96,1536]{1,0:T(8,128)(2,1)S(1)}, u32[]{:S(2)}, u32[]{:S(2)}) collective-permute-start(bf16[96,1536]{1,0:T(8,128)(2,1)S(1)} %owned_sum.1.refs_1_), channel_id=1, source_target_pairs={{0,2},{1,3},{2,0},{3,1},{4,6},{5,7},{6,4},{7,5},{8,10},{9,11},{10,... | collective-permute-start | bytes 884744 | tf_op jit(solution)/shard_map/ppermute | solution.py:1184
  157.3 16.8 %collective-permute-start.37 = (bf16[256,768]{1,0:T(8,128)(2,1)S(1)}, bf16[256,768]{1,0:T(8,128)(2,1)}, u32[]{:S(2)}, u32[]{:S(2)}) collective-permute-start(bf16[256,768]{1,0:T(8,128)(2,1)S(1)} %get-tuple-element.218), channel_id=1, source_target_pairs={{0,2},{1,3},{2,0},{3,1},{4,6},{5,7},{6,4},{7,5},{8,10},{9,11},{10,... | collective-permute-start | bytes 1179656 | tf_op jit(solution)/shard_map/ppermute | solution.py:1184
  158.9 9.7 %collective-permute-start.38 = (bf16[96,1536]{1,0:T(8,128)(2,1)S(1)}, bf16[96,1536]{1,0:T(8,128)(2,1)S(1)}, u32[]{:S(2)}, u32[]{:S(2)}) collective-permute-start(bf16[96,1536]{1,0:T(8,128)(2,1)S(1)} %owned_sum.1.refs_1_), channel_id=1, source_target_pairs={{0,1},{1,0},{2,3},{3,2},{4,5},{5,4},{6,7},{7,6},{8,9},{9,8},{10,11... | collective-permute-start | bytes 884744 | tf_op jit(solution)/shard_map/ppermute | solution.py:1184
  165.9 2.7 %collective-permute-start.40 = (bf16[96,1536]{1,0:T(8,128)(2,1)S(1)}, bf16[96,1536]{1,0:T(8,128)(2,1)S(1)}, u32[]{:S(2)}, u32[]{:S(2)}) collective-permute-start(bf16[96,1536]{1,0:T(8,128)(2,1)S(1)} %collective-permute-done.39.refs_3_), channel_id=1, source_target_pairs={{0,1},{1,0},{2,3},{3,2},{4,5},{5,4},{6,7},{7,6},{8,9},{9,8},{10,11... | collective-permute-start | bytes 884744 | tf_op jit(solution)/shard_map/ppermute | solution.py:1184
  181.1 5.3 %collective-permute-start.42 = (bf16[104,768]{1,0:T(8,128)(2,1)S(1)}, bf16[104,768]{1,0:T(8,128)(2,1)S(1)}, u32[]{:S(2)}, u32[]{:S(2)}) collective-permute-start(bf16[104,768]{1,0:T(8,128)(2,1)S(1)} %owned_vector.1.refs_1_.refs_0_), channel_id=1, source_target_pairs={{0,2},{1,3},{2,0},{3,1},{4,6},{5,7},{6,4},{7,5},{8,10},{9,11},{10,... | collective-permute-start | bytes 479240 | tf_op jit(solution)/shard_map/ppermute | solution.py:1184
  181.7 4.8 %collective-permute-start.41 = (bf16[104,768]{1,0:T(8,128)(2,1)S(1)}, bf16[104,768]{1,0:T(8,128)(2,1)S(1)}, u32[]{:S(2)}, u32[]{:S(2)}) collective-permute-start(bf16[104,768]{1,0:T(8,128)(2,1)S(1)} %owned_vector.1.refs_1_.refs_0_), channel_id=1, source_target_pairs={{0,1},{1,0},{2,3},{3,2},{4,5},{5,4},{6,7},{7,6},{8,9},{9,8},{10,11... | collective-permute-start | bytes 479240 | tf_op jit(solution)/shard_map/ppermute | solution.py:1184
  186.5 1.4 collective-permute-start.43
  189.3 11.1 %all-to-all-start.2 = ((f32[8,8,128]{2,1,0:T(8,128)}), f32[8,8,128]{2,1,0:T(8,128)S(1)}, u32[]{:S(2)}, u32[]{:S(2)}) async-start(f32[8,8,128]{2,1,0:T(8,128)} %bitcast.3), calls=%async_computation.2 | async-start | bytes 65536 | tf_op jit(solution)/shard_map/all_to_all | solution.py:1430
